TPU v7x, 32 devices: a whole 2x2x4 slice. The times are simulated.
32 devices in a mesh: groups: 2 (over x), seq: 16 (over z, y, core).
Axes of the slice: x: 2, y: 2, z: 4, core: 2. Of those that a mesh axis runs over, the one named last changes fastest.
Arguments:
- query_in: bfloat16 [16384, 2048], P(('groups', 'seq')), parts along dimension 0, may hold values from -6 to 6
- key_in: bfloat16 [16384, 2048], P(('groups', 'seq')), parts along dimension 0, may hold values from -6 to 6
- value_in: bfloat16 [16384, 2048], P(('groups', 'seq')), parts along dimension 0, may hold values from -6 to 6
- conv_weight: float32 [4, 6144], replicated, may hold values from -3 to 3
- level_weight: bfloat16 [16, 14, 16384], P(None, None, ('groups', 'seq')), parts along dimension 2, may hold values from 0.099609375 to 1
- out_gain: float32 [2048], replicated, may hold values from 0.1 to 1.9
- doc_starts: int32 [16], P('groups'), parts along dimension 0, may hold values from 0 to 8191, as said below
Outputs:
- mixed: bfloat16 [16384, 2048], P(('groups', 'seq')), parts along dimension 0
There are 2 independent parts, one for each index of `groups`. A program takes and returns all parts, laid end to end along the dimension named above; an argument that names none is the same for every part. Nothing has to cross between parts.
Inputs may be any that keep to these rules, and one draw needn't show every extreme that they name: doc_starts is strictly increasing, its first entry is 0, its last entry is 8191, and no document starts above a quarter of 8192 and at or below three quarters of 8192.
All inputs are finite; a program needn't handle non-finite values.
Results may differ from a plain program's by a relative error of at most 0.0034.
Values may be sent and summed in bfloat16 or wider, within the bound.
No kernel may reach another device: no remote copies, remote signals or barrier semaphores. Data moves between devices by JAX's collectives and lax.ppermute only.
A program may use at most 128 MiB of HBM per device.

v0:
```python
import jax
import jax.numpy as jnp
from jax import lax
from jax.sharding import PartitionSpec as P


def swapped(block, axis, bit):
    count = lax.axis_size(axis)
    route = []
    for low in range(count):
        high = low | 1 << bit
        if high != low and high < count:
            route += [(low, high), (high, low)]
    return lax.ppermute(block, axis, route)


def passed_along(block, axis, distance):
    devices = range(lax.axis_size(axis))
    route = [(i - distance, i) for i in devices if i - distance in devices]
    return lax.ppermute(block, axis, route)


def start_of(doc_starts, positions):
    is_before = doc_starts[None, :] <= positions[:, None]
    return jnp.max(jnp.where(is_before, doc_starts[None, :], 0), axis=1)


def bit_width(values, bit_count):
    summed = jnp.zeros(values.shape, jnp.int32)
    for bit_place in range(bit_count):
        summed = summed + (values >= 1 << bit_place).astype(jnp.int32)
    return summed


def convolve(extended, weights, starts_tok, positions):
    conv_width = weights.shape[0]
    row_count = positions.shape[0]
    summed = jnp.zeros((row_count, extended.shape[1]), jnp.float32)
    for offset in range(conv_width):
        shifted = extended[conv_width - 1 - offset : conv_width - 1 - offset + row_count].astype(
            jnp.float32
        )
        usable = (positions - offset >= starts_tok)[:, None]
        summed = summed + jnp.where(usable, weights[offset][None, :] * shifted, 0.0)
    return summed


def prepare_heads(query_ext, key_ext, value_ext, conv_weight, starts_tok, positions, head_count):
    width_all = query_ext.shape[1]
    row_count = positions.shape[0]
    queries = jax.nn.silu(convolve(query_ext, conv_weight[:, :width_all], starts_tok, positions))
    queries = queries.astype(jnp.bfloat16).reshape(row_count, head_count, width_all // head_count)
    key_rows = jax.nn.silu(
        convolve(key_ext, conv_weight[:, width_all : 2 * width_all], starts_tok, positions)
    )
    key_rows = key_rows.reshape(row_count, head_count, width_all // head_count)
    key_rows = (
        key_rows / jnp.sqrt(jnp.sum(key_rows * key_rows, axis=2, keepdims=True) + 1e-06)
    ).astype(jnp.bfloat16)
    value_rows = jax.nn.silu(
        convolve(value_ext, conv_weight[:, 2 * width_all :], starts_tok, positions)
    )
    value_rows = value_rows.astype(jnp.bfloat16).reshape(
        row_count, head_count, width_all // head_count
    )
    return (queries, key_rows, value_rows)


def swap_states(carried, bit_place):
    return swapped(carried, "seq", bit_place)


def fetch_state(carried, bit_place):
    return swap_states(carried, bit_place)


def local(query_in, key_in, value_in, conv_weight, level_weight, out_gain, doc_starts):
    row_count, width_all = query_in.shape
    head_count = level_weight.shape[0]
    head_size = width_all // head_count
    conv_width = conv_weight.shape[0]
    dev_index = lax.axis_index("seq")
    dev_count = lax.axis_size("seq")
    dev_bits = dev_count.bit_length() - 1
    tok_bits = row_count.bit_length() - 1
    first_pos = dev_index * row_count
    positions = first_pos + jnp.arange(row_count, dtype=jnp.int32)
    starts_tok = start_of(doc_starts, positions)
    tail_rows = row_count - conv_width + 1
    rims = passed_along((query_in[tail_rows:], key_in[tail_rows:], value_in[tail_rows:]), "seq", 1)
    queries, key_rows, value_rows = prepare_heads(
        jnp.concatenate([rims[0], query_in], axis=0),
        jnp.concatenate([rims[1], key_in], axis=0),
        jnp.concatenate([rims[2], value_in], axis=0),
        conv_weight,
        starts_tok,
        positions,
        head_count,
    )
    local_ids = jnp.arange(row_count, dtype=jnp.int32)
    level_map = bit_width(local_ids[:, None] ^ local_ids[None, :], tok_bits)
    local_scale = jnp.exp2(-0.5 * level_map.astype(jnp.float32))
    onehot = (
        level_map[:, :, None] == jnp.arange(tok_bits + 1, dtype=jnp.int32)[None, None, :]
    ).astype(jnp.bfloat16)
    picked = jnp.einsum(
        "ijl,hli->hij",
        onehot,
        level_weight[:, : tok_bits + 1, :],
        preferred_element_type=jnp.float32,
    )
    pair_weight = picked * local_scale[None]
    valid = (local_ids[None, :] <= local_ids[:, None]) & (
        first_pos + local_ids[None, :] >= starts_tok[:, None]
    )
    scores = jnp.einsum("ihd,jhd->hij", queries, key_rows, preferred_element_type=jnp.float32)
    weighted = jnp.where(valid[None], scores * pair_weight, 0.0).astype(jnp.bfloat16)
    near_sum = jnp.einsum("hij,jhd->ihd", weighted, value_rows, preferred_element_type=jnp.float32)
    keep_rows = positions >= starts_tok[-1]
    tail_keys = jnp.where(keep_rows[:, None, None], key_rows, jnp.zeros_like(key_rows))
    carried = jnp.einsum("shd,she->hde", tail_keys, value_rows, preferred_element_type=jnp.float32)
    weights_float = level_weight.astype(jnp.float32)
    states = []
    coef_list = []
    for bit_place in range(dev_bits):
        stride = 1 << bit_place
        partner = fetch_state(carried, bit_place)
        is_upper = dev_index >> bit_place & 1 == 1
        if bit_place < dev_bits - 1:
            upper_first = ((dev_index >> bit_place + 1 << bit_place + 1) + stride) * row_count
            upper_has = jnp.any(
                (doc_starts >= upper_first) & (doc_starts < upper_first + stride * row_count)
            )
            upper_part = jnp.where(is_upper, carried, partner)
            lower_part = jnp.where(is_upper, partner, carried)
            carried = jnp.where(upper_has, upper_part, lower_part + upper_part)
        state = partner.astype(jnp.bfloat16)
        level_id = tok_bits + 1 + bit_place
        level_mask = is_upper & (starts_tok < (dev_index >> bit_place << bit_place) * row_count)
        coefs_level = jnp.where(
            level_mask[:, None],
            weights_float[:, level_id, :].T * jnp.exp2(jnp.float32(-0.5 * level_id)),
            0.0,
        )
        states.append(state)
        coef_list.append(coefs_level)
    stacked = jnp.stack(states)
    coef_all = jnp.stack(coef_list)
    images = jnp.einsum("thd,lhde->lthe", queries, stacked, preferred_element_type=jnp.float32)
    far_sum = jnp.sum(coef_all[:, :, :, None] * images, axis=0)
    summed = near_sum + far_sum
    normed = summed / jnp.sqrt(jnp.mean(summed * summed, axis=2, keepdims=True) + 1e-06)
    return (
        (normed * out_gain.reshape(head_count, head_size))
        .astype(jnp.bfloat16)
        .reshape(row_count, width_all)
    )


def solution(mesh):
    in_specs = (
        P(("groups", "seq"), None),
        P(("groups", "seq"), None),
        P(("groups", "seq"), None),
        P(),
        P(None, None, ("groups", "seq")),
        P(),
        P("groups"),
    )
    out_specs = P(("groups", "seq"), None)
    return jax.shard_map(local, mesh=mesh, in_specs=in_specs, out_specs=out_specs, check_vma=False)
```

profile of v0, /device:TPU:0, one launch (start us, length us, event | category | flops | bytes accessed | tf_op | source)
XLA Modules:
  0.0 156.5 jit_solution(10341092209387386657)
XLA Ops:
  0.0 0.8 slice.123
  0.8 2.4 %collective-permute-start.2 = (bf16[3,2048]{1,0:T(4,128)(2,1)S(1)}, bf16[3,2048]{1,0:T(4,128)(2,1)S(1)}, u32[]{:S(2)}, u32[]{:S(2)}) collective-permute-start(bf16[3,2048]{1,0:T(4,128)(2,1)S(1)} %slice.123), channel_id=1, source_target_pairs={{0,1},{1,2},{2,3},{3,4},{4,5},{5,6},{6,7},{7,8},{8,9},{9,10},{10,1... | collective-permute-start | bytes 36872 | tf_op jit(solution)/shard_map/ppermute | solution.py:20
  3.1 0.8 slice.107
  3.9 4.5 %collective-permute-start = (bf16[3,2048]{1,0:T(4,128)(2,1)S(1)}, bf16[3,2048]{1,0:T(4,128)(2,1)S(1)}, u32[]{:S(2)}, u32[]{:S(2)}) collective-permute-start(bf16[3,2048]{1,0:T(4,128)(2,1)S(1)} %slice.107), channel_id=1, source_target_pairs={{0,1},{1,2},{2,3},{3,4},{4,5},{5,6},{6,7},{7,8},{8,9},{9,10},{10,1... | collective-permute-start | bytes 36872 | tf_op jit(solution)/shard_map/ppermute | solution.py:20
  8.5 1.8 %fusion.58 = (f32[1,2048]{1,0:T(1,128)S(1)}, f32[1,2048]{1,0:T(1,128)S(1)}, f32[1,2048]{1,0:T(1,128)S(1)}, f32[1,2048]{1,0:T(1,128)S(1)}, f32[1,2048]{1,0:T(1,12...) fusion(f32[4,6144]{1,0:T(4,128)} %param.10), kind=kLoop, calls=%fused_computation.102 | loop fusion | bytes 196608 | tf_op jit(solution)/shard_map/slice | solution.py:44
  12.9 8.3 %multiply_bitcast_fusion = f32[64,8,16,128]{3,1,2,0:T(8,128)S(1)} fusion(bf16[512,2048]{1,0:T(8,128)(2,1)} %param.8, bf16[3,2048]{1,0:T(4,128)(2,1)S(1)} %collective-permute-done.2, f32[2048]{0:T(1024)S(1)} %bitcast.134, f32[2048]{0:T(1024)S(1)} %bitcast.135, f32[2048]{0:T(1024)S(1)} %bitcast.132, f32[2048]{0:T(1024)S(1)} %bitcast.133, ...), kind=kLoop, calls=%fused_computation.14 | loop fusion | flops 29360128 | bytes 6338560
  21.2 0.9 copy.73
  22.2 1.9 %copy-done = f32[64,8,16,128]{3,2,1,0:T(8,128)} copy-done((f32[64,8,16,128]{3,2,1,0:T(8,128)}, f32[64,8,16,128]{3,2,1,0:T(8,128)S(1)}, u32[]{:S(2)}) %copy-start) | copy-done | bytes 4194328
  24.2 1.2 multiply_reduce_fusion.1
  25.6 6.9 %broadcast_select_fusion = (bf16[512,16,128]{2,1,0:T(8,128)(2,1)S(1)}, bf16[512,16,128]{2,1,0:T(8,128)(2,1)}) fusion(pred[512]{0:T(512)(128)(4,1)S(1)} %fusion.55, f32[512,16]{1,0:T(8,128)S(1)} %copy.54, f32[64,8,16,128]{3,2,1,0:T(8,128)} %copy-done), kind=kLoop, calls=%fused_computation.43 | loop fusion | flops 3145728 | bytes 8421888 | tf_op jit(solution)/shard_map/jit(_where)/select_n | solution.py:120
  32.5 4.6 %fusion.24 = bf16[64,16,8,128]{3,2,1,0:T(8,128)(2,1)S(1)} fusion(bf16[512,2048]{1,0:T(8,128)(2,1)S(1)} %copy-done.1, bf16[3,2048]{1,0:T(4,128)(2,1)S(1)} %collective-permute-done, f32[2048]{0:T(1024)S(1)} %bitcast.129, pred[512]{0:T(512)(128)(4,1)S(1)} %get-tuple-element.35, f32[2048]{0:T(1024)S(1)} %bitcast.130, pred[512]{0:T(512)(128)(4,1)S(1)} %get-tuple-element.36, ...), kind=kLoop, calls=%fused_computation.44 | loop fusion | flops 30408704 | bytes 4241408
  37.2 1.5 fusion.17
  39.5 1.9 %collective-permute-done.3 = f32[16,128,128]{2,1,0:T(8,128)S(1)} collective-permute-done((f32[16,128,128]{2,1,0:T(8,128)S(1)}, f32[16,128,128]{2,1,0:T(8,128)S(1)}, u32[]{:S(2)}, u32[]{:S(2)}) %collective-permute-start.3) | collective-permute-done | bytes 1048608 | tf_op jit(solution)/shard_map/ppermute | solution.py:14
  41.4 1.7 %convert_bitcast_fusion.3 = (bf16[1,16,128,128]{3,2,1,0:T(8,128)(2,1)}, f32[16,128,128]{2,1,0:T(8,128)S(1)}) fusion(f32[16,128,128]{2,1,0:T(8,128)S(1)} %collective-permute-done.3, f32[16,128,128]{2,1,0:T(8,128)S(1)} %fusion.17, pred[]{:T(512)S(6)} %eq.28, pred[]{:T(512)} %get-tuple-element.6), kind=kLoop, calls=%fused_computation.67 | loop fusion | flops 1310720 | bytes 3670018 | tf_op jit(solution)/shard_map/stack | solution.py:147
  43.1 1.5 collective-permute-start.4
  44.6 1.4 slice.115
  46.0 2.3 %collective-permute-start.1 = (bf16[3,2048]{1,0:T(4,128)(2,1)}, bf16[3,2048]{1,0:T(4,128)(2,1)}, u32[]{:S(2)}, u32[]{:S(2)}) collective-permute-start(bf16[3,2048]{1,0:T(4,128)(2,1)} %slice.115), channel_id=1, source_target_pairs={{0,1},{1,2},{2,3},{3,4},{4,5},{5,6},{6,7},{7,8},{8,9},{9,10},{10,1... | collective-permute-start | bytes 36872 | tf_op jit(solution)/shard_map/ppermute | solution.py:20
  49.9 2.1 %copy.57 = bf16[16,10,512]{1,0,2:T(8,128)(2,1)S(1)} copy(bf16[16,10,512]{2,0,1:T(8,128)(2,1)S(1)} %slice-done) | data formatting | bytes 327680 | tf_op jit(solution)/shard_map/slice | solution.py:109
  52.2 16.2 %collective-permute-done.4 = f32[16,128,128]{2,1,0:T(8,128)} collective-permute-done((f32[16,128,128]{2,1,0:T(8,128)S(1)}, f32[16,128,128]{2,1,0:T(8,128)}, u32[]{:S(2)}, u32[]{:S(2)}) %collective-permute-start.4) | collective-permute-done | bytes 1048608 | tf_op jit(solution)/shard_map/ppermute | solution.py:14
  68.4 2.4 %convert_bitcast_fusion.2 = (bf16[1,16,128,128]{3,2,1,0:T(8,128)(2,1)S(1)}, f32[16,128,128]{2,1,0:T(8,128)S(1)}) fusion(f32[16,128,128]{2,1,0:T(8,128)} %collective-permute-done.4, f32[16,128,128]{2,1,0:T(8,128)S(1)} %get-tuple-element.11, pred[]{:T(512)S(6)} %eq.29, pred[]{:T(512)} %get-tuple-element.7), kind=kLoop, calls=%fused_computation.66 | loop fusion | flops 1310720 | bytes 3670018 | tf_op jit(solution)/shard_map/stack | solution.py:147
  70.8 1.8 %collective-permute-start.5 = (f32[16,128,128]{2,1,0:T(8,128)S(1)}, f32[16,128,128]{2,1,0:T(8,128)S(1)}, u32[]{:S(2)}, u32[]{:S(2)}) collective-permute-start(f32[16,128,128]{2,1,0:T(8,128)S(1)} %get-tuple-element.13), channel_id=1, source_target_pairs={{0,4},{4,0},{1,5},{5,1},{2,6},{6,2},{3,7},{7,3},{8,12},{12,8},{9,1... | collective-permute-start | bytes 3145736 | tf_op jit(solution)/shard_map/ppermute | solution.py:14
  72.7 1.3 multiply_exponential_fusion
  74.0 0.9 fusion.42
  74.9 7.7 %fusion.3 = f32[512,512,16]{1,2,0:T(8,128)} fusion(bf16[16,10,512]{1,0,2:T(8,128)(2,1)S(1)} %copy.57, s32[512,512]{1,0:T(8,128)S(1)} %convert_add_fusion), kind=kOutput, calls=%fused_computation.7 | convolution fusion | flops 86507520 | bytes 17989632 | tf_op jit(solution)/shard_map/ijl,hli->hij/dot_general | solution.py:106
  82.6 12.7 %collective-permute-done.5 = f32[16,128,128]{2,1,0:T(8,128)S(1)} collective-permute-done((f32[16,128,128]{2,1,0:T(8,128)S(1)}, f32[16,128,128]{2,1,0:T(8,128)S(1)}, u32[]{:S(2)}, u32[]{:S(2)}) %collective-permute-start.5) | collective-permute-done | bytes 1048608 | tf_op jit(solution)/shard_map/ppermute | solution.py:14
  96.0 2.8 %collective-permute-start.6 = (bf16[16,128,128]{2,1,0:T(8,128)(2,1)S(1)}, bf16[16,128,128]{2,1,0:T(8,128)(2,1)S(1)}, u32[]{:S(2)}, u32[]{:S(2)}) collective-permute-start(bf16[16,128,128]{2,1,0:T(8,128)(2,1)S(1)} %add_select_fusion), channel_id=1, source_target_pairs={{0,8},{8,0},{1,9},{9,1},{2,10},{10,2},{3,11},{11,3},{4,12},{12,4},... | collective-permute-start | bytes 1572872 | tf_op jit(solution)/shard_map/ppermute | solution.py:14
  98.9 5.6 %fusion.65 = bf16[64,8,16,128]{3,1,2,0:T(8,128)(2,1)S(1)} fusion(bf16[512,2048]{1,0:T(8,128)(2,1)S(1)} %copy-done.2, bf16[3,2048]{1,0:T(4,128)(2,1)} %collective-permute-done.1, f32[2048]{0:T(1024)S(1)} %bitcast.120, pred[512]{0:T(512)(128)(4,1)S(1)} %copy-done.17, f32[2048]{0:T(1024)S(1)} %bitcast.122, pred[512]{0:T(512)(128)(4,1)S(1)} %copy-done.19, ...), kind=kLoop, calls=%fused_computation.104 | loop fusion | flops 30408704 | bytes 4241408
  105.2 15.3 %collective-permute-done.6 = bf16[16,128,128]{2,1,0:T(8,128)(2,1)S(1)} collective-permute-done((bf16[16,128,128]{2,1,0:T(8,128)(2,1)S(1)}, bf16[16,128,128]{2,1,0:T(8,128)(2,1)S(1)}, u32[]{:S(2)}, u32[]{:S(2)}) %collective-permute-start.6) | collective-permute-done | bytes 524320 | tf_op jit(solution)/shard_map/ppermute | solution.py:14
  120.6 5.1 %fusion = f32[512,16,128]{0,2,1:T(8,128)} fusion(f32[4,512,16]{1,0,2:T(4,128)S(1)} %copy-done.8, bf16[512,16,128,1]{2,1,0,3:T(8,128)(2,1)S(1)} %bitcast.119, bf16[1,16,128,128]{3,2,1,0:T(8,128)(2,1)S(1)} %bitcast.137, bf16[1,16,128,128]{3,2,1,0:T(8,128)(2,1)S(1)} %convert_bitcast_fusion.1, bf16[1,16,128,128]{3,2,1,0:T(8,128)(2,1)S(1)} %get-tuple-element.12, ...), kind=kOutput, calls=%fused_computation.1 | convolution fusion | flops 1084227584 | bytes 8519680 | tf_op jit(solution)/shard_map/thd,lhde->lthe/dot_general | solution.py:149
  125.7 25.6 %multiply_reduce_fusion = (f32[512,16]{0,1:T(8,128)S(1)}, f32[512,16,128]{0,2,1:T(8,128)}) fusion(f32[512,16,128]{0,2,1:T(8,128)} %fusion, f32[512,512,16]{1,2,0:T(8,128)} %fusion.3, f32[512,512]{1,0:T(8,128)S(1)} %copy-done.5, pred[512,512]{1,0:T(8,128)(4,1)S(1)} %fusion.42, bf16[512,16,128]{2,1,0:T(8,128)(2,1)} %get-tuple-element.9, ...), kind=kOutput, calls=%fused_computation.11 | convolution fusion | flops 2197807104 | bytes 32847872 | tf_op jit(solution)/shard_map/hij,jhd->ihd/dot_general | solution.py:118
  151.3 2.7 %multiply_convert_fusion = bf16[512,16,128]{0,2,1:T(8,128)(2,1)S(1)} fusion(f32[512,16,128]{0,2,1:T(8,128)} %get-tuple-element.39, f32[16,128]{1,0:T(8,128)S(1)} %bitcast.136, f32[512,16]{0,1:T(8,128)S(1)} %add_sqrt_fusion), kind=kLoop, calls=%fused_computation.10 | loop fusion | flops 3145728 | bytes 6332416 | tf_op jit(solution)/shard_map/convert_element_type | solution.py:155
  154.1 2.4 %copy.65 = bf16[512,2048]{1,0:T(8,128)(2,1)} copy(bf16[512,2048]{0,1:T(8,128)(2,1)S(1)} %bitcast.118) | data formatting | bytes 4194304 | tf_op jit(solution)/shard_map/reshape | solution.py:156
  (69 shorter events, 6.9 us)
Async XLA Ops:
  0.8 12.1 %collective-permute-start.2 = (bf16[3,2048]{1,0:T(4,128)(2,1)S(1)}, bf16[3,2048]{1,0:T(4,128)(2,1)S(1)}, u32[]{:S(2)}, u32[]{:S(2)}) collective-permute-start(bf16[3,2048]{1,0:T(4,128)(2,1)S(1)} %slice.123), channel_id=1, source_target_pairs={{0,1},{1,2},{2,3},{3,4},{4,5},{5,6},{6,7},{7,8},{8,9},{9,10},{10,1... | collective-permute-start | bytes 36872 | tf_op jit(solution)/shard_map/ppermute | solution.py:20
  3.9 28.5 %collective-permute-start = (bf16[3,2048]{1,0:T(4,128)(2,1)S(1)}, bf16[3,2048]{1,0:T(4,128)(2,1)S(1)}, u32[]{:S(2)}, u32[]{:S(2)}) collective-permute-start(bf16[3,2048]{1,0:T(4,128)(2,1)S(1)} %slice.107), channel_id=1, source_target_pairs={{0,1},{1,2},{2,3},{3,4},{4,5},{5,6},{6,7},{7,8},{8,9},{9,10},{10,1... | collective-permute-start | bytes 36872 | tf_op jit(solution)/shard_map/ppermute | solution.py:20
  8.5 13.7 %copy-start.11 = (s32[512]{0:T(512)}, s32[512]{0:T(512)S(1)}, u32[]{:S(2)}) copy-start(s32[512]{0:T(512)S(1)} %iota_add_fusion) | copy-start | bytes 6148
  11.0 11.2 %copy-start.12 = (s32[512]{0:T(512)}, s32[512]{0:T(512)S(1)}, u32[]{:S(2)}) copy-start(s32[512]{0:T(512)S(1)} %select_reduce_fusion) | copy-start | bytes 6148
  12.2 20.2 %copy-start.14 = (pred[512]{0:T(512)(128)(4,1)}, pred[512]{0:T(512)(128)(4,1)S(1)}, u32[]{:S(2)}) copy-start(pred[512]{0:T(512)(128)(4,1)S(1)} %get-tuple-element.30) | copy-start | bytes 1540
  12.2 20.2 %copy-start.16 = (pred[512]{0:T(512)(128)(4,1)}, pred[512]{0:T(512)(128)(4,1)S(1)}, u32[]{:S(2)}) copy-start(pred[512]{0:T(512)(128)(4,1)S(1)} %get-tuple-element.35) | copy-start | bytes 1540
  12.2 20.2 %copy-start.18 = (pred[512]{0:T(512)(128)(4,1)}, pred[512]{0:T(512)(128)(4,1)S(1)}, u32[]{:S(2)}) copy-start(pred[512]{0:T(512)(128)(4,1)S(1)} %get-tuple-element.36) | copy-start | bytes 1540
  12.2 20.2 %copy-start.20 = (pred[512]{0:T(512)(128)(4,1)}, pred[512]{0:T(512)(128)(4,1)S(1)}, u32[]{:S(2)}) copy-start(pred[512]{0:T(512)(128)(4,1)S(1)} %get-tuple-element.37) | copy-start | bytes 1540
  22.2 2.0 %copy-start = (f32[64,8,16,128]{3,2,1,0:T(8,128)}, f32[64,8,16,128]{3,2,1,0:T(8,128)S(1)}, u32[]{:S(2)}) copy-start(f32[64,8,16,128]{3,2,1,0:T(8,128)S(1)} %copy.73) | copy-start | bytes 12582916
  25.6 6.9 %copy-start.1 = (bf16[512,2048]{1,0:T(8,128)(2,1)S(1)}, bf16[512,2048]{1,0:T(8,128)(2,1)}, u32[]{:S(2)}) copy-start(bf16[512,2048]{1,0:T(8,128)(2,1)} %param.9) | copy-start | bytes 6291460
  32.5 6.3 %copy-start.22 = (s32[8]{0:T(128)S(1)}, s32[8]{0:T(128)}, u32[]{:S(2)}) copy-start(s32[8]{0:T(128)} %param.13) | copy-start | bytes 100
  37.1 1.6 %copy-start.4 = (bf16[64,16,8,128]{3,2,1,0:T(8,128)(2,1)}, bf16[64,16,8,128]{3,2,1,0:T(8,128)(2,1)S(1)}, u32[]{:S(2)}) copy-start(bf16[64,16,8,128]{3,2,1,0:T(8,128)(2,1)S(1)} %fusion.24) | copy-start | bytes 6291460
  37.2 11.2 %copy-start.6 = (bf16[16,14,512]{2,0,1:T(8,128)(2,1)S(1)}, bf16[16,14,512]{2,0,1:T(8,128)(2,1)}, u32[]{:S(2)}) copy-start(bf16[16,14,512]{2,0,1:T(8,128)(2,1)} %param.11) | copy-start | bytes 688132
  37.2 12.7 %slice-start = ((bf16[16,14,512]{2,0,1:T(8,128)(2,1)}), bf16[16,10,512]{2,0,1:T(8,128)(2,1)S(1)}, s32[]{:S(2)}) async-start(bf16[16,14,512]{2,0,1:T(8,128)(2,1)} %param.11), calls=%async_computation | async-start | bytes 327680 | tf_op jit(solution)/shard_map/slice | solution.py:109
  38.7 2.7 %collective-permute-start.3 = (f32[16,128,128]{2,1,0:T(8,128)S(1)}, f32[16,128,128]{2,1,0:T(8,128)S(1)}, u32[]{:S(2)}, u32[]{:S(2)}) collective-permute-start(f32[16,128,128]{2,1,0:T(8,128)S(1)} %fusion.17), channel_id=1, source_target_pairs={{0,1},{1,0},{2,3},{3,2},{4,5},{5,4},{6,7},{7,6},{8,9},{9,8},{10,11... | collective-permute-start | bytes 3145736 | tf_op jit(solution)/shard_map/ppermute | solution.py:14
  43.1 25.3 %collective-permute-start.4 = (f32[16,128,128]{2,1,0:T(8,128)S(1)}, f32[16,128,128]{2,1,0:T(8,128)}, u32[]{:S(2)}, u32[]{:S(2)}) collective-permute-start(f32[16,128,128]{2,1,0:T(8,128)S(1)} %get-tuple-element.11), channel_id=1, source_target_pairs={{0,2},{2,0},{1,3},{3,1},{4,6},{6,4},{5,7},{7,5},{8,10},{10,8},{9,1... | collective-permute-start | bytes 3145736 | tf_op jit(solution)/shard_map/ppermute | solution.py:14
  46.0 52.9 %collective-permute-start.1 = (bf16[3,2048]{1,0:T(4,128)(2,1)}, bf16[3,2048]{1,0:T(4,128)(2,1)}, u32[]{:S(2)}, u32[]{:S(2)}) collective-permute-start(bf16[3,2048]{1,0:T(4,128)(2,1)} %slice.115), channel_id=1, source_target_pairs={{0,1},{1,2},{2,3},{3,4},{4,5},{5,6},{6,7},{7,8},{8,9},{9,10},{10,1... | collective-permute-start | bytes 36872 | tf_op jit(solution)/shard_map/ppermute | solution.py:20
  70.8 24.5 %collective-permute-start.5 = (f32[16,128,128]{2,1,0:T(8,128)S(1)}, f32[16,128,128]{2,1,0:T(8,128)S(1)}, u32[]{:S(2)}, u32[]{:S(2)}) collective-permute-start(f32[16,128,128]{2,1,0:T(8,128)S(1)} %get-tuple-element.13), channel_id=1, source_target_pairs={{0,4},{4,0},{1,5},{5,1},{2,6},{6,2},{3,7},{7,3},{8,12},{12,8},{9,1... | collective-permute-start | bytes 3145736 | tf_op jit(solution)/shard_map/ppermute | solution.py:14
  74.9 24.0 %copy-start.2 = (bf16[512,2048]{1,0:T(8,128)(2,1)S(1)}, bf16[512,2048]{1,0:T(8,128)(2,1)}, u32[]{:S(2)}) copy-start(bf16[512,2048]{1,0:T(8,128)(2,1)} %param.7) | copy-start | bytes 6291460
  74.9 24.0 %copy-start.9 = (f32[1,2048]{1,0:T(1,128)S(1)}, f32[1,2048]{1,0:T(1,128)}, u32[]{:S(2)}) copy-start(f32[1,2048]{1,0:T(1,128)} %get-tuple-element.23) | copy-start | bytes 24580
  74.9 24.0 %copy-start.10 = (f32[1,2048]{1,0:T(1,128)S(1)}, f32[1,2048]{1,0:T(1,128)}, u32[]{:S(2)}) copy-start(f32[1,2048]{1,0:T(1,128)} %get-tuple-element.24) | copy-start | bytes 24580
  74.9 24.0 %copy-start.15 = (pred[512]{0:T(512)(128)(4,1)S(1)}, pred[512]{0:T(512)(128)(4,1)}, u32[]{:S(2)}) copy-start(pred[512]{0:T(512)(128)(4,1)} %copy-done.14) | copy-start | bytes 1540
  74.9 24.0 %copy-start.17 = (pred[512]{0:T(512)(128)(4,1)S(1)}, pred[512]{0:T(512)(128)(4,1)}, u32[]{:S(2)}) copy-start(pred[512]{0:T(512)(128)(4,1)} %copy-done.16) | copy-start | bytes 1540
  74.9 24.0 %copy-start.19 = (pred[512]{0:T(512)(128)(4,1)S(1)}, pred[512]{0:T(512)(128)(4,1)}, u32[]{:S(2)}) copy-start(pred[512]{0:T(512)(128)(4,1)} %copy-done.18) | copy-start | bytes 1540
  74.9 24.0 %copy-start.21 = (pred[512]{0:T(512)(128)(4,1)S(1)}, pred[512]{0:T(512)(128)(4,1)}, u32[]{:S(2)}) copy-start(pred[512]{0:T(512)(128)(4,1)} %copy-done.20) | copy-start | bytes 1540
  96.0 24.5 %collective-permute-start.6 = (bf16[16,128,128]{2,1,0:T(8,128)(2,1)S(1)}, bf16[16,128,128]{2,1,0:T(8,128)(2,1)S(1)}, u32[]{:S(2)}, u32[]{:S(2)}) collective-permute-start(bf16[16,128,128]{2,1,0:T(8,128)(2,1)S(1)} %add_select_fusion), channel_id=1, source_target_pairs={{0,8},{8,0},{1,9},{9,1},{2,10},{10,2},{3,11},{11,3},{4,12},{12,4},... | collective-permute-start | bytes 1572872 | tf_op jit(solution)/shard_map/ppermute | solution.py:14
  98.9 21.7 %copy-start.7 = (bf16[1,16,128,128]{3,2,1,0:T(8,128)(2,1)S(1)}, bf16[1,16,128,128]{3,2,1,0:T(8,128)(2,1)}, u32[]{:S(2)}) copy-start(bf16[1,16,128,128]{3,2,1,0:T(8,128)(2,1)} %get-tuple-element.10) | copy-start | bytes 1572868
  98.9 21.6 %copy-start.8 = (f32[4,512,16]{1,0,2:T(4,128)S(1)}, f32[4,512,16]{1,0,2:T(4,128)}, u32[]{:S(2)}) copy-start(f32[4,512,16]{1,0,2:T(4,128)} %copy.60) | copy-start | bytes 393220
  120.6 5.1 %copy-start.3 = (bf16[512,2048]{1,0:T(8,128)(2,1)S(1)}, bf16[512,2048]{1,0:T(8,128)(2,1)}, u32[]{:S(2)}) copy-start(bf16[512,2048]{1,0:T(8,128)(2,1)} %param.7) | copy-start | bytes 6291460
  120.6 5.1 %copy-start.5 = (f32[512,512]{1,0:T(8,128)S(1)}, f32[512,512]{1,0:T(8,128)}, u32[]{:S(2)}) copy-start(f32[512,512]{1,0:T(8,128)} %multiply_exponential_fusion) | copy-start | bytes 3145732
  125.7 25.6 %copy-start.13 = (f32[2048]{0:T(1024)S(1)}, f32[2048]{0:T(1024)}, u32[]{:S(2)}) copy-start(f32[2048]{0:T(1024)} %param.12) | copy-start | bytes 24580
where the time goes:
time: 157 us; the launch traced here: 156 us
  waiting for transfers between devices  46.1 us (29%)
  other arithmetic  40.2 us (26%)
  matrix products  39.9 us (25%)
  starting transfers between devices  15.4 us (10%)
  local copies, waits for them, and re-layouts  14.4 us (9%)
    ppermute x4, waiting for transfers between devices, swapped(): return lax.ppermute(block, axis, route)  46.1 us
    dot_general x1, matrix products, local(): jnp.einsum('hij,jhd->ihd', weighted, value_rows, preferred_element_type=j...  25.6 us
    unnamed x3, other arithmetic  18.5 us
    ppermute x3, starting transfers between devices, passed_along(): return lax.ppermute(block, axis, route)  9.24 us
    dot_general x1, matrix products, local(): jnp.einsum('ijl,hli->hij', onehot, level_weight[:, :tok_bits + 1, :], pre...  7.69 us
    select_n x1, other arithmetic, local(): jnp.where(keep_rows[:, None, None], key_rows, jnp.zeros_like(key_rows))  6.87 us
    ppermute x4, starting transfers between devices, swapped(): return lax.ppermute(block, axis, route)  6.18 us
    dot_general x1, matrix products, local(): jnp.einsum('thd,lhde->lthe', queries, stacked, preferred_element_type=jnp...  5.1 us
  transfers between devices with their start and end apart: 7, of which 4 were waited for; matrix products, arithmetic and copies ran while one was open for 31% of the time, Pallas kernels for 0%

commit v1 on v0

v1 whole, which is shorter than its diff:
```python
import functools

import jax
import jax.numpy as jnp
from jax import lax
from jax.experimental import pallas as pl
from jax.experimental.pallas import tpu as pltpu
from jax.sharding import PartitionSpec as P

LANES = 128
PAD = 8
NT = (((1,), (1,)), ((), ()))
VMEM_LIMIT = 40 * 1024 * 1024


def exchange(block, partner):
    count = lax.axis_size("seq")
    route = [(i, partner(i)) for i in range(count) if partner(i) is not None]
    return lax.ppermute(block, "seq", route)


def swapped(block, bit):
    return exchange(block, lambda i: i ^ (1 << bit))


def sent_up(block, bit):
    return exchange(block, lambda i: None if i >> bit & 1 else i | 1 << bit)


def start_at(docs_ref, doc_count, positions):
    def step(i, start):
        doc = docs_ref[i]
        return jnp.where(positions >= doc, doc, start)

    return lax.fori_loop(0, doc_count, step, jnp.zeros_like(positions))


def silu(values):
    return values * (0.5 + 0.5 * jnp.tanh(0.5 * values))


def fill_window(window_ref, rim, rows):
    rim_rows = rim.shape[0]
    window_ref[0:PAD, :] = jnp.concatenate(
        [jnp.zeros((PAD - rim_rows, rim.shape[1]), jnp.float32), rim.astype(jnp.float32)], axis=0
    )
    window_ref[PAD:, :] = rows.astype(jnp.float32)


def convolved(window_ref, taps, distance, first, count):
    summed = taps[0:1, :] * window_ref[pl.ds(PAD + first, count), :]
    for offset in range(1, taps.shape[0]):
        term = taps[offset : offset + 1, :] * window_ref[pl.ds(PAD + first - offset, count), :]
        summed = summed + jnp.where(distance >= offset, term, 0.0)
    return summed


def logical_place(head, core_bit, y_bit):
    return ((head >> 3) ^ core_bit) * 8 + (((head >> 2) & 1) ^ y_bit) * 4 + (head & 3)


def distance_rows(docs_ref, doc_count, first_pos, row_count):
    positions = first_pos + lax.broadcasted_iota(jnp.int32, (row_count, LANES), 0)
    return positions - start_at(docs_ref, doc_count, positions)


def key_value_kernel(
    docs_ref,
    key_ref,
    value_ref,
    key_rim_ref,
    value_rim_ref,
    key_taps_ref,
    value_taps_ref,
    key_out_ref,
    value_out_ref,
    state_ref,
    window_ref,
    distance_ref,
    *,
    doc_count,
    chunk,
):
    step = pl.program_id(0)
    row_count, width = key_ref.shape
    heads = width // LANES
    index = lax.axis_index("seq")
    first_pos = index * row_count

    @pl.when(step == 0)
    def _():
        distance_ref[...] = distance_rows(docs_ref, doc_count, first_pos, row_count)

    last_pos = first_pos + row_count - 1
    last_start = start_at(docs_ref, doc_count, jnp.full((1, row_count), last_pos, jnp.int32))
    lanes_pos = first_pos + lax.broadcasted_iota(jnp.int32, (1, row_count), 1)
    keep = jnp.where(lanes_pos >= last_start, 1.0, 0.0)
    for which in range(heads):
        cols = slice(which * LANES, (which + 1) * LANES)
        key_window = window_ref.at[2 * which]
        value_window = window_ref.at[2 * which + 1]
        fill_window(key_window, key_rim_ref[:, cols], key_ref[:, cols])
        fill_window(value_window, value_rim_ref[:, cols], value_ref[:, cols])
        key_taps = key_taps_ref[:, cols]
        value_taps = value_taps_ref[:, cols]
        total = jnp.zeros((LANES, LANES), jnp.float32)
        for first in range(0, row_count, chunk):
            distance = distance_ref[pl.ds(first, chunk), :]
            grown = silu(convolved(key_window, key_taps, distance, first, chunk))
            square = jnp.sum(grown * grown, axis=1, keepdims=True)
            keys = (grown * lax.rsqrt(square + 1e-6)).astype(jnp.bfloat16)
            key_out_ref[pl.ds(first, chunk), cols] = keys
            values = silu(convolved(value_window, value_taps, distance, first, chunk))
            turned = values.T
            value_out_ref[cols, pl.ds(first, chunk)] = turned.astype(jnp.bfloat16)
            kept = (turned * keep[:, first : first + chunk]).astype(jnp.bfloat16)
            total = total + jnp.dot(kept, keys, preferred_element_type=jnp.float32)
        head = step * heads + which
        place = logical_place(head, index & 1, (index >> 1) & 1)
        state_ref[place] = total.astype(jnp.bfloat16)


def near_kernel(
    docs_ref,
    query_ref,
    query_rim_ref,
    query_taps_ref,
    level_ref,
    key_ref,
    value_ref,
    query_out_ref,
    near_ref,
    window_ref,
    distance_ref,
    start_ref,
    coarse_ref,
    *pair_refs,
    doc_count,
    chunk,
):
    step = pl.program_id(0)
    row_count = query_ref.shape[0]
    index = lax.axis_index("seq")
    first_pos = index * row_count
    span = 2 * LANES

    @pl.when(step == 0)
    def _():
        distance_ref[...] = distance_rows(docs_ref, doc_count, first_pos, row_count)
        positions = first_pos + lax.broadcasted_iota(jnp.int32, (8, row_count), 1)
        start_ref[...] = start_at(docs_ref, doc_count, positions) - first_pos
        for pair_ref in pair_refs:
            pair_ref[...] = jnp.zeros_like(pair_ref)

    fill_window(window_ref, query_rim_ref[...], query_ref[...])
    taps = query_taps_ref[...]
    for first in range(0, row_count, chunk):
        distance = distance_ref[pl.ds(first, chunk), :]
        grown = silu(convolved(window_ref, taps, distance, first, chunk))
        query_out_ref[pl.ds(first, chunk), :] = grown.astype(jnp.bfloat16)

    weights = level_ref[0].astype(jnp.float32)
    tok_bits = row_count.bit_length() - 1
    scaled = [weights[lv : lv + 1, :] * 2.0 ** (-lv / 2) for lv in range(tok_bits + 1)]
    row = lax.broadcasted_iota(jnp.int32, (8, row_count), 0)
    lane = lax.broadcasted_iota(jnp.int32, (8, row_count), 1)
    low = row ^ (lane & 7)
    fine = jnp.where(
        low == 0,
        scaled[0],
        jnp.where(low == 1, scaled[1], jnp.where(low < 4, scaled[2], scaled[3])),
    )
    fine = jnp.where(row > (lane & 7), 0.0, fine)
    row = lax.broadcasted_iota(jnp.int32, (16, row_count), 0)
    group = (lax.broadcasted_iota(jnp.int32, (16, row_count), 1) >> 3) & 15
    high = row ^ group
    coarse = jnp.where(
        high < 2,
        scaled[4],
        jnp.where(high < 4, scaled[5], jnp.where(high < 8, scaled[6], scaled[7])),
    )
    coarse = jnp.where(row > group, 0.0, coarse)
    for tile in range(row_count // LANES):
        coarse_ref[tile] = coarse[:, tile * LANES : (tile + 1) * LANES]
    lane_group = lax.broadcasted_iota(jnp.int32, (8, LANES), 1) >> 3
    sublane = lax.broadcasted_iota(jnp.int32, (LANES, LANES), 0)

    for part, pair_ref in enumerate(pair_refs):
        rows = (part + 1) * span
        scores = lax.dot_general(
            key_ref[0:rows, :],
            query_out_ref[part * span : rows, :],
            NT,
            preferred_element_type=jnp.float32,
        )
        for side in range(2):
            tile = 2 * part + side
            lanes = slice(tile * LANES, (tile + 1) * LANES)
            starts = start_ref[0:1, lanes]
            fine_tile = fine[:, lanes]
            for other in range(tile + 1):
                if other == tile:
                    weight = jnp.concatenate(
                        [
                            jnp.where(
                                lane_group == a,
                                fine_tile,
                                coarse_ref[tile, pl.ds(a, 8, stride=0), :],
                            )
                            for a in range(LANES // 8)
                        ],
                        axis=0,
                    )
                else:
                    weight = scaled[7 + (tile ^ other).bit_length()][:, lanes]
                piece = scores[
                    other * LANES : (other + 1) * LANES, side * LANES : (side + 1) * LANES
                ]
                valid = sublane >= starts - other * LANES
                pair_ref[
                    other * LANES : (other + 1) * LANES, side * LANES : (side + 1) * LANES
                ] = jnp.where(valid, piece * weight, 0.0).astype(jnp.bfloat16)
        near_ref[:, part * span : rows] = jnp.dot(
            value_ref[:, 0:rows], pair_ref[...], preferred_element_type=jnp.float32
        )


def far_kernel(
    docs_ref,
    query_ref,
    near_ref,
    level_ref,
    first_state_ref,
    own_state_ref,
    other_state_ref,
    gain_ref,
    out_ref,
    start_ref,
    *,
    doc_count,
    dev_bits,
):
    head = pl.program_id(0)
    row_count = query_ref.shape[0]
    index = lax.axis_index("seq")
    first_pos = index * row_count

    @pl.when(head == 0)
    def _():
        positions = first_pos + lax.broadcasted_iota(jnp.int32, (8, row_count), 1)
        start_ref[...] = start_at(docs_ref, doc_count, positions)

    core_bit = index & 1
    y_bit = (index >> 1) & 1
    tok_bits = row_count.bit_length() - 1
    first_place = logical_place(head, 1 - core_bit, y_bit)
    place = logical_place(head, core_bit, y_bit)
    is_own = place < 8
    states = [first_state_ref[first_place]]
    for level in range(dev_bits - 1):
        states.append(
            jnp.where(is_own, own_state_ref[level, place & 7], other_state_ref[level, place & 7])
        )
    images = lax.dot_general(
        jnp.concatenate(states, axis=0), query_ref[...], NT, preferred_element_type=jnp.float32
    )
    weights = level_ref[0].astype(jnp.float32)
    starts = start_ref[0:1, :]
    summed = near_ref[...]
    for bit in range(dev_bits):
        level_id = tok_bits + 1 + bit
        limit = jnp.where((index >> bit) & 1 == 1, (index >> bit << bit) * row_count, 0)
        coef = jnp.where(
            starts < limit, weights[level_id : level_id + 1, :] * 2.0 ** (-level_id / 2), 0.0
        )
        summed = summed + coef * images[bit * LANES : (bit + 1) * LANES, :]
    mean = jnp.mean(summed * summed, axis=0, keepdims=True)
    normed = summed * lax.rsqrt(mean + 1e-6)
    out_ref[...] = (normed.T * gain_ref[0]).astype(jnp.bfloat16)


def local(query_in, key_in, value_in, conv_weight, level_weight, out_gain, doc_starts):
    row_count, width_all = query_in.shape
    head_count, level_count, _ = level_weight.shape
    head_size = width_all // head_count
    conv_width = conv_weight.shape[0]
    doc_count = doc_starts.shape[0]
    dev_index = lax.axis_index("seq")
    dev_count = lax.axis_size("seq")
    dev_bits = dev_count.bit_length() - 1
    rim_rows = conv_width - 1
    params = pltpu.CompilerParams(vmem_limit_bytes=VMEM_LIMIT)
    smem = pl.BlockSpec(memory_space=pltpu.SMEM)
    whole = pl.BlockSpec(memory_space=pltpu.VMEM)

    tails = jnp.concatenate(
        [query_in[row_count - rim_rows :], key_in[row_count - rim_rows :], value_in[row_count - rim_rows :]],
        axis=1,
    )
    rims = exchange(tails, lambda i: i + 1 if i + 1 < dev_count else None)

    heads = 2
    steps = head_count // heads
    wide = heads * head_size
    keys, values_t, state = pl.pallas_call(
        functools.partial(key_value_kernel, doc_count=doc_count, chunk=LANES),
        grid=(steps,),
        in_specs=[
            smem,
            pl.BlockSpec((row_count, wide), lambda i: (0, i)),
            pl.BlockSpec((row_count, wide), lambda i: (0, i)),
            pl.BlockSpec((rim_rows, wide), lambda i: (0, steps + i)),
            pl.BlockSpec((rim_rows, wide), lambda i: (0, 2 * steps + i)),
            pl.BlockSpec((conv_width, wide), lambda i: (0, steps + i)),
            pl.BlockSpec((conv_width, wide), lambda i: (0, 2 * steps + i)),
        ],
        out_specs=[
            pl.BlockSpec((row_count, wide), lambda i: (0, i)),
            pl.BlockSpec((wide, row_count), lambda i: (i, 0)),
            pl.BlockSpec((head_count, head_size, head_size), lambda i: (0, 0, 0)),
        ],
        out_shape=[
            jax.ShapeDtypeStruct((row_count, width_all), jnp.bfloat16),
            jax.ShapeDtypeStruct((width_all, row_count), jnp.bfloat16),
            jax.ShapeDtypeStruct((head_count, head_size, head_size), jnp.bfloat16),
        ],
        scratch_shapes=[
            pltpu.VMEM((2 * heads, row_count + PAD, LANES), jnp.float32),
            pltpu.VMEM((row_count, LANES), jnp.int32),
        ],
        compiler_params=params,
        cost_estimate=pl.CostEstimate(flops=300_000_000, bytes_accessed=8_000_000, transcendentals=2_000_000),
        name="key_value",
    )(doc_starts, key_in, value_in, rims, rims, conv_weight, conv_weight)

    def joined(mine, theirs, bit):
        stride = 1 << bit
        upper_first = ((dev_index >> bit + 1 << bit + 1) + stride) * row_count
        upper_has = jnp.any(
            (doc_starts >= upper_first) & (doc_starts < upper_first + stride * row_count)
        )
        mine = mine.astype(jnp.float32)
        theirs = theirs.astype(jnp.float32)
        is_upper = dev_index >> bit & 1 == 1
        keep_mine = jnp.where(upper_has & ~is_upper, 0.0, 1.0)
        keep_theirs = jnp.where(upper_has & is_upper, 0.0, 1.0)
        return (mine * keep_mine + theirs * keep_theirs).astype(jnp.bfloat16)

    half = head_count // 2
    quarter = head_count // 4
    first_state = swapped(state, 0)
    pair = joined(state[:half], first_state[half:], 0)
    pair_in = swapped(pair[quarter:], 1)
    carried = joined(pair[:quarter], pair_in, 1)
    received = []
    for bit in range(2, dev_bits):
        last = bit == dev_bits - 1
        arrived = sent_up(carried, bit) if last else swapped(carried, bit)
        received.append(arrived)
        if not last:
            carried = joined(carried, arrived, bit)

    grid = (head_count,)
    queries, near = pl.pallas_call(
        functools.partial(near_kernel, doc_count=doc_count, chunk=LANES),
        grid=grid,
        in_specs=[
            smem,
            pl.BlockSpec((row_count, head_size), lambda i: (0, i)),
            pl.BlockSpec((rim_rows, head_size), lambda i: (0, i)),
            pl.BlockSpec((conv_width, head_size), lambda i: (0, i)),
            pl.BlockSpec((1, level_count, row_count), lambda i: (i, 0, 0)),
            pl.BlockSpec((row_count, head_size), lambda i: (0, i)),
            pl.BlockSpec((head_size, row_count), lambda i: (i, 0)),
        ],
        out_specs=[
            pl.BlockSpec((row_count, head_size), lambda i: (0, i)),
            pl.BlockSpec((head_size, row_count), lambda i: (i, 0)),
        ],
        out_shape=[
            jax.ShapeDtypeStruct((row_count, width_all), jnp.bfloat16),
            jax.ShapeDtypeStruct((width_all, row_count), jnp.float32),
        ],
        scratch_shapes=[
            pltpu.VMEM((row_count + PAD, LANES), jnp.float32),
            pltpu.VMEM((row_count, LANES), jnp.int32),
            pltpu.VMEM((8, row_count), jnp.int32),
            pltpu.VMEM((row_count // LANES, 16, LANES), jnp.float32),
        ]
        + [
            pltpu.VMEM(((part + 1) * 2 * LANES, 2 * LANES), jnp.bfloat16)
            for part in range(row_count // (2 * LANES))
        ],
        compiler_params=params,
        cost_estimate=pl.CostEstimate(flops=2_000_000_000, bytes_accessed=14_000_000, transcendentals=1_000_000),
        name="near",
    )(doc_starts, query_in, rims, conv_weight, level_weight, keys, values_t)

    mine = jnp.stack([pair[:quarter]] + received)
    theirs = swapped(mine, 1)
    own = jnp.concatenate(
        [jnp.concatenate([pair_in[None], mine[1:]], axis=0), theirs], axis=1
    )
    other = swapped(own, 0)

    return pl.pallas_call(
        functools.partial(far_kernel, doc_count=doc_count, dev_bits=dev_bits),
        grid=grid,
        in_specs=[
            smem,
            pl.BlockSpec((row_count, head_size), lambda i: (0, i)),
            pl.BlockSpec((head_size, row_count), lambda i: (i, 0)),
            pl.BlockSpec((1, level_count, row_count), lambda i: (i, 0, 0)),
            whole,
            whole,
            whole,
            pl.BlockSpec((1, 1, head_size), lambda i: (i, 0, 0)),
        ],
        out_specs=pl.BlockSpec((row_count, head_size), lambda i: (0, i)),
        out_shape=jax.ShapeDtypeStruct((row_count, width_all), jnp.bfloat16),
        scratch_shapes=[pltpu.VMEM((8, row_count), jnp.int32)],
        compiler_params=params,
        cost_estimate=pl.CostEstimate(flops=1_000_000_000, bytes_accessed=10_000_000, transcendentals=10_000),
        name="far",
    )(
        doc_starts,
        queries,
        near,
        level_weight,
        first_state,
        own,
        other,
        out_gain.reshape(head_count, 1, head_size),
    )


def solution(mesh):
    in_specs = (
        P(("groups", "seq"), None),
        P(("groups", "seq"), None),
        P(("groups", "seq"), None),
        P(),
        P(None, None, ("groups", "seq")),
        P(),
        P("groups"),
    )
    out_specs = P(("groups", "seq"), None)
    return jax.shard_map(local, mesh=mesh, in_specs=in_specs, out_specs=out_specs, check_vma=False)
```

time: 157 us -> 93.3 us (0.59)
  the two profiles are of different devices: /device:TPU:0 before, /device:TPU:25 now
where the time goes in v1:
time: 93.3 us; the launch traced here: 92.7 us
  Pallas kernels  38.3 us (41%)
  waiting for transfers between devices  24.8 us (27%)
  local copies, waits for them, and re-layouts  14 us (15%)
  starting transfers between devices  10.5 us (11%)
  between operations  3.99 us (4%)
  other arithmetic  1.05 us (1%)
    ppermute x7, waiting for transfers between devices, exchange(): return lax.ppermute(block, 'seq', route)  24.8 us
    pallas_call x1, Pallas kernels, local(): pl.pallas_call(functools.partial(near_kernel, doc_count=doc_count, chunk=...  16.3 us
    pallas_call x1, Pallas kernels, local(): pl.pallas_call(functools.partial(key_value_kernel, doc_count=doc_count, c...  11.7 us
    unnamed x25, local copies, waits for them, and re-layouts  11.6 us
    ppermute x7, starting transfers between devices, exchange(): return lax.ppermute(block, 'seq', route)  10.5 us
    pallas_call x1, Pallas kernels, local(): pl.pallas_call(functools.partial(far_kernel, doc_count=doc_count, dev_bit...  10.4 us
  transfers between devices with their start and end apart: 7, of which 5 were waited for; matrix products, arithmetic and copies ran while one was open for 2% of the time, Pallas kernels for 18%

profile of v1, /device:TPU:25, one launch (start us, length us, event | category | flops | bytes accessed | tf_op | source)
XLA Modules:
  0.0 92.7 jit_solution(8435060571185712513)
XLA Ops:
  0.0 0.8 slice.26
  0.8 0.8 slice.25
  1.5 0.8 slice.24
  2.4 3.7 %collective-permute-start = (bf16[3,6144]{1,0:T(4,128)(2,1)S(1)}, bf16[3,6144]{1,0:T(4,128)(2,1)S(1)}, u32[]{:S(2)}, u32[]{:S(2)}) collective-permute-start(bf16[3,6144]{1,0:T(4,128)(2,1)S(1)} %pad_maximum_fusion.2), channel_id=1, source_target_pairs={{0,1},{1,2},{2,3},{3,4},{4,5},{5,6},{6,7},{7,8},{8,9},{9,10},{10,1... | collective-permute-start | bytes 110600 | tf_op jit(solution)/shard_map/ppermute | solution.py:19
  6.1 1.2 %collective-permute-done.key_rim_ref.value_rim_ref.query_rim_ref = bf16[3,6144]{1,0:T(4,128)(2,1)S(1)} collective-permute-done((bf16[3,6144]{1,0:T(4,128)(2,1)S(1)}, bf16[3,6144]{1,0:T(4,128)(2,1)S(1)}, u32[]{:S(2)}, u32[]{:S(2)}) %collective-permute-start) | collective-permute-done | bytes 36896 | tf_op jit(solution)/shard_map/ppermute | solution.py:19
  7.2 1.6 %copy-done = bf16[512,2048]{1,0:T(8,128)(2,1)S(1)} copy-done((bf16[512,2048]{1,0:T(8,128)(2,1)S(1)}, bf16[512,2048]{1,0:T(8,128)(2,1)}, u32[]{:S(2)}) %copy-start) | copy-done | bytes 2097176
  8.8 1.6 %copy-done.1 = bf16[512,2048]{1,0:T(8,128)(2,1)S(1)} copy-done((bf16[512,2048]{1,0:T(8,128)(2,1)S(1)}, bf16[512,2048]{1,0:T(8,128)(2,1)}, u32[]{:S(2)}) %copy-start.1) | copy-done | bytes 2097176
  10.4 0.9 copy-done.2
  11.3 0.7 copy-done.5
  12.0 11.7 %key_value.1 = (bf16[512,2048]{1,0:T(8,128)(2,1)S(1)}, bf16[2048,512]{1,0:T(8,128)(2,1)S(1)}, bf16[16,128,128]{2,1,0:T(8,128)(2,1)S(1)}) custom-call(s32[8]{0:T(128)S(1)} %copy-done.5, bf16[512,2048]{1,0:T(8,128)(2,1)S(1)} %copy-done.1, bf16[512,2048]{1,0:T(8,128)(2,1)S(1)} %copy-done, ...), custom_call_target="tpu_custom_call" | custom-call | flops 300000000 | bytes 8000000 | tf_op jit(solution)/shard_map/key_value/pallas_call | solution.py:305
  23.7 1.3 %copy-done.8 = bf16[512,2048]{1,0:T(8,128)(2,1)} copy-done((bf16[512,2048]{1,0:T(8,128)(2,1)}, bf16[512,2048]{1,0:T(8,128)(2,1)S(1)}, u32[]{:S(2)}) %copy-start.8) | copy-done | bytes 2097176
  25.0 1.3 %copy-done.10 = bf16[2048,512]{1,0:T(8,128)(2,1)} copy-done((bf16[2048,512]{1,0:T(8,128)(2,1)}, bf16[2048,512]{1,0:T(8,128)(2,1)S(1)}, u32[]{:S(2)}) %copy-start.10) | copy-done | bytes 2097176
  26.3 2.1 %collective-permute-start.1 = (bf16[16,128,128]{2,1,0:T(8,128)(2,1)S(1)}, bf16[16,128,128]{2,1,0:T(8,128)(2,1)S(1)}, u32[]{:S(2)}, u32[]{:S(2)}) collective-permute-start(bf16[16,128,128]{2,1,0:T(8,128)(2,1)S(1)} %get-tuple-element.14), channel_id=1, source_target_pairs={{0,1},{1,0},{2,3},{3,2},{4,5},{5,4},{6,7},{7,6},{8,9},{9,8},{10,11... | collective-permute-start | bytes 1572872 | tf_op jit(solution)/shard_map/ppermute | solution.py:19
  28.5 0.7 and_reduce_fusion
  30.3 0.1 add_convert_fusion
  30.4 0.4 collective-permute-start.2
  32.3 3.2 %collective-permute-done.2 = bf16[4,128,128]{2,1,0:T(8,128)(2,1)S(1)} collective-permute-done((bf16[4,128,128]{2,1,0:T(8,128)(2,1)S(1)}, bf16[4,128,128]{2,1,0:T(8,128)(2,1)S(1)}, u32[]{:S(2)}, u32[]{:S(2)}) %collective-permute-start.2) | collective-permute-done | bytes 131104 | tf_op jit(solution)/shard_map/ppermute | solution.py:19
  35.6 0.1 add_convert_fusion.2
  35.6 0.2 collective-permute-start.3
  37.1 2.8 %collective-permute-done.3 = bf16[4,128,128]{2,1,0:T(8,128)(2,1)S(1)} collective-permute-done((bf16[4,128,128]{2,1,0:T(8,128)(2,1)S(1)}, bf16[4,128,128]{2,1,0:T(8,128)(2,1)S(1)}, u32[]{:S(2)}, u32[]{:S(2)}) %collective-permute-start.3) | collective-permute-done | bytes 131104 | tf_op jit(solution)/shard_map/ppermute | solution.py:19
  39.9 0.1 add_convert_fusion.1
  39.9 1.3 %collective-permute-start.4 = (bf16[4,128,128]{2,1,0:T(8,128)(2,1)S(1)}, bf16[4,128,128]{2,1,0:T(8,128)(2,1)S(1)}, u32[]{:S(2)}, u32[]{:S(2)}) collective-permute-start(bf16[4,128,128]{2,1,0:T(8,128)(2,1)S(1)} %add_convert_fusion.1), channel_id=1, source_target_pairs={{0,8},{1,9},{2,10},{3,11},{4,12},{5,13},{6,14},{7,15},{16,24},{17,... | collective-permute-start | bytes 393224 | tf_op jit(solution)/shard_map/ppermute | solution.py:19
  41.2 8.7 %collective-permute-done.4 = bf16[4,128,128]{2,1,0:T(8,128)(2,1)S(1)} collective-permute-done((bf16[4,128,128]{2,1,0:T(8,128)(2,1)S(1)}, bf16[4,128,128]{2,1,0:T(8,128)(2,1)S(1)}, u32[]{:S(2)}, u32[]{:S(2)}) %collective-permute-start.4) | collective-permute-done | bytes 131104 | tf_op jit(solution)/shard_map/ppermute | solution.py:19
  50.0 0.4 collective-permute-start.5
  50.4 8.9 %collective-permute-done.5 = bf16[3,4,128,128]{3,2,1,0:T(8,128)(2,1)S(1)} collective-permute-done((bf16[3,4,128,128]{3,2,1,0:T(8,128)(2,1)S(1)}, bf16[3,4,128,128]{3,2,1,0:T(8,128)(2,1)S(1)}, u32[]{:S(2)}, u32[]{:S(2)}) %collective-permute-start.5) | collective-permute-done | bytes 393248 | tf_op jit(solution)/shard_map/ppermute | solution.py:19
  59.3 0.1 pad_maximum_fusion.own_state_ref
  59.4 2.4 %collective-permute-start.6 = (bf16[3,8,128,128]{3,2,1,0:T(8,128)(2,1)S(1)}, bf16[3,8,128,128]{3,2,1,0:T(8,128)(2,1)S(1)}, u32[]{:S(2)}, u32[]{:S(2)}) collective-permute-start(bf16[3,8,128,128]{3,2,1,0:T(8,128)(2,1)S(1)} %pad_maximum_fusion.own_state_ref), channel_id=1, source_target_pairs={{0,1},{1,0},{2,3},{3,2},{4,5},{5,4},{6,7},{7,6},{8,9},{9,8},{10,11... | collective-permute-start | bytes 2359304 | tf_op jit(solution)/shard_map/ppermute | solution.py:19
  61.7 1.1 %copy.8.level_ref = bf16[16,14,512]{2,1,0:T(8,128)(2,1)S(1)} copy(bf16[16,14,512]{2,0,1:T(8,128)(2,1)} %param.11) | data formatting | bytes 458752 | tf_op args[4]
  62.8 1.6 %copy-done.9 = bf16[512,2048]{1,0:T(8,128)(2,1)S(1)} copy-done((bf16[512,2048]{1,0:T(8,128)(2,1)S(1)}, bf16[512,2048]{1,0:T(8,128)(2,1)}, u32[]{:S(2)}) %copy-start.9) | copy-done | bytes 2097176
  64.4 1.6 %copy-done.11 = bf16[2048,512]{1,0:T(8,128)(2,1)S(1)} copy-done((bf16[2048,512]{1,0:T(8,128)(2,1)S(1)}, bf16[2048,512]{1,0:T(8,128)(2,1)}, u32[]{:S(2)}) %copy-start.11) | copy-done | bytes 2097176
  66.0 16.3 %near.1 = (bf16[512,2048]{1,0:T(8,128)(2,1)S(1)}, f32[2048,512]{1,0:T(8,128)S(1)}) custom-call(s32[8]{0:T(128)S(1)} %copy-done.6, bf16[512,2048]{1,0:T(8,128)(2,1)S(1)} %copy-done.7, bf16[3,6144]{1,0:T(4,128)(2,1)S(1)} %collective-permute-done.key_rim_ref.value_rim_ref.query_rim_ref, f32[4,6144]{1,0:T(4,128)S(1)} %copy-done.3, ...), custom_call_target="tpu_custom_call" | custom-call | flops 2000000000 | bytes 14000000 | tf_op jit(solution)/shard_map/near/pallas_call | solution.py:364
  82.3 10.4 %far.1 = bf16[512,2048]{1,0:T(8,128)(2,1)} custom-call(s32[8]{0:T(128)S(1)} %copy-done.6, bf16[512,2048]{1,0:T(8,128)(2,1)S(1)} %get-tuple-element.12.query_ref, f32[2048,512]{1,0:T(8,128)S(1)} %get-tuple-element.13.near_ref, bf16[16,14,512]{2,1,0:T(8,128)(2,1)S(1)} %copy.8.level_ref, bf16[16,128,128]{2,1,0:T(8,128)(2,1)S(1)} %collective-permute-done.1.first_state_ref, ...), custom_call_target="tpu_custom_call" | custom-call | flops 1000000000 | bytes 10000000 | tf_op jit(solution)/shard_map/far/pallas_call | solution.py:406
  (21 shorter events, 0.1 us)
Async XLA Ops:
  2.3 26.1 %copy-start.6 = (s32[8]{0:T(128)S(1)}, s32[8]{0:T(128)}, u32[]{:S(2)}) copy-start(s32[8]{0:T(128)} %docs_ref.5) | copy-start | bytes 100
  2.4 4.9 %collective-permute-start = (bf16[3,6144]{1,0:T(4,128)(2,1)S(1)}, bf16[3,6144]{1,0:T(4,128)(2,1)S(1)}, u32[]{:S(2)}, u32[]{:S(2)}) collective-permute-start(bf16[3,6144]{1,0:T(4,128)(2,1)S(1)} %pad_maximum_fusion.2), channel_id=1, source_target_pairs={{0,1},{1,2},{2,3},{3,4},{4,5},{5,6},{6,7},{7,8},{8,9},{9,10},{10,1... | collective-permute-start | bytes 110600 | tf_op jit(solution)/shard_map/ppermute | solution.py:19
  7.2 1.6 %copy-start = (bf16[512,2048]{1,0:T(8,128)(2,1)S(1)}, bf16[512,2048]{1,0:T(8,128)(2,1)}, u32[]{:S(2)}) copy-start(bf16[512,2048]{1,0:T(8,128)(2,1)} %value_ref.1) | copy-start | bytes 6291460
  8.8 1.6 %copy-start.1 = (bf16[512,2048]{1,0:T(8,128)(2,1)S(1)}, bf16[512,2048]{1,0:T(8,128)(2,1)}, u32[]{:S(2)}) copy-start(bf16[512,2048]{1,0:T(8,128)(2,1)} %key_ref.1) | copy-start | bytes 6291460
  10.4 0.9 copy-start.2
  11.3 0.7 copy-start.5
  23.7 1.3 %copy-start.8 = (bf16[512,2048]{1,0:T(8,128)(2,1)}, bf16[512,2048]{1,0:T(8,128)(2,1)S(1)}, u32[]{:S(2)}) copy-start(bf16[512,2048]{1,0:T(8,128)(2,1)S(1)} %get-tuple-element.10.key_ref) | copy-start | bytes 6291460
  25.0 1.3 %copy-start.10 = (bf16[2048,512]{1,0:T(8,128)(2,1)}, bf16[2048,512]{1,0:T(8,128)(2,1)S(1)}, u32[]{:S(2)}) copy-start(bf16[2048,512]{1,0:T(8,128)(2,1)S(1)} %get-tuple-element.11.value_ref) | copy-start | bytes 6291460
  26.3 3.9 %collective-permute-start.1 = (bf16[16,128,128]{2,1,0:T(8,128)(2,1)S(1)}, bf16[16,128,128]{2,1,0:T(8,128)(2,1)S(1)}, u32[]{:S(2)}, u32[]{:S(2)}) collective-permute-start(bf16[16,128,128]{2,1,0:T(8,128)(2,1)S(1)} %get-tuple-element.14), channel_id=1, source_target_pairs={{0,1},{1,0},{2,3},{3,2},{4,5},{5,4},{6,7},{7,6},{8,9},{9,8},{10,11... | collective-permute-start | bytes 1572872 | tf_op jit(solution)/shard_map/ppermute | solution.py:19
  30.4 32.4 %copy-start.3 = (f32[4,6144]{1,0:T(4,128)S(1)}, f32[4,6144]{1,0:T(4,128)}, u32[]{:S(2)}) copy-start(f32[4,6144]{1,0:T(4,128)} %query_taps_ref.1) | copy-start | bytes 294916
  30.4 32.4 %copy-start.7 = (bf16[512,2048]{1,0:T(8,128)(2,1)S(1)}, bf16[512,2048]{1,0:T(8,128)(2,1)}, u32[]{:S(2)}) copy-start(bf16[512,2048]{1,0:T(8,128)(2,1)} %query_ref.1) | copy-start | bytes 6291460
  30.4 5.1 %collective-permute-start.2 = (bf16[4,128,128]{2,1,0:T(8,128)(2,1)S(1)}, bf16[4,128,128]{2,1,0:T(8,128)(2,1)S(1)}, u32[]{:S(2)}, u32[]{:S(2)}) collective-permute-start(bf16[4,128,128]{2,1,0:T(8,128)(2,1)S(1)} %get-tuple-element.19), channel_id=1, source_target_pairs={{0,2},{1,3},{2,0},{3,1},{4,6},{5,7},{6,4},{7,5},{8,10},{9,11},{10,... | collective-permute-start | bytes 393224 | tf_op jit(solution)/shard_map/ppermute | solution.py:19
  35.6 4.2 %collective-permute-start.3 = (bf16[4,128,128]{2,1,0:T(8,128)(2,1)S(1)}, bf16[4,128,128]{2,1,0:T(8,128)(2,1)S(1)}, u32[]{:S(2)}, u32[]{:S(2)}) collective-permute-start(bf16[4,128,128]{2,1,0:T(8,128)(2,1)S(1)} %add_convert_fusion.2), channel_id=1, source_target_pairs={{0,4},{1,5},{2,6},{3,7},{4,0},{5,1},{6,2},{7,3},{8,12},{9,13},{10,... | collective-permute-start | bytes 393224 | tf_op jit(solution)/shard_map/ppermute | solution.py:19
  39.9 10.0 %collective-permute-start.4 = (bf16[4,128,128]{2,1,0:T(8,128)(2,1)S(1)}, bf16[4,128,128]{2,1,0:T(8,128)(2,1)S(1)}, u32[]{:S(2)}, u32[]{:S(2)}) collective-permute-start(bf16[4,128,128]{2,1,0:T(8,128)(2,1)S(1)} %add_convert_fusion.1), channel_id=1, source_target_pairs={{0,8},{1,9},{2,10},{3,11},{4,12},{5,13},{6,14},{7,15},{16,24},{17,... | collective-permute-start | bytes 393224 | tf_op jit(solution)/shard_map/ppermute | solution.py:19
  50.0 9.3 %collective-permute-start.5 = (bf16[3,4,128,128]{3,2,1,0:T(8,128)(2,1)S(1)}, bf16[3,4,128,128]{3,2,1,0:T(8,128)(2,1)S(1)}, u32[]{:S(2)}, u32[]{:S(2)}) collective-permute-start(bf16[3,4,128,128]{3,2,1,0:T(8,128)(2,1)S(1)} %pad_maximum_fusion.1), channel_id=1, source_target_pairs={{0,2},{1,3},{2,0},{3,1},{4,6},{5,7},{6,4},{7,5},{8,10},{9,11},{10,... | collective-permute-start | bytes 1179656 | tf_op jit(solution)/shard_map/ppermute | solution.py:19
  59.4 22.9 %collective-permute-start.6 = (bf16[3,8,128,128]{3,2,1,0:T(8,128)(2,1)S(1)}, bf16[3,8,128,128]{3,2,1,0:T(8,128)(2,1)S(1)}, u32[]{:S(2)}, u32[]{:S(2)}) collective-permute-start(bf16[3,8,128,128]{3,2,1,0:T(8,128)(2,1)S(1)} %pad_maximum_fusion.own_state_ref), channel_id=1, source_target_pairs={{0,1},{1,0},{2,3},{3,2},{4,5},{5,4},{6,7},{7,6},{8,9},{9,8},{10,11... | collective-permute-start | bytes 2359304 | tf_op jit(solution)/shard_map/ppermute | solution.py:19
  62.8 1.6 %copy-start.9 = (bf16[512,2048]{1,0:T(8,128)(2,1)S(1)}, bf16[512,2048]{1,0:T(8,128)(2,1)}, u32[]{:S(2)}) copy-start(bf16[512,2048]{1,0:T(8,128)(2,1)} %copy-done.8) | copy-start | bytes 6291460
  64.4 1.6 %copy-start.11 = (bf16[2048,512]{1,0:T(8,128)(2,1)S(1)}, bf16[2048,512]{1,0:T(8,128)(2,1)}, u32[]{:S(2)}) copy-start(bf16[2048,512]{1,0:T(8,128)(2,1)} %copy-done.10) | copy-start | bytes 6291460
  66.0 16.3 %copy-start.4 = (f32[2048]{0:T(1024)S(1)}, f32[2048]{0:T(1024)}, u32[]{:S(2)}) copy-start(f32[2048]{0:T(1024)} %param.12) | copy-start | bytes 24580

commit v2 on v1

--- a/solution.py
+++ b/solution.py
@@ -10,7 +10,7 @@
 LANES = 128
 PAD = 8
 NT = (((1,), (1,)), ((), ()))
-VMEM_LIMIT = 40 * 1024 * 1024
+VMEM_LIMIT = 56 * 1024 * 1024
 
 
 def exchange(block, partner):
@@ -62,6 +62,14 @@
 def distance_rows(docs_ref, doc_count, first_pos, row_count):
     positions = first_pos + lax.broadcasted_iota(jnp.int32, (row_count, LANES), 0)
     return positions - start_at(docs_ref, doc_count, positions)
+
+
+def rim_kernel(query_ref, key_ref, value_ref, out_ref):
+    rim_rows = out_ref.shape[0]
+    width = query_ref.shape[1]
+    for part, ref in enumerate((query_ref, key_ref, value_ref)):
+        rows = ref.shape[0]
+        out_ref[:, part * width : (part + 1) * width] = ref[rows - rim_rows : rows, :]
 
 
 def key_value_kernel(
@@ -128,16 +136,14 @@
     level_ref,
     key_ref,
     value_ref,
-    query_out_ref,
-    near_ref,
-    window_ref,
-    distance_ref,
-    start_ref,
-    coarse_ref,
-    *pair_refs,
+    *rest,
     doc_count,
     chunk,
+    skipped,
 ):
+    query_out_ref, near_ref, window_ref, distance_ref, start_ref, coarse_ref, *pair_refs = rest[
+        skipped:
+    ]
     step = pl.program_id(0)
     row_count = query_ref.shape[0]
     index = lax.axis_index("seq")
@@ -293,10 +299,15 @@
     smem = pl.BlockSpec(memory_space=pltpu.SMEM)
     whole = pl.BlockSpec(memory_space=pltpu.VMEM)
 
-    tails = jnp.concatenate(
-        [query_in[row_count - rim_rows :], key_in[row_count - rim_rows :], value_in[row_count - rim_rows :]],
-        axis=1,
-    )
+    edge = 16
+    tails = pl.pallas_call(
+        rim_kernel,
+        grid=(1,),
+        in_specs=[pl.BlockSpec((edge, width_all), lambda i: (row_count // edge - 1, 0))] * 3,
+        out_specs=pl.BlockSpec((rim_rows, 3 * width_all), lambda i: (0, 0)),
+        out_shape=jax.ShapeDtypeStruct((rim_rows, 3 * width_all), query_in.dtype),
+        name="rim",
+    )(query_in, key_in, value_in)
     rims = exchange(tails, lambda i: i + 1 if i + 1 < dev_count else None)
 
     heads = 2
@@ -346,58 +357,84 @@
         keep_theirs = jnp.where(upper_has & is_upper, 0.0, 1.0)
         return (mine * keep_mine + theirs * keep_theirs).astype(jnp.bfloat16)
 
+    buffers = None
+    piece_heads = head_count // 4
+
+    def near_piece(piece, buffers, docs):
+        first = piece * piece_heads
+        aliased = {} if buffers is None else {7: 0, 8: 1}
+        extra_specs = [] if buffers is None else [pl.BlockSpec(memory_space=pl.ANY)] * 2
+        kernel = functools.partial(
+            near_kernel, doc_count=doc_count, chunk=LANES, skipped=len(extra_specs)
+        )
+        return pl.pallas_call(
+            kernel,
+            grid=(piece_heads,),
+            in_specs=[
+                smem,
+                pl.BlockSpec((row_count, head_size), lambda i: (0, first + i)),
+                pl.BlockSpec((rim_rows, head_size), lambda i: (0, first + i)),
+                pl.BlockSpec((conv_width, head_size), lambda i: (0, first + i)),
+                pl.BlockSpec((1, level_count, row_count), lambda i: (first + i, 0, 0)),
+                pl.BlockSpec((row_count, head_size), lambda i: (0, first + i)),
+                pl.BlockSpec((head_size, row_count), lambda i: (first + i, 0)),
+            ]
+            + extra_specs,
+            out_specs=[
+                pl.BlockSpec((row_count, head_size), lambda i: (0, first + i)),
+                pl.BlockSpec((head_size, row_count), lambda i: (first + i, 0)),
+            ],
+            out_shape=[
+                jax.ShapeDtypeStruct((row_count, width_all), jnp.bfloat16),
+                jax.ShapeDtypeStruct((width_all, row_count), jnp.float32),
+            ],
+            scratch_shapes=[
+                pltpu.VMEM((row_count + PAD, LANES), jnp.float32),
+                pltpu.VMEM((row_count, LANES), jnp.int32),
+                pltpu.VMEM((8, row_count), jnp.int32),
+                pltpu.VMEM((row_count // LANES, 16, LANES), jnp.float32),
+            ]
+            + [
+                pltpu.VMEM(((part + 1) * 2 * LANES, 2 * LANES), jnp.bfloat16)
+                for part in range(row_count // (2 * LANES))
+            ],
+            input_output_aliases=aliased,
+            compiler_params=params,
+            cost_estimate=pl.CostEstimate(
+                flops=500_000_000, bytes_accessed=3_500_000, transcendentals=300_000
+            ),
+            name="near",
+        )(docs, query_in, rims, conv_weight, level_weight, keys, values_t, *(buffers or ()))
+
+    def covered(payload, send, piece, buffers):
+        payload, docs = lax.optimization_barrier((payload, doc_starts))
+        arrived = send(payload)
+        buffers = near_piece(piece, buffers, docs)
+        arrived, buffers = lax.optimization_barrier((arrived, buffers))
+        return arrived, buffers
+
     half = head_count // 2
     quarter = head_count // 4
     first_state = swapped(state, 0)
     pair = joined(state[:half], first_state[half:], 0)
-    pair_in = swapped(pair[quarter:], 1)
+    pair_in, buffers = covered(pair[quarter:], lambda x: swapped(x, 1), 0, buffers)
     carried = joined(pair[:quarter], pair_in, 1)
     received = []
     for bit in range(2, dev_bits):
         last = bit == dev_bits - 1
-        arrived = sent_up(carried, bit) if last else swapped(carried, bit)
+        if last:
+            arrived, buffers = covered(carried, lambda x: sent_up(x, bit), 2, buffers)
+        elif bit == 2:
+            arrived, buffers = covered(carried, lambda x: swapped(x, bit), 1, buffers)
+        else:
+            arrived = swapped(carried, bit)
         received.append(arrived)
         if not last:
             carried = joined(carried, arrived, bit)
 
-    grid = (head_count,)
-    queries, near = pl.pallas_call(
-        functools.partial(near_kernel, doc_count=doc_count, chunk=LANES),
-        grid=grid,
-        in_specs=[
-            smem,
-            pl.BlockSpec((row_count, head_size), lambda i: (0, i)),
-            pl.BlockSpec((rim_rows, head_size), lambda i: (0, i)),
-            pl.BlockSpec((conv_width, head_size), lambda i: (0, i)),
-            pl.BlockSpec((1, level_count, row_count), lambda i: (i, 0, 0)),
-            pl.BlockSpec((row_count, head_size), lambda i: (0, i)),
-            pl.BlockSpec((head_size, row_count), lambda i: (i, 0)),
-        ],
-        out_specs=[
-            pl.BlockSpec((row_count, head_size), lambda i: (0, i)),
-            pl.BlockSpec((head_size, row_count), lambda i: (i, 0)),
-        ],
-        out_shape=[
-            jax.ShapeDtypeStruct((row_count, width_all), jnp.bfloat16),
-            jax.ShapeDtypeStruct((width_all, row_count), jnp.float32),
-        ],
-        scratch_shapes=[
-            pltpu.VMEM((row_count + PAD, LANES), jnp.float32),
-            pltpu.VMEM((row_count, LANES), jnp.int32),
-            pltpu.VMEM((8, row_count), jnp.int32),
-            pltpu.VMEM((row_count // LANES, 16, LANES), jnp.float32),
-        ]
-        + [
-            pltpu.VMEM(((part + 1) * 2 * LANES, 2 * LANES), jnp.bfloat16)
-            for part in range(row_count // (2 * LANES))
-        ],
-        compiler_params=params,
-        cost_estimate=pl.CostEstimate(flops=2_000_000_000, bytes_accessed=14_000_000, transcendentals=1_000_000),
-        name="near",
-    )(doc_starts, query_in, rims, conv_weight, level_weight, keys, values_t)
-
     mine = jnp.stack([pair[:quarter]] + received)
-    theirs = swapped(mine, 1)
+    theirs, buffers = covered(mine, lambda x: swapped(x, 1), 3, buffers)
+    queries, near = buffers
     own = jnp.concatenate(
         [jnp.concatenate([pair_in[None], mine[1:]], axis=0), theirs], axis=1
     )
@@ -405,7 +442,7 @@
 
     return pl.pallas_call(
         functools.partial(far_kernel, doc_count=doc_count, dev_bits=dev_bits),
-        grid=grid,
+        grid=(head_count,),
         in_specs=[
             smem,
             pl.BlockSpec((row_count, head_size), lambda i: (0, i)),

time: 93.3 us -> 84.3 us (0.904)
  the two profiles are of different devices: /device:TPU:25 before, /device:TPU:0 now
where the time goes in v2:
time: 84.3 us; the launch traced here: 83.4 us
  Pallas kernels  53 us (63%)
  starting transfers between devices  15.5 us (18%)
  waiting for transfers between devices  6.53 us (8%)
  between operations  3.76 us (4%)
  local copies, waits for them, and re-layouts  2.41 us (3%)
  other arithmetic  2.19 us (3%)
    pallas_call x4, Pallas kernels, near_piece(): pl.pallas_call(kernel, grid=(piece_heads,), in_specs=[smem, pl.BlockSpec(...  24.3 us
    ppermute x7, starting transfers between devices, exchange(): return lax.ppermute(block, 'seq', route)  15.5 us
    pallas_call x1, Pallas kernels, local(): pl.pallas_call(functools.partial(far_kernel, doc_count=doc_count, dev_bit...  14.4 us
    pallas_call x1, Pallas kernels, local(): pl.pallas_call(functools.partial(key_value_kernel, doc_count=doc_count, c...  12.8 us
    ppermute x7, waiting for transfers between devices, exchange(): return lax.ppermute(block, 'seq', route)  6.53 us
    unnamed x13, local copies, waits for them, and re-layouts  2.39 us
  transfers between devices with their start and end apart: 7, of which 3 were waited for; matrix products, arithmetic and copies ran while one was open for 2% of the time, Pallas kernels for 29%

profile of v2, /device:TPU:0, one launch (start us, length us, event | category | flops | bytes accessed | tf_op | source)
XLA Modules:
  0.0 83.4 jit_solution(5428213255464356870)
XLA Ops:
  0.0 1.5 %rim.1 = bf16[3,6144]{1,0:T(4,128)(2,1)} custom-call(bf16[512,2048]{1,0:T(8,128)(2,1)} %query_ref.9, bf16[512,2048]{1,0:T(8,128)(2,1)} %key_ref.3, bf16[512,2048]{1,0:T(8,128)(2,1)} %value_ref.3), custom_call_target="tpu_custom_call" | custom-call | tf_op jit(solution)/shard_map/rim/pallas_call | solution.py:303
  1.6 2.5 %collective-permute-start = (bf16[3,6144]{1,0:T(4,128)(2,1)}, bf16[3,6144]{1,0:T(4,128)(2,1)S(1)}, u32[]{:S(2)}, u32[]{:S(2)}) collective-permute-start(bf16[3,6144]{1,0:T(4,128)(2,1)} %rim.1), channel_id=1, source_target_pairs={{0,1},{1,2},{2,3},{3,4},{4,5},{5,6},{6,7},{7,8},{8,9},{9,10},{10,1... | collective-permute-start | bytes 110600 | tf_op jit(solution)/shard_map/ppermute | solution.py:19
  4.0 1.1 %collective-permute-done.key_rim_ref.value_rim_ref.query_rim_ref = bf16[3,6144]{1,0:T(4,128)(2,1)S(1)} collective-permute-done((bf16[3,6144]{1,0:T(4,128)(2,1)}, bf16[3,6144]{1,0:T(4,128)(2,1)S(1)}, u32[]{:S(2)}, u32[]{:S(2)}) %collective-permute-start) | collective-permute-done | bytes 36896 | tf_op jit(solution)/shard_map/ppermute | solution.py:19
  5.1 0.6 copy-done.1
  5.7 12.8 %key_value.1 = (bf16[512,2048]{1,0:T(8,128)(2,1)}, bf16[2048,512]{1,0:T(8,128)(2,1)}, bf16[16,128,128]{2,1,0:T(8,128)(2,1)}) custom-call(s32[8]{0:T(128)} %docs_ref.7, bf16[512,2048]{1,0:T(8,128)(2,1)} %key_ref.3, bf16[512,2048]{1,0:T(8,128)(2,1)} %value_ref.3, bf16[3,6144]{1,0:T(4,128)(2,1)} %copy-done.1, bf16[3,6144]{1,0:T(4,128)(2,1)} %copy-done.1, ...), custom_call_target="tpu_custom_call" | custom-call | flops 300000000 | bytes 8000000 | tf_op jit(solution)/shard_map/key_value/pallas_call | solution.py:316
  18.5 3.1 %collective-permute-start.1 = (bf16[16,128,128]{2,1,0:T(8,128)(2,1)}, bf16[16,128,128]{2,1,0:T(8,128)(2,1)S(1)}, u32[]{:S(2)}, u32[]{:S(2)}) collective-permute-start(bf16[16,128,128]{2,1,0:T(8,128)(2,1)} %get-tuple-element.36), channel_id=1, source_target_pairs={{0,1},{1,0},{2,3},{3,2},{4,5},{5,4},{6,7},{7,6},{8,9},{9,8},{10,11... | collective-permute-start | bytes 1572872 | tf_op jit(solution)/shard_map/ppermute | solution.py:19
  21.6 0.0 copy-done.5
  21.6 0.7 and_reduce_fusion
  23.6 0.0 collective-permute-done.1.first_state_ref
  23.6 0.0 copy-start.2
  23.6 1.2 %add_convert_fusion = bf16[8,128,128]{2,1,0:T(8,128)(2,1)S(1)} fusion(bf16[16,128,128]{2,1,0:T(8,128)(2,1)S(1)} %collective-permute-done.1.first_state_ref, f32[]{:T(128)S(6)} %select_n.20, f32[]{:T(128)S(6)} %select_n.19, bf16[16,128,128]{2,1,0:T(8,128)(2,1)} %get-tuple-element.36), kind=kLoop, calls=%fused_computation.1 | loop fusion | flops 786432 | bytes 786440 | tf_op jit(solution)/shard_map/convert_element_type | solution.py:358
  24.9 2.3 %collective-permute-start.2 = (bf16[4,128,128]{2,1,0:T(8,128)(2,1)S(1)}, bf16[4,128,128]{2,1,0:T(8,128)(2,1)S(1)}, u32[]{:S(2)}, u32[]{:S(2)}) collective-permute-start(bf16[4,128,128]{2,1,0:T(8,128)(2,1)S(1)} %get-tuple-element.37), channel_id=1, source_target_pairs={{0,2},{1,3},{2,0},{3,1},{4,6},{5,7},{6,4},{7,5},{8,10},{9,11},{10,... | collective-permute-start | bytes 393224 | tf_op jit(solution)/shard_map/ppermute | solution.py:19
  27.2 0.0 copy-done.4
  27.2 0.9 %copy.14.level_ref = bf16[16,14,512]{2,1,0:T(8,128)(2,1)} copy(bf16[16,14,512]{2,0,1:T(8,128)(2,1)S(1)} %copy-done.4) | data formatting | bytes 458752 | tf_op args[4]
  29.1 6.1 %near.4 = (bf16[512,2048]{1,0:T(8,128)(2,1)}, f32[2048,512]{1,0:T(8,128)}) custom-call(s32[8]{0:T(128)} %docs_ref.7, bf16[512,2048]{1,0:T(8,128)(2,1)} %query_ref.9, bf16[3,6144]{1,0:T(4,128)(2,1)} %copy-done.1, f32[4,6144]{1,0:T(4,128)} %query_taps_ref.7, bf16[16,14,512]{2,1,0:T(8,128)(2,1)} %copy.14.level_ref, ...), custom_call_target="tpu_custom_call" | custom-call | flops 500000000 | bytes 3500000 | tf_op jit(solution)/shard_map/near/pallas_call | solution.py:370
  35.2 0.0 collective-permute-done.2
  35.2 0.1 add_convert_fusion.2
  35.3 1.6 %collective-permute-start.3 = (bf16[4,128,128]{2,1,0:T(8,128)(2,1)S(1)}, bf16[4,128,128]{2,1,0:T(8,128)(2,1)S(1)}, u32[]{:S(2)}, u32[]{:S(2)}) collective-permute-start(bf16[4,128,128]{2,1,0:T(8,128)(2,1)S(1)} %add_convert_fusion.2), channel_id=1, source_target_pairs={{0,4},{1,5},{2,6},{3,7},{4,0},{5,1},{6,2},{7,3},{8,12},{9,13},{10,... | collective-permute-start | bytes 393224 | tf_op jit(solution)/shard_map/ppermute | solution.py:19
  38.2 6.1 %near.5 = (bf16[512,2048]{1,0:T(8,128)(2,1)}, f32[2048,512]{1,0:T(8,128)}) custom-call(s32[8]{0:T(128)} %docs_ref.7, bf16[512,2048]{1,0:T(8,128)(2,1)} %query_ref.9, bf16[3,6144]{1,0:T(4,128)(2,1)} %copy-done.1, f32[4,6144]{1,0:T(4,128)} %query_taps_ref.7, bf16[16,14,512]{2,1,0:T(8,128)(2,1)} %copy.14.level_ref, ...), custom_call_target="tpu_custom_call", output_to_operand_aliasing={{0}: (7, {}), {1}: (8, {})} | custom-call | flops 500000000 | bytes 3500000 | tf_op jit(solution)/shard_map/near/pallas_call | solution.py:370
  44.3 0.0 collective-permute-done.3
  44.3 0.1 add_convert_fusion.1
  44.3 4.5 %collective-permute-start.4 = (bf16[4,128,128]{2,1,0:T(8,128)(2,1)S(1)}, bf16[4,128,128]{2,1,0:T(8,128)(2,1)S(1)}, u32[]{:S(2)}, u32[]{:S(2)}) collective-permute-start(bf16[4,128,128]{2,1,0:T(8,128)(2,1)S(1)} %add_convert_fusion.1), channel_id=1, source_target_pairs={{0,8},{1,9},{2,10},{3,11},{4,12},{5,13},{6,14},{7,15},{16,24},{17,... | collective-permute-start | bytes 393224 | tf_op jit(solution)/shard_map/ppermute | solution.py:19
  48.8 6.1 %near.6 = (bf16[512,2048]{1,0:T(8,128)(2,1)}, f32[2048,512]{1,0:T(8,128)}) custom-call(s32[8]{0:T(128)} %docs_ref.7, bf16[512,2048]{1,0:T(8,128)(2,1)} %query_ref.9, bf16[3,6144]{1,0:T(4,128)(2,1)} %copy-done.1, f32[4,6144]{1,0:T(4,128)} %query_taps_ref.7, bf16[16,14,512]{2,1,0:T(8,128)(2,1)} %copy.14.level_ref, ...), custom_call_target="tpu_custom_call", output_to_operand_aliasing={{0}: (7, {}), {1}: (8, {})} | custom-call | flops 500000000 | bytes 3500000 | tf_op jit(solution)/shard_map/near/pallas_call | solution.py:370
  54.9 0.0 collective-permute-done.4
  55.0 1.5 %collective-permute-start.5 = (bf16[3,4,128,128]{3,2,1,0:T(8,128)(2,1)S(1)}, bf16[3,4,128,128]{3,2,1,0:T(8,128)(2,1)S(1)}, u32[]{:S(2)}, u32[]{:S(2)}) collective-permute-start(bf16[3,4,128,128]{3,2,1,0:T(8,128)(2,1)S(1)} %pad_maximum_fusion.1), channel_id=1, source_target_pairs={{0,2},{1,3},{2,0},{3,1},{4,6},{5,7},{6,4},{7,5},{8,10},{9,11},{10,... | collective-permute-start | bytes 1179656 | tf_op jit(solution)/shard_map/ppermute | solution.py:19
  56.5 6.0 %near.7 = (bf16[512,2048]{1,0:T(8,128)(2,1)}, f32[2048,512]{1,0:T(8,128)}) custom-call(s32[8]{0:T(128)} %docs_ref.7, bf16[512,2048]{1,0:T(8,128)(2,1)} %query_ref.9, bf16[3,6144]{1,0:T(4,128)(2,1)} %copy-done.1, f32[4,6144]{1,0:T(4,128)} %query_taps_ref.7, bf16[16,14,512]{2,1,0:T(8,128)(2,1)} %copy.14.level_ref, ...), custom_call_target="tpu_custom_call", output_to_operand_aliasing={{0}: (7, {}), {1}: (8, {})} | custom-call | flops 500000000 | bytes 3500000 | tf_op jit(solution)/shard_map/near/pallas_call | solution.py:370
  62.5 3.2 %collective-permute-done.5 = bf16[3,4,128,128]{3,2,1,0:T(8,128)(2,1)S(1)} collective-permute-done((bf16[3,4,128,128]{3,2,1,0:T(8,128)(2,1)S(1)}, bf16[3,4,128,128]{3,2,1,0:T(8,128)(2,1)S(1)}, u32[]{:S(2)}, u32[]{:S(2)}) %collective-permute-start.5) | collective-permute-done | bytes 393248 | tf_op jit(solution)/shard_map/ppermute | solution.py:19
  65.7 0.1 pad_maximum_fusion.own_state_ref
  65.8 0.1 collective-permute-start.6
  65.8 2.3 %collective-permute-done.6.other_state_ref = bf16[3,8,128,128]{3,2,1,0:T(8,128)(2,1)S(1)} collective-permute-done((bf16[3,8,128,128]{3,2,1,0:T(8,128)(2,1)S(1)}, bf16[3,8,128,128]{3,2,1,0:T(8,128)(2,1)S(1)}, u32[]{:S(2)}, u32[]{:S(2)}) %collective-permute-start.6) | collective-permute-done | bytes 786464 | tf_op jit(solution)/shard_map/ppermute | solution.py:19
  68.1 0.9 %copy-done.3 = bf16[3,8,128,128]{3,2,1,0:T(8,128)(2,1)} copy-done((bf16[3,8,128,128]{3,2,1,0:T(8,128)(2,1)}, bf16[3,8,128,128]{3,2,1,0:T(8,128)(2,1)S(1)}, u32[]{:S(2)}) %copy-start.3) | copy-done | bytes 786456
  69.0 14.4 %far.1 = bf16[512,2048]{1,0:T(8,128)(2,1)} custom-call(s32[8]{0:T(128)} %docs_ref.7, bf16[512,2048]{1,0:T(8,128)(2,1)} %get-tuple-element.64.query_ref, f32[2048,512]{1,0:T(8,128)} %get-tuple-element.65.near_ref, bf16[16,14,512]{2,1,0:T(8,128)(2,1)} %copy.14.level_ref, bf16[16,128,128]{2,1,0:T(8,128)(2,1)} %copy-done.2, bf16[3,8,128,128]{3,2,1,0:T(8,128)(2,1)} %copy-done, ...), custom_call_target="tpu_custom_call" | custom-call | flops 1000000000 | bytes 10000000 | tf_op jit(solution)/shard_map/far/pallas_call | solution.py:443
  (9 shorter events, 0.1 us)
Async XLA Ops:
  1.5 20.1 %copy-start.5 = (s32[8]{0:T(128)S(1)}, s32[8]{0:T(128)}, u32[]{:S(2)}) copy-start(s32[8]{0:T(128)} %docs_ref.7) | copy-start | bytes 100
  1.5 25.6 %copy-start.4 = (bf16[16,14,512]{2,0,1:T(8,128)(2,1)S(1)}, bf16[16,14,512]{2,0,1:T(8,128)(2,1)}, u32[]{:S(2)}) copy-start(bf16[16,14,512]{2,0,1:T(8,128)(2,1)} %param.11) | copy-start | bytes 688132
  1.6 3.6 %collective-permute-start = (bf16[3,6144]{1,0:T(4,128)(2,1)}, bf16[3,6144]{1,0:T(4,128)(2,1)S(1)}, u32[]{:S(2)}, u32[]{:S(2)}) collective-permute-start(bf16[3,6144]{1,0:T(4,128)(2,1)} %rim.1), channel_id=1, source_target_pairs={{0,1},{1,2},{2,3},{3,4},{4,5},{5,6},{6,7},{7,8},{8,9},{9,10},{10,1... | collective-permute-start | bytes 110600 | tf_op jit(solution)/shard_map/ppermute | solution.py:19
  5.1 0.6 copy-start.1
  18.5 5.1 %collective-permute-start.1 = (bf16[16,128,128]{2,1,0:T(8,128)(2,1)}, bf16[16,128,128]{2,1,0:T(8,128)(2,1)S(1)}, u32[]{:S(2)}, u32[]{:S(2)}) collective-permute-start(bf16[16,128,128]{2,1,0:T(8,128)(2,1)} %get-tuple-element.36), channel_id=1, source_target_pairs={{0,1},{1,0},{2,3},{3,2},{4,5},{5,4},{6,7},{7,6},{8,9},{9,8},{10,11... | collective-permute-start | bytes 1572872 | tf_op jit(solution)/shard_map/ppermute | solution.py:19
  23.6 11.6 %copy-start.2 = (bf16[16,128,128]{2,1,0:T(8,128)(2,1)}, bf16[16,128,128]{2,1,0:T(8,128)(2,1)S(1)}, u32[]{:S(2)}) copy-start(bf16[16,128,128]{2,1,0:T(8,128)(2,1)S(1)} %collective-permute-done.1.first_state_ref) | copy-start | bytes 1572868
  24.9 10.3 %collective-permute-start.2 = (bf16[4,128,128]{2,1,0:T(8,128)(2,1)S(1)}, bf16[4,128,128]{2,1,0:T(8,128)(2,1)S(1)}, u32[]{:S(2)}, u32[]{:S(2)}) collective-permute-start(bf16[4,128,128]{2,1,0:T(8,128)(2,1)S(1)} %get-tuple-element.37), channel_id=1, source_target_pairs={{0,2},{1,3},{2,0},{3,1},{4,6},{5,7},{6,4},{7,5},{8,10},{9,11},{10,... | collective-permute-start | bytes 393224 | tf_op jit(solution)/shard_map/ppermute | solution.py:19
  35.3 9.0 %collective-permute-start.3 = (bf16[4,128,128]{2,1,0:T(8,128)(2,1)S(1)}, bf16[4,128,128]{2,1,0:T(8,128)(2,1)S(1)}, u32[]{:S(2)}, u32[]{:S(2)}) collective-permute-start(bf16[4,128,128]{2,1,0:T(8,128)(2,1)S(1)} %add_convert_fusion.2), channel_id=1, source_target_pairs={{0,4},{1,5},{2,6},{3,7},{4,0},{5,1},{6,2},{7,3},{8,12},{9,13},{10,... | collective-permute-start | bytes 393224 | tf_op jit(solution)/shard_map/ppermute | solution.py:19
  44.3 10.6 %collective-permute-start.4 = (bf16[4,128,128]{2,1,0:T(8,128)(2,1)S(1)}, bf16[4,128,128]{2,1,0:T(8,128)(2,1)S(1)}, u32[]{:S(2)}, u32[]{:S(2)}) collective-permute-start(bf16[4,128,128]{2,1,0:T(8,128)(2,1)S(1)} %add_convert_fusion.1), channel_id=1, source_target_pairs={{0,8},{1,9},{2,10},{3,11},{4,12},{5,13},{6,14},{7,15},{16,24},{17,... | collective-permute-start | bytes 393224 | tf_op jit(solution)/shard_map/ppermute | solution.py:19
  55.0 10.7 %collective-permute-start.5 = (bf16[3,4,128,128]{3,2,1,0:T(8,128)(2,1)S(1)}, bf16[3,4,128,128]{3,2,1,0:T(8,128)(2,1)S(1)}, u32[]{:S(2)}, u32[]{:S(2)}) collective-permute-start(bf16[3,4,128,128]{3,2,1,0:T(8,128)(2,1)S(1)} %pad_maximum_fusion.1), channel_id=1, source_target_pairs={{0,2},{1,3},{2,0},{3,1},{4,6},{5,7},{6,4},{7,5},{8,10},{9,11},{10,... | collective-permute-start | bytes 1179656 | tf_op jit(solution)/shard_map/ppermute | solution.py:19
  65.8 2.4 %copy-start = (bf16[3,8,128,128]{3,2,1,0:T(8,128)(2,1)}, bf16[3,8,128,128]{3,2,1,0:T(8,128)(2,1)S(1)}, u32[]{:S(2)}) copy-start(bf16[3,8,128,128]{3,2,1,0:T(8,128)(2,1)S(1)} %pad_maximum_fusion.own_state_ref) | copy-start | bytes 2359300
  65.8 2.4 %collective-permute-start.6 = (bf16[3,8,128,128]{3,2,1,0:T(8,128)(2,1)S(1)}, bf16[3,8,128,128]{3,2,1,0:T(8,128)(2,1)S(1)}, u32[]{:S(2)}, u32[]{:S(2)}) collective-permute-start(bf16[3,8,128,128]{3,2,1,0:T(8,128)(2,1)S(1)} %pad_maximum_fusion.own_state_ref), channel_id=1, source_target_pairs={{0,1},{1,0},{2,3},{3,2},{4,5},{5,4},{6,7},{7,6},{8,9},{9,8},{10,11... | collective-permute-start | bytes 2359304 | tf_op jit(solution)/shard_map/ppermute | solution.py:19
  68.1 0.9 %copy-start.3 = (bf16[3,8,128,128]{3,2,1,0:T(8,128)(2,1)}, bf16[3,8,128,128]{3,2,1,0:T(8,128)(2,1)S(1)}, u32[]{:S(2)}) copy-start(bf16[3,8,128,128]{3,2,1,0:T(8,128)(2,1)S(1)} %collective-permute-done.6.other_state_ref) | copy-start | bytes 2359300

commit v3 on v0

v3 whole, which is shorter than its diff:
```python
import functools

import jax
import jax.numpy as jnp
from jax import lax
from jax.experimental import pallas as pl
from jax.experimental.pallas import tpu as pltpu
from jax.sharding import PartitionSpec as P

LANES = 128
PAD = 8
NT = (((1,), (1,)), ((), ()))


def exchange(block, partner):
    count = lax.axis_size("seq")
    route = [(i, partner(i)) for i in range(count) if partner(i) is not None]
    return lax.ppermute(block, "seq", route)


def swapped(block, bit):
    return exchange(block, lambda i: i ^ (1 << bit))


def sent_up(block, bit):
    return exchange(block, lambda i: None if i >> bit & 1 else i | 1 << bit)


def limited(mebibytes):
    return pltpu.CompilerParams(vmem_limit_bytes=mebibytes * 1024 * 1024)


def start_at(docs_ref, doc_count, positions):
    def step(i, start):
        doc = docs_ref[i]
        return jnp.where(positions >= doc, doc, start)

    return lax.fori_loop(0, doc_count, step, jnp.zeros_like(positions))


def silu(values):
    return values * (0.5 + 0.5 * jnp.tanh(0.5 * values))


def logical_place(head, core_bit, y_bit):
    return ((head >> 3) ^ core_bit) * 8 + (((head >> 2) & 1) ^ y_bit) * 4 + (head & 3)


def row_at(place):
    return ((place & 7) << 4) | ((place >> 3) & 15)


def selection(row_of, place_of):
    shape = (LANES, LANES)
    rows = lax.broadcasted_iota(jnp.int32, shape, row_of)
    places = lax.broadcasted_iota(jnp.int32, shape, place_of)
    return jnp.where(rows == row_at(places), 1.0, 0.0).astype(jnp.bfloat16)


def rim_kernel(query_ref, key_ref, value_ref, out_ref, buffer, sems):
    rim_rows = out_ref.shape[0]
    edge, width = buffer.shape[1:]
    copies = []
    for part, ref in enumerate((query_ref, key_ref, value_ref)):
        rows = ref.shape[0]
        copy = pltpu.make_async_copy(
            ref.at[rows - edge : rows, :], buffer.at[part], sems.at[part]
        )
        copy.start()
        copies.append(copy)
    for part, copy in enumerate(copies):
        copy.wait()
        out_ref[:, part * width : (part + 1) * width] = buffer[part, edge - rim_rows : edge, :]


def tables_kernel(
    docs_ref,
    level_ref,
    gain_ref,
    table_ref,
    start_ref,
    distance_ref,
    gain_out_ref,
    flag_ref,
    *,
    doc_count,
):
    level_count, head_count, row_count = level_ref.shape
    tiles = row_count // LANES
    tok_bits = row_count.bit_length() - 1
    index = lax.axis_index("seq")
    first_pos = index * row_count
    lanes = lax.broadcasted_iota(jnp.int32, (8, row_count), 1)
    positions = first_pos + (lanes & -LANES) + row_at(lanes & (LANES - 1))
    starts = start_at(docs_ref, doc_count, positions)
    start_ref[...] = starts - first_pos
    select = selection(0, 1)
    starts = jnp.concatenate([starts] * (head_count // 8), axis=0)
    for level in range(level_count):
        scale = 2.0 ** (-level / 2)
        for tile in range(tiles):
            cols = slice(tile * LANES, (tile + 1) * LANES)
            weights = jnp.dot(level_ref[level, :, cols], select, preferred_element_type=jnp.float32)
            weights = weights * scale
            if level > tok_bits:
                bit = level - tok_bits - 1
                limit = jnp.where((index >> bit) & 1 == 1, (index >> bit << bit) * row_count, 0)
                weights = jnp.where(starts[:, cols] < limit, weights, 0.0)
            table_ref[level, :, cols] = weights
    places = lax.broadcasted_iota(jnp.int32, (row_count, LANES), 0)
    positions = first_pos + (places & -LANES) + row_at(places & (LANES - 1))
    distance_ref[...] = positions - start_at(docs_ref, doc_count, positions)

    def gain_step(head, carry):
        gain_out_ref[head] = jnp.broadcast_to(gain_ref[head], (LANES, LANES)).T
        return carry

    lax.fori_loop(0, head_count, gain_step, 0)

    for tile in range(tiles):
        tile_first = first_pos + tile * LANES

        def step(i, flag):
            gap = docs_ref[i] - tile_first
            return jnp.where((gap > -8) & (gap < LANES), 1, flag)

        flag_ref[tile] = lax.fori_loop(0, doc_count, step, jnp.int32(0))


def fill_window(window_ref, rim, rows):
    rim_rows = rim.shape[0]
    window_ref[0:PAD, :] = jnp.concatenate(
        [jnp.zeros((PAD - rim_rows, rim.shape[1]), jnp.float32), rim.astype(jnp.float32)], axis=0
    )
    window_ref[PAD:, :] = rows.astype(jnp.float32)


def convolved(window_ref, taps, tile, distance):
    reach = taps.shape[0] - 1
    rows = [
        window_ref[pl.ds(PAD + tile * LANES + i, 8, stride=16), :] for i in range(-reach, 16)
    ]
    summed = taps[0:1, :] * jnp.concatenate(rows[reach:], axis=0)
    for offset in range(1, reach + 1):
        term = taps[offset : offset + 1, :] * jnp.concatenate(
            rows[reach - offset : reach - offset + 16], axis=0
        )
        if distance is not None:
            term = jnp.where(distance >= offset, term, 0.0)
        summed = summed + term
    return summed


def per_tile(flag_ref, tiles, body):
    for tile in range(tiles):
        flagged = flag_ref[tile] == 1

        @pl.when(flagged)
        def _():
            body(tile, True)

        @pl.when(jnp.logical_not(flagged))
        def _():
            body(tile, False)


def columns(first):
    return pl.ds(pl.multiple_of(first, LANES), LANES)


def key_value_kernel(
    docs_ref,
    flag_ref,
    key_ref,
    value_ref,
    rim_ref,
    taps_ref,
    distance_ref,
    key_out_ref,
    value_out_ref,
    state_ref,
    window_ref,
    *,
    doc_count,
    heads,
):
    row_count, width = key_ref.shape
    head_count = width // LANES
    steps = head_count // heads
    tiles = row_count // LANES
    index = lax.axis_index("seq")
    first_pos = index * row_count

    last_pos = jnp.full((1, row_count), first_pos + row_count - 1, jnp.int32)
    last_start = start_at(docs_ref, doc_count, last_pos)
    lanes = lax.broadcasted_iota(jnp.int32, (1, row_count), 1)
    lanes_pos = first_pos + (lanes & -LANES) + row_at(lanes & (LANES - 1))
    keep = jnp.where(lanes_pos >= last_start, 1.0, 0.0).astype(jnp.bfloat16)

    def pair(step, carry):
        for which in range(heads):
            first = (step * heads + which) * LANES
            fill_window(
                window_ref.at[2 * which],
                rim_ref[:, columns(width + first)],
                key_ref[:, columns(first)],
            )
            fill_window(
                window_ref.at[2 * which + 1],
                rim_ref[:, columns(2 * width + first)],
                value_ref[:, columns(first)],
            )

        def body(tile, masked):
            places = slice(tile * LANES, (tile + 1) * LANES)
            distance = distance_ref[places, :] if masked else None
            for which in range(heads):
                head = step * heads + which
                first = head * LANES
                key_taps = taps_ref[:, columns(width + first)]
                value_taps = taps_ref[:, columns(2 * width + first)]
                grown = silu(convolved(window_ref.at[2 * which], key_taps, tile, distance))
                square = jnp.sum(grown * grown, axis=1, keepdims=True)
                keys = (grown * lax.rsqrt(square + 1e-6)).astype(jnp.bfloat16)
                key_out_ref[head, places, :] = keys
                values = silu(convolved(window_ref.at[2 * which + 1], value_taps, tile, distance))
                value_out_ref[head, :, places] = values.T.astype(jnp.bfloat16)

        per_tile(flag_ref, tiles, body)
        for which in range(heads):
            head = step * heads + which
            place = logical_place(head, index & 1, (index >> 1) & 1)
            state_ref[place] = jnp.dot(
                value_out_ref[head] * keep, key_out_ref[head], preferred_element_type=jnp.float32
            ).astype(jnp.bfloat16)
        return carry

    lax.fori_loop(0, steps, pair, 0)


def join_kernel(docs_ref, mine_ref, theirs_ref, *out_refs, doc_count, row_count, bit, parts):
    index = lax.axis_index("seq")
    stride = 1 << bit
    upper_first = (((index >> (bit + 1)) << (bit + 1)) + stride) * row_count

    def step(i, found):
        gap = docs_ref[i] - upper_first
        return jnp.where((gap >= 0) & (gap < stride * row_count), 1, found)

    upper_has = lax.fori_loop(0, doc_count, step, jnp.int32(0))
    is_upper = (index >> bit) & 1
    keep_mine = jnp.where((upper_has == 1) & (is_upper == 0), 0.0, 1.0)
    keep_theirs = jnp.where((upper_has == 1) & (is_upper == 1), 0.0, 1.0)
    skip = theirs_ref.shape[0] // 2 if parts == 2 else 0
    count = out_refs[0].shape[0]
    for part, out_ref in enumerate(out_refs):
        mine = mine_ref[part * count : (part + 1) * count].astype(jnp.float32)
        theirs = theirs_ref[skip + part * count : skip + (part + 1) * count].astype(jnp.float32)
        out_ref[...] = (mine * keep_mine + theirs * keep_theirs).astype(jnp.bfloat16)


def near_kernel(
    flag_ref,
    query_ref,
    rim_ref,
    taps_ref,
    distance_ref,
    table_ref,
    start_ref,
    key_ref,
    value_ref,
    *rest,
    first_head,
    head_count,
    heads,
    skipped,
):
    query_out_ref, near_ref, window_ref, fine_ref, pair_ref = rest[skipped:]
    row_count = query_ref.shape[0]
    tiles = row_count // LANES
    span = 2 * LANES
    sub = lax.broadcasted_iota(jnp.int32, (8, row_count), 0)
    lane = lax.broadcasted_iota(jnp.int32, (8, row_count), 1)
    high = sub ^ (lane & 7)
    sub16 = lax.broadcasted_iota(jnp.int32, (16, row_count), 0)
    low_row = (lax.broadcasted_iota(jnp.int32, (16, row_count), 1) >> 3) & 15
    low = sub16 ^ low_row
    same_group = lax.broadcasted_iota(jnp.int32, (8, LANES), 0) == (
        lax.broadcasted_iota(jnp.int32, (8, LANES), 1) & 7
    )
    key_row = row_at(lax.broadcasted_iota(jnp.int32, (LANES, LANES), 0))

    def group(step, carry):
        for which in range(heads):
            head = first_head + step * heads + which
            fill_window(
                window_ref.at[which],
                rim_ref[:, columns(head * LANES)],
                query_ref[:, columns(head * LANES)],
            )

        def body(tile, masked):
            places = slice(tile * LANES, (tile + 1) * LANES)
            distance = distance_ref[places, :] if masked else None
            for which in range(heads):
                head = first_head + step * heads + which
                taps = taps_ref[:, columns(head * LANES)]
                grown = silu(convolved(window_ref.at[which], taps, tile, distance))
                query_out_ref[head, places, :] = grown.astype(jnp.bfloat16)

        per_tile(flag_ref, tiles, body)

        for which in range(heads):
            head = first_head + step * heads + which
            tok_bits = row_count.bit_length() - 1
            scaled = [table_ref[level, pl.ds(head, 1), :] for level in range(tok_bits + 1)]
            coarse = jnp.where(high < 2, scaled[5], jnp.where(high < 4, scaled[6], scaled[7]))
            coarse = jnp.where(sub > (lane & 7), 0.0, coarse)
            fine = jnp.where(
                low == 0,
                scaled[0],
                jnp.where(
                    low == 1,
                    scaled[1],
                    jnp.where(low < 4, scaled[2], jnp.where(low < 8, scaled[3], scaled[4])),
                ),
            )
            fine = jnp.where(sub16 > low_row, 0.0, fine)
            for tile in range(tiles):
                fine_ref[which, tile] = fine[:, tile * LANES : (tile + 1) * LANES]
            for part in range(row_count // span):
                rows = (part + 1) * span
                scores = lax.dot_general(
                    key_ref[head, 0:rows, :],
                    query_out_ref[head, part * span : rows, :],
                    NT,
                    preferred_element_type=jnp.float32,
                )
                for side in range(2):
                    tile = 2 * part + side
                    cols = slice(tile * LANES, (tile + 1) * LANES)
                    starts = start_ref[0:1, cols]
                    for other in range(tile + 1):
                        if other == tile:
                            weight = jnp.concatenate(
                                [
                                    jnp.where(
                                        same_group,
                                        fine_ref[which, tile, pl.ds(a, 8, stride=0), :],
                                        coarse[:, cols],
                                    )
                                    for a in range(16)
                                ],
                                axis=0,
                            )
                        else:
                            weight = scaled[7 + (tile ^ other).bit_length()][:, cols]
                        piece = scores[
                            other * LANES : (other + 1) * LANES,
                            side * LANES : (side + 1) * LANES,
                        ]
                        valid = key_row >= starts - other * LANES
                        pair_ref[which, other * LANES : (other + 1) * LANES, cols] = jnp.where(
                            valid, piece * weight, 0.0
                        ).astype(jnp.bfloat16)
                    if side == 0:
                        pair_ref[which, (tile + 1) * LANES : rows, cols] = jnp.zeros(
                            (LANES, LANES), jnp.bfloat16
                        )
                near_ref[head, :, part * span : rows] = jnp.dot(
                    value_ref[head, :, 0:rows],
                    pair_ref[which, 0:rows, part * span : rows],
                    preferred_element_type=jnp.float32,
                )
        return carry

    lax.fori_loop(0, head_count // heads, group, 0)


def far_kernel(
    query_ref,
    near_ref,
    table_ref,
    first_state_ref,
    own_state_ref,
    other_state_ref,
    gain_ref,
    out_hbm_ref,
    out_buffer,
    sems,
    *,
    dev_bits,
    heads,
):
    head_count, row_count, _ = query_ref.shape
    tiles = row_count // LANES
    steps = head_count // heads
    wide = heads * LANES
    index = lax.axis_index("seq")
    core_bit = index & 1
    y_bit = (index >> 1) & 1
    tok_bits = row_count.bit_length() - 1
    select = selection(0, 1)

    def copy(step):
        cols = pl.ds(pl.multiple_of(step * wide, wide), wide)
        return pltpu.make_async_copy(
            out_buffer.at[:, cols], out_hbm_ref.at[:, cols], sems.at[step]
        )

    def group(step, carry):
        for which in range(heads):
            head = step * heads + which
            first_place = logical_place(head, 1 - core_bit, y_bit)
            place = logical_place(head, core_bit, y_bit)
            is_own = place < 8
            states = [first_state_ref[first_place]]
            for level in range(dev_bits - 1):
                states.append(
                    jnp.where(
                        is_own, own_state_ref[level, place & 7], other_state_ref[level, place & 7]
                    )
                )
            images = lax.dot_general(
                jnp.concatenate(states, axis=0),
                query_ref[head],
                NT,
                preferred_element_type=jnp.float32,
            )
            summed = near_ref[head]
            for bit in range(dev_bits):
                coef = table_ref[tok_bits + 1 + bit, pl.ds(head, 1), :]
                summed = summed + coef * images[bit * LANES : (bit + 1) * LANES, :]
            mean = jnp.mean(summed * summed, axis=0, keepdims=True)
            normed = summed * lax.rsqrt(mean + 1e-6)
            gain = gain_ref[head]
            for tile in range(tiles):
                cols = slice(tile * LANES, (tile + 1) * LANES)
                done = (normed[:, cols] * gain).astype(jnp.bfloat16)
                turned = lax.dot_general(select, done, NT, preferred_element_type=jnp.float32)
                out_buffer[cols, columns(head * LANES)] = turned.astype(jnp.bfloat16)
        copy(step).start()
        return carry

    lax.fori_loop(0, steps, group, 0)
    for step in range(steps):
        copy(step).wait()


def local(query_in, key_in, value_in, conv_weight, level_weight, out_gain, doc_starts):
    row_count, width_all = query_in.shape
    head_count, level_count, _ = level_weight.shape
    head_size = width_all // head_count
    conv_width = conv_weight.shape[0]
    doc_count = doc_starts.shape[0]
    dev_index = lax.axis_index("seq")
    dev_count = lax.axis_size("seq")
    dev_bits = dev_count.bit_length() - 1
    rim_rows = conv_width - 1
    tiles = row_count // LANES
    smem = pl.BlockSpec(memory_space=pltpu.SMEM)
    vmem = pl.BlockSpec(memory_space=pltpu.VMEM)
    anywhere = pl.BlockSpec(memory_space=pl.ANY)

    tails = pl.pallas_call(
        rim_kernel,
        in_specs=[pl.BlockSpec(memory_space=pltpu.HBM)] * 3,
        out_specs=vmem,
        out_shape=pltpu.VMEM((rim_rows, 3 * width_all), query_in.dtype),
        scratch_shapes=[
            pltpu.VMEM((3, 16, width_all), query_in.dtype),
            pltpu.SemaphoreType.DMA((3,)),
        ],
        compiler_params=limited(1),
        name="rim",
    )(*(pltpu.with_memory_space_constraint(x, pltpu.HBM) for x in (query_in, key_in, value_in)))
    tails, docs = lax.optimization_barrier((tails, doc_starts))
    rims = exchange(tails, lambda i: i + 1 if i + 1 < dev_count else None)
    table, starts, distance, gains, flags = pl.pallas_call(
        functools.partial(tables_kernel, doc_count=doc_count),
        in_specs=[smem, vmem, vmem],
        out_specs=[vmem, vmem, vmem, vmem, smem],
        out_shape=[
            pltpu.VMEM((level_count, head_count, row_count), jnp.float32),
            pltpu.VMEM((8, row_count), jnp.int32),
            pltpu.VMEM((row_count, LANES), jnp.int32),
            pltpu.VMEM((head_count, head_size, LANES), jnp.float32),
            pltpu.SMEM((tiles,), jnp.int32),
        ],
        compiler_params=limited(4),
        name="tables",
    )(docs, jnp.transpose(level_weight, (1, 0, 2)), out_gain.reshape(head_count, 1, head_size))
    rims, table, starts, distance, gains, flags = lax.optimization_barrier(
        (rims, table, starts, distance, gains, flags)
    )

    heads = 2
    steps = head_count // heads
    keys, values_t, state = pl.pallas_call(
        functools.partial(key_value_kernel, doc_count=doc_count, heads=heads),
        in_specs=[smem, smem] + [vmem] * 5,
        out_specs=[vmem] * 3,
        out_shape=[
            pltpu.VMEM((head_count, row_count, head_size), jnp.bfloat16),
            pltpu.VMEM((head_count, head_size, row_count), jnp.bfloat16),
            pltpu.VMEM((head_count, head_size, head_size), jnp.bfloat16),
        ],
        scratch_shapes=[
            pltpu.VMEM((2 * heads, row_count + PAD, LANES), jnp.float32),
        ],
        compiler_params=limited(4),
        name="key_value",
    )(docs, flags, key_in, value_in, rims, conv_weight, distance)

    def joined(mine, theirs, bit, parts=1):
        count = mine.shape[0] // (2 if parts == 2 else 1)
        shape = (count // parts, head_size, head_size)
        return pl.pallas_call(
            functools.partial(
                join_kernel, doc_count=doc_count, row_count=row_count, bit=bit, parts=parts
            ),
            in_specs=[smem, vmem, vmem],
            out_specs=[vmem] * parts,
            out_shape=[pltpu.VMEM(shape, jnp.bfloat16)] * parts,
            compiler_params=limited(1),
            name="join",
        )(doc_starts, mine, theirs)

    buffers = None
    piece_heads = head_count // 4

    def near_piece(piece, buffers, flags):
        extra = [] if buffers is None else list(buffers)
        return pl.pallas_call(
            functools.partial(
                near_kernel,
                first_head=piece * piece_heads,
                head_count=piece_heads,
                heads=heads,
                skipped=len(extra),
            ),
            in_specs=[smem] + [vmem] * (8 + len(extra)),
            out_specs=[vmem] * 2,
            out_shape=[
                pltpu.VMEM((head_count, row_count, head_size), jnp.bfloat16),
                pltpu.VMEM((head_count, head_size, row_count), jnp.float32),
            ],
            scratch_shapes=[
                pltpu.VMEM((heads, row_count + PAD, LANES), jnp.float32),
                pltpu.VMEM((heads, tiles, 16, LANES), jnp.float32),
                pltpu.VMEM((heads, row_count, row_count), jnp.bfloat16),
            ],
            input_output_aliases={9: 0, 10: 1} if extra else {},
            compiler_params=limited(6),
            cost_estimate=pl.CostEstimate(
                flops=500_000_000, bytes_accessed=3_500_000, transcendentals=300_000
            ),
            name="near",
        )(flags, query_in, rims, conv_weight, distance, table, starts, keys, values_t, *extra)

    def covered(payload, send, piece, buffers):
        payload, tied = lax.optimization_barrier((payload, flags))
        arrived = send(payload)
        buffers = near_piece(piece, buffers, tied)
        arrived, buffers = lax.optimization_barrier((arrived, buffers))
        return arrived, buffers

    first_state = swapped(state, 0)
    pair_kept, pair_sent = joined(state, first_state, 0, parts=2)
    pair_in, buffers = covered(pair_sent, lambda x: swapped(x, 1), 0, buffers)
    (carried,) = joined(pair_kept, pair_in, 1)
    received = []
    for bit in range(2, dev_bits):
        last = bit == dev_bits - 1
        if last:
            arrived, buffers = covered(carried, lambda x: sent_up(x, bit), 2, buffers)
        elif bit == 2:
            arrived, buffers = covered(carried, lambda x: swapped(x, bit), 1, buffers)
        else:
            arrived = swapped(carried, bit)
        received.append(arrived)
        if not last:
            (carried,) = joined(carried, arrived, bit)

    mine = jnp.stack([pair_kept] + received)
    theirs, buffers = covered(mine, lambda x: swapped(x, 1), 3, buffers)
    queries, near = buffers
    own = jnp.concatenate(
        [jnp.concatenate([pair_in[None], mine[1:]], axis=0), theirs], axis=1
    )
    other = swapped(own, 0)

    return pl.pallas_call(
        functools.partial(far_kernel, dev_bits=dev_bits, heads=heads),
        in_specs=[vmem] * 7,
        out_specs=anywhere,
        out_shape=jax.ShapeDtypeStruct((row_count, width_all), jnp.bfloat16),
        scratch_shapes=[
            pltpu.VMEM((row_count, width_all), jnp.bfloat16),
            pltpu.SemaphoreType.DMA((steps,)),
        ],
        compiler_params=limited(8),
        name="far",
    )(queries, near, table, first_state, own, other, gains)


def solution(mesh):
    in_specs = (
        P(("groups", "seq"), None),
        P(("groups", "seq"), None),
        P(("groups", "seq"), None),
        P(),
        P(None, None, ("groups", "seq")),
        P(),
        P("groups"),
    )
    out_specs = P(("groups", "seq"), None)
    return jax.shard_map(local, mesh=mesh, in_specs=in_specs, out_specs=out_specs, check_vma=False)
```

time: 157 us -> 65 us (0.41)
  the two profiles are of different devices: /device:TPU:0 before, /device:TPU:27 now
where the time goes in v3:
time: 65 us; the launch traced here: 64.8 us
  Pallas kernels  38.9 us (60%)
  waiting for transfers between devices  17.1 us (26%)
  starting transfers between devices  8.4 us (13%)
    ppermute x7, waiting for transfers between devices, exchange(): return lax.ppermute(block, 'seq', route)  17.1 us
    pallas_call x4, Pallas kernels, near_piece(): pl.pallas_call(functools.partial(near_kernel, first_head=piece * piece_he...  12.9 us
    pallas_call x1, Pallas kernels, local(): pl.pallas_call(functools.partial(key_value_kernel, doc_count=doc_count, h...  11.2 us
    ppermute x7, starting transfers between devices, exchange(): return lax.ppermute(block, 'seq', route)  8.4 us
    pallas_call x1, Pallas kernels, local(): pl.pallas_call(functools.partial(far_kernel, dev_bits=dev_bits, heads=hea...  8.29 us
    pallas_call x1, Pallas kernels, local(): pl.pallas_call(functools.partial(tables_kernel, doc_count=doc_count), in_...  3.46 us
    pallas_call x3, Pallas kernels, joined(): pl.pallas_call(functools.partial(join_kernel, doc_count=doc_count, row_co...  2.04 us
  transfers between devices with their start and end apart: 7, of which 6 were waited for; matrix products, arithmetic and copies ran while one was open for 0% of the time, Pallas kernels for 25%

profile of v3, /device:TPU:27, one launch (start us, length us, event | category | flops | bytes accessed | tf_op | source)
XLA Modules:
  0.0 64.8 jit_solution(1187433061809497855)
XLA Ops:
  0.0 0.0 copy-start.6
  0.0 0.0 copy-start.4
  0.0 0.0 copy-start.3
  0.0 1.1 %rim.1 = bf16[3,6144]{1,0:T(4,128)(2,1)S(1)} custom-call(bf16[512,2048]{1,0:T(8,128)(2,1)} %query_ref.9, bf16[512,2048]{1,0:T(8,128)(2,1)} %key_ref.3, bf16[512,2048]{1,0:T(8,128)(2,1)} %value_ref.3), custom_call_target="tpu_custom_call" | custom-call | tf_op jit(solution)/shard_map/rim/pallas_call | solution.py:465
  1.1 3.8 %collective-permute-start = (bf16[3,6144]{1,0:T(4,128)(2,1)S(1)}, bf16[3,6144]{1,0:T(4,128)(2,1)S(1)}, u32[]{:S(2)}, u32[]{:S(2)}) collective-permute-start(bf16[3,6144]{1,0:T(4,128)(2,1)S(1)} %rim.1), channel_id=1, source_target_pairs={{0,1},{1,2},{2,3},{3,4},{4,5},{5,6},{6,7},{7,8},{8,9},{9,10},{10,1... | collective-permute-start | bytes 110600 | tf_op jit(solution)/shard_map/ppermute | solution.py:18
  5.0 0.0 copy-done.5
  5.0 3.5 %tables.1 = (f32[14,16,512]{2,1,0:T(8,128)S(1)}, s32[8,512]{1,0:T(8,128)S(1)}, s32[512,128]{1,0:T(8,128)S(1)}, f32[16,128,128]{2,1,0:T(8,128)S(1)}, s32[4]{0:T(128)S(4)}) custom-call(s32[8]{0:T(128)S(1)} %copy-done.5, bf16[14,16,512]{2,1,0:T(8,128)(2,1)S(1)} %bitcast.10, f32[16,1,128]{2,1,0:T(1,128)S(1)} %bitcast.11), custom_call_target="tpu_custom_call" | custom-call | tf_op jit(solution)/shard_map/tables/pallas_call | solution.py:479
  8.5 0.0 collective-permute-done.rim_ref
  8.5 0.0 copy-start
  8.5 11.2 %key_value.1 = (bf16[16,512,128]{2,1,0:T(8,128)(2,1)S(1)}, bf16[16,128,512]{2,1,0:T(8,128)(2,1)S(1)}, bf16[16,128,128]{2,1,0:T(8,128)(2,1)S(1)}) custom-call(s32[8]{0:T(128)S(1)} %copy-done.5, s32[4]{0:T(128)S(4)} %get-tuple-element.88.flag_ref, bf16[512,2048]{1,0:T(8,128)(2,1)S(1)} %copy-done.1, bf16[512,2048]{1,0:T(8,128)(2,1)S(1)} %copy-done.2, ...), custom_call_target="tpu_custom_call" | custom-call | tf_op jit(solution)/shard_map/key_value/pallas_call | solution.py:499
  19.7 0.1 collective-permute-start.1
  19.8 1.9 %collective-permute-done.1.theirs_ref.first_state_ref = bf16[16,128,128]{2,1,0:T(8,128)(2,1)S(1)} collective-permute-done((bf16[16,128,128]{2,1,0:T(8,128)(2,1)S(1)}, bf16[16,128,128]{2,1,0:T(8,128)(2,1)S(1)}, u32[]{:S(2)}, u32[]{:S(2)}) %collective-permute-start.1) | collective-permute-done | bytes 524320 | tf_op jit(solution)/shard_map/ppermute | solution.py:18
  21.7 0.7 %join.3 = (bf16[4,128,128]{2,1,0:T(8,128)(2,1)S(1)}, bf16[4,128,128]{2,1,0:T(8,128)(2,1)S(1)}) custom-call(s32[8]{0:T(128)S(1)} %copy-done.5, bf16[16,128,128]{2,1,0:T(8,128)(2,1)S(1)} %get-tuple-element.61.mine_ref, bf16[16,128,128]{2,1,0:T(8,128)(2,1)S(1)} %collective-permute-done.1.theirs_ref.first_state_ref), custom_call_target="tpu_custom_call" | custom-call | tf_op jit(solution)/shard_map/join/pallas_call | solution.py:518
  22.4 0.1 collective-permute-start.2
  22.5 0.0 copy-done
  22.5 3.2 %near.4 = (bf16[16,512,128]{2,1,0:T(8,128)(2,1)S(1)}, f32[16,128,512]{2,1,0:T(8,128)S(1)}) custom-call(s32[4]{0:T(128)S(4)} %get-tuple-element.88.flag_ref, bf16[512,2048]{1,0:T(8,128)(2,1)S(1)} %copy-done, bf16[3,6144]{1,0:T(4,128)(2,1)S(1)} %collective-permute-done.rim_ref, f32[4,6144]{1,0:T(4,128)S(1)} %copy-done.3, ...), custom_call_target="tpu_custom_call" | custom-call | flops 500000000 | bytes 3500000 | tf_op jit(solution)/shard_map/near/pallas_call | solution.py:534
  25.7 1.7 %collective-permute-done.2.theirs_ref = bf16[4,128,128]{2,1,0:T(8,128)(2,1)S(1)} collective-permute-done((bf16[4,128,128]{2,1,0:T(8,128)(2,1)S(1)}, bf16[4,128,128]{2,1,0:T(8,128)(2,1)S(1)}, u32[]{:S(2)}, u32[]{:S(2)}) %collective-permute-start.2) | collective-permute-done | bytes 131104 | tf_op jit(solution)/shard_map/ppermute | solution.py:18
  27.4 0.7 %join.4.mine_ref = bf16[4,128,128]{2,1,0:T(8,128)(2,1)S(1)} custom-call(s32[8]{0:T(128)S(1)} %copy-done.5, bf16[4,128,128]{2,1,0:T(8,128)(2,1)S(1)} %get-tuple-element.62.mine_ref, bf16[4,128,128]{2,1,0:T(8,128)(2,1)S(1)} %collective-permute-done.2.theirs_ref), custom_call_target="tpu_custom_call" | custom-call | tf_op jit(solution)/shard_map/join/pallas_call | solution.py:518
  28.1 0.1 collective-permute-start.3
  28.2 3.2 %near.5 = (bf16[16,512,128]{2,1,0:T(8,128)(2,1)S(1)}, f32[16,128,512]{2,1,0:T(8,128)S(1)}) custom-call(s32[4]{0:T(128)S(4)} %get-tuple-element.88.flag_ref, bf16[512,2048]{1,0:T(8,128)(2,1)S(1)} %copy-done, bf16[3,6144]{1,0:T(4,128)(2,1)S(1)} %collective-permute-done.rim_ref, ...), custom_call_target="tpu_custom_call", output_to_operand_aliasing={{0}: (9, {}), {1}: (10, {})} | custom-call | flops 500000000 | bytes 3500000 | tf_op jit(solution)/shard_map/near/pallas_call | solution.py:534
  31.4 0.6 collective-permute-done.3.theirs_ref
  32.0 0.7 %join.5 = bf16[4,128,128]{2,1,0:T(8,128)(2,1)S(1)} custom-call(s32[8]{0:T(128)S(1)} %copy-done.5, bf16[4,128,128]{2,1,0:T(8,128)(2,1)S(1)} %join.4.mine_ref, bf16[4,128,128]{2,1,0:T(8,128)(2,1)S(1)} %collective-permute-done.3.theirs_ref), custom_call_target="tpu_custom_call" | custom-call | tf_op jit(solution)/shard_map/join/pallas_call | solution.py:518
  32.7 1.3 %collective-permute-start.4 = (bf16[4,128,128]{2,1,0:T(8,128)(2,1)S(1)}, bf16[4,128,128]{2,1,0:T(8,128)(2,1)S(1)}, u32[]{:S(2)}, u32[]{:S(2)}) collective-permute-start(bf16[4,128,128]{2,1,0:T(8,128)(2,1)S(1)} %join.5), channel_id=1, source_target_pairs={{0,8},{1,9},{2,10},{3,11},{4,12},{5,13},{6,14},{7,15},{16,24},{17,... | collective-permute-start | bytes 393224 | tf_op jit(solution)/shard_map/ppermute | solution.py:18
  34.0 3.2 %near.6 = (bf16[16,512,128]{2,1,0:T(8,128)(2,1)S(1)}, f32[16,128,512]{2,1,0:T(8,128)S(1)}) custom-call(s32[4]{0:T(128)S(4)} %get-tuple-element.88.flag_ref, bf16[512,2048]{1,0:T(8,128)(2,1)S(1)} %copy-done, bf16[3,6144]{1,0:T(4,128)(2,1)S(1)} %collective-permute-done.rim_ref, ...), custom_call_target="tpu_custom_call", output_to_operand_aliasing={{0}: (9, {}), {1}: (10, {})} | custom-call | flops 500000000 | bytes 3500000 | tf_op jit(solution)/shard_map/near/pallas_call | solution.py:534
  37.2 5.7 %collective-permute-done.4 = bf16[4,128,128]{2,1,0:T(8,128)(2,1)S(1)} collective-permute-done((bf16[4,128,128]{2,1,0:T(8,128)(2,1)S(1)}, bf16[4,128,128]{2,1,0:T(8,128)(2,1)S(1)}, u32[]{:S(2)}, u32[]{:S(2)}) %collective-permute-start.4) | collective-permute-done | bytes 131104 | tf_op jit(solution)/shard_map/ppermute | solution.py:18
  42.9 0.7 %collective-permute-start.5 = (bf16[3,4,128,128]{3,2,1,0:T(8,128)(2,1)S(1)}, bf16[3,4,128,128]{3,2,1,0:T(8,128)(2,1)S(1)}, u32[]{:S(2)}, u32[]{:S(2)}) collective-permute-start(bf16[3,4,128,128]{3,2,1,0:T(8,128)(2,1)S(1)} %pad_maximum_fusion.1), channel_id=1, source_target_pairs={{0,2},{1,3},{2,0},{3,1},{4,6},{5,7},{6,4},{7,5},{8,10},{9,11},{10,... | collective-permute-start | bytes 1179656 | tf_op jit(solution)/shard_map/ppermute | solution.py:18
  43.6 3.2 %near.7 = (bf16[16,512,128]{2,1,0:T(8,128)(2,1)S(1)}, f32[16,128,512]{2,1,0:T(8,128)S(1)}) custom-call(s32[4]{0:T(128)S(4)} %get-tuple-element.88.flag_ref, bf16[512,2048]{1,0:T(8,128)(2,1)S(1)} %copy-done, bf16[3,6144]{1,0:T(4,128)(2,1)S(1)} %collective-permute-done.rim_ref, ...), custom_call_target="tpu_custom_call", output_to_operand_aliasing={{0}: (9, {}), {1}: (10, {})} | custom-call | flops 500000000 | bytes 3500000 | tf_op jit(solution)/shard_map/near/pallas_call | solution.py:534
  46.9 5.4 %collective-permute-done.5 = bf16[3,4,128,128]{3,2,1,0:T(8,128)(2,1)S(1)} collective-permute-done((bf16[3,4,128,128]{3,2,1,0:T(8,128)(2,1)S(1)}, bf16[3,4,128,128]{3,2,1,0:T(8,128)(2,1)S(1)}, u32[]{:S(2)}, u32[]{:S(2)}) %collective-permute-start.5) | collective-permute-done | bytes 393248 | tf_op jit(solution)/shard_map/ppermute | solution.py:18
  52.2 0.1 pad_maximum_fusion.own_state_ref
  52.3 2.3 %collective-permute-start.6 = (bf16[3,8,128,128]{3,2,1,0:T(8,128)(2,1)S(1)}, bf16[3,8,128,128]{3,2,1,0:T(8,128)(2,1)S(1)}, u32[]{:S(2)}, u32[]{:S(2)}) collective-permute-start(bf16[3,8,128,128]{3,2,1,0:T(8,128)(2,1)S(1)} %pad_maximum_fusion.own_state_ref), channel_id=1, source_target_pairs={{0,1},{1,0},{2,3},{3,2},{4,5},{5,4},{6,7},{7,6},{8,9},{9,8},{10,11... | collective-permute-start | bytes 2359304 | tf_op jit(solution)/shard_map/ppermute | solution.py:18
  54.6 1.9 %collective-permute-done.6.other_state_ref = bf16[3,8,128,128]{3,2,1,0:T(8,128)(2,1)S(1)} collective-permute-done((bf16[3,8,128,128]{3,2,1,0:T(8,128)(2,1)S(1)}, bf16[3,8,128,128]{3,2,1,0:T(8,128)(2,1)S(1)}, u32[]{:S(2)}, u32[]{:S(2)}) %collective-permute-start.6) | collective-permute-done | bytes 786464 | tf_op jit(solution)/shard_map/ppermute | solution.py:18
  56.6 8.3 %far.1 = bf16[512,2048]{1,0:T(8,128)(2,1)} custom-call(bf16[16,512,128]{2,1,0:T(8,128)(2,1)S(1)} %get-tuple-element.93.query_ref, f32[16,128,512]{2,1,0:T(8,128)S(1)} %get-tuple-element.94.near_ref, f32[14,16,512]{2,1,0:T(8,128)S(1)} %get-tuple-element.66.table_ref, bf16[16,128,128]{2,1,0:T(8,128)(2,1)S(1)} %collective-permute-done.1.theirs_ref.first_state_ref, ...), custom_call_target="tpu_custom_call" | custom-call | tf_op jit(solution)/shard_map/far/pallas_call | solution.py:593
  (9 shorter events, 0.1 us)
Async XLA Ops:
  0.0 8.5 %copy-start.2 = (bf16[512,2048]{1,0:T(8,128)(2,1)S(1)}, bf16[512,2048]{1,0:T(8,128)(2,1)}, u32[]{:S(2)}) copy-start(bf16[512,2048]{1,0:T(8,128)(2,1)} %value_ref.3) | copy-start | bytes 6291460
  0.0 8.5 %copy-start.1 = (bf16[512,2048]{1,0:T(8,128)(2,1)S(1)}, bf16[512,2048]{1,0:T(8,128)(2,1)}, u32[]{:S(2)}) copy-start(bf16[512,2048]{1,0:T(8,128)(2,1)} %key_ref.3) | copy-start | bytes 6291460
  0.0 5.0 %copy-start.5 = (s32[8]{0:T(128)S(1)}, s32[8]{0:T(128)}, u32[]{:S(2)}) copy-start(s32[8]{0:T(128)} %docs_ref.7) | copy-start | bytes 100
  0.0 5.0 %copy-start.6 = (f32[2048]{0:T(1024)S(1)}, f32[2048]{0:T(1024)}, u32[]{:S(2)}) copy-start(f32[2048]{0:T(1024)} %param.12) | copy-start | bytes 24580
  0.0 5.0 %copy-start.4 = (bf16[16,14,512]{2,0,1:T(8,128)(2,1)S(1)}, bf16[16,14,512]{2,0,1:T(8,128)(2,1)}, u32[]{:S(2)}) copy-start(bf16[16,14,512]{2,0,1:T(8,128)(2,1)} %param.11) | copy-start | bytes 688132
  0.0 8.5 %copy-start.3 = (f32[4,6144]{1,0:T(4,128)S(1)}, f32[4,6144]{1,0:T(4,128)}, u32[]{:S(2)}) copy-start(f32[4,6144]{1,0:T(4,128)} %taps_ref.9) | copy-start | bytes 294916
  1.1 7.3 %collective-permute-start = (bf16[3,6144]{1,0:T(4,128)(2,1)S(1)}, bf16[3,6144]{1,0:T(4,128)(2,1)S(1)}, u32[]{:S(2)}, u32[]{:S(2)}) collective-permute-start(bf16[3,6144]{1,0:T(4,128)(2,1)S(1)} %rim.1), channel_id=1, source_target_pairs={{0,1},{1,2},{2,3},{3,4},{4,5},{5,6},{6,7},{7,8},{8,9},{9,10},{10,1... | collective-permute-start | bytes 110600 | tf_op jit(solution)/shard_map/ppermute | solution.py:18
  8.5 14.0 %copy-start = (bf16[512,2048]{1,0:T(8,128)(2,1)S(1)}, bf16[512,2048]{1,0:T(8,128)(2,1)}, u32[]{:S(2)}) copy-start(bf16[512,2048]{1,0:T(8,128)(2,1)} %query_ref.9) | copy-start | bytes 6291460
  19.7 2.0 %collective-permute-start.1 = (bf16[16,128,128]{2,1,0:T(8,128)(2,1)S(1)}, bf16[16,128,128]{2,1,0:T(8,128)(2,1)S(1)}, u32[]{:S(2)}, u32[]{:S(2)}) collective-permute-start(bf16[16,128,128]{2,1,0:T(8,128)(2,1)S(1)} %get-tuple-element.61.mine_ref), channel_id=1, source_target_pairs={{0,1},{1,0},{2,3},{3,2},{4,5},{5,4},{6,7},{7,6},{8,9},{9,8},{10,11... | collective-permute-start | bytes 1572872 | tf_op jit(solution)/shard_map/ppermute | solution.py:18
  22.4 5.0 %collective-permute-start.2 = (bf16[4,128,128]{2,1,0:T(8,128)(2,1)S(1)}, bf16[4,128,128]{2,1,0:T(8,128)(2,1)S(1)}, u32[]{:S(2)}, u32[]{:S(2)}) collective-permute-start(bf16[4,128,128]{2,1,0:T(8,128)(2,1)S(1)} %get-tuple-element.64), channel_id=1, source_target_pairs={{0,2},{1,3},{2,0},{3,1},{4,6},{5,7},{6,4},{7,5},{8,10},{9,11},{10,... | collective-permute-start | bytes 393224 | tf_op jit(solution)/shard_map/ppermute | solution.py:18
  28.1 3.9 %collective-permute-start.3 = (bf16[4,128,128]{2,1,0:T(8,128)(2,1)S(1)}, bf16[4,128,128]{2,1,0:T(8,128)(2,1)S(1)}, u32[]{:S(2)}, u32[]{:S(2)}) collective-permute-start(bf16[4,128,128]{2,1,0:T(8,128)(2,1)S(1)} %join.4.mine_ref), channel_id=1, source_target_pairs={{0,4},{1,5},{2,6},{3,7},{4,0},{5,1},{6,2},{7,3},{8,12},{9,13},{10,... | collective-permute-start | bytes 393224 | tf_op jit(solution)/shard_map/ppermute | solution.py:18
  32.7 10.2 %collective-permute-start.4 = (bf16[4,128,128]{2,1,0:T(8,128)(2,1)S(1)}, bf16[4,128,128]{2,1,0:T(8,128)(2,1)S(1)}, u32[]{:S(2)}, u32[]{:S(2)}) collective-permute-start(bf16[4,128,128]{2,1,0:T(8,128)(2,1)S(1)} %join.5), channel_id=1, source_target_pairs={{0,8},{1,9},{2,10},{3,11},{4,12},{5,13},{6,14},{7,15},{16,24},{17,... | collective-permute-start | bytes 393224 | tf_op jit(solution)/shard_map/ppermute | solution.py:18
  42.9 9.3 %collective-permute-start.5 = (bf16[3,4,128,128]{3,2,1,0:T(8,128)(2,1)S(1)}, bf16[3,4,128,128]{3,2,1,0:T(8,128)(2,1)S(1)}, u32[]{:S(2)}, u32[]{:S(2)}) collective-permute-start(bf16[3,4,128,128]{3,2,1,0:T(8,128)(2,1)S(1)} %pad_maximum_fusion.1), channel_id=1, source_target_pairs={{0,2},{1,3},{2,0},{3,1},{4,6},{5,7},{6,4},{7,5},{8,10},{9,11},{10,... | collective-permute-start | bytes 1179656 | tf_op jit(solution)/shard_map/ppermute | solution.py:18
  52.3 4.2 %collective-permute-start.6 = (bf16[3,8,128,128]{3,2,1,0:T(8,128)(2,1)S(1)}, bf16[3,8,128,128]{3,2,1,0:T(8,128)(2,1)S(1)}, u32[]{:S(2)}, u32[]{:S(2)}) collective-permute-start(bf16[3,8,128,128]{3,2,1,0:T(8,128)(2,1)S(1)} %pad_maximum_fusion.own_state_ref), channel_id=1, source_target_pairs={{0,1},{1,0},{2,3},{3,2},{4,5},{5,4},{6,7},{7,6},{8,9},{9,8},{10,11... | collective-permute-start | bytes 2359304 | tf_op jit(solution)/shard_map/ppermute | solution.py:18

commit v4 on v3

--- a/solution.py
+++ b/solution.py
@@ -73,20 +73,8 @@
         out_ref[:, part * width : (part + 1) * width] = buffer[part, edge - rim_rows : edge, :]
 
 
-def tables_kernel(
-    docs_ref,
-    level_ref,
-    gain_ref,
-    table_ref,
-    start_ref,
-    distance_ref,
-    gain_out_ref,
-    flag_ref,
-    *,
-    doc_count,
-):
+def tables_kernel(docs_ref, level_ref, gain_ref, table_ref, start_ref, gain_out_ref, *, doc_count):
     level_count, head_count, row_count = level_ref.shape
-    tiles = row_count // LANES
     tok_bits = row_count.bit_length() - 1
     index = lax.axis_index("seq")
     first_pos = index * row_count
@@ -94,45 +82,32 @@
     positions = first_pos + (lanes & -LANES) + row_at(lanes & (LANES - 1))
     starts = start_at(docs_ref, doc_count, positions)
     start_ref[...] = starts - first_pos
+    starts = jnp.concatenate([starts] * (head_count // 8), axis=0)
     select = selection(0, 1)
-    starts = jnp.concatenate([starts] * (head_count // 8), axis=0)
-    for level in range(level_count):
-        scale = 2.0 ** (-level / 2)
-        for tile in range(tiles):
-            cols = slice(tile * LANES, (tile + 1) * LANES)
-            weights = jnp.dot(level_ref[level, :, cols], select, preferred_element_type=jnp.float32)
-            weights = weights * scale
+    levels = level_ref[...].reshape(level_count * head_count, row_count)
+    for tile in range(row_count // LANES):
+        cols = slice(tile * LANES, (tile + 1) * LANES)
+        weights = jnp.dot(levels[:, cols], select, preferred_element_type=jnp.float32)
+        for level in range(level_count):
+            scaled = weights[level * head_count : (level + 1) * head_count] * 2.0 ** (-level / 2)
             if level > tok_bits:
                 bit = level - tok_bits - 1
                 limit = jnp.where((index >> bit) & 1 == 1, (index >> bit << bit) * row_count, 0)
-                weights = jnp.where(starts[:, cols] < limit, weights, 0.0)
-            table_ref[level, :, cols] = weights
-    places = lax.broadcasted_iota(jnp.int32, (row_count, LANES), 0)
-    positions = first_pos + (places & -LANES) + row_at(places & (LANES - 1))
-    distance_ref[...] = positions - start_at(docs_ref, doc_count, positions)
-
-    def gain_step(head, carry):
+                scaled = jnp.where(starts[:, cols] < limit, scaled, 0.0)
+            table_ref[level, :, cols] = scaled
+    for head in range(head_count):
         gain_out_ref[head] = jnp.broadcast_to(gain_ref[head], (LANES, LANES)).T
-        return carry
-
-    lax.fori_loop(0, head_count, gain_step, 0)
-
-    for tile in range(tiles):
-        tile_first = first_pos + tile * LANES
-
-        def step(i, flag):
-            gap = docs_ref[i] - tile_first
-            return jnp.where((gap > -8) & (gap < LANES), 1, flag)
-
-        flag_ref[tile] = lax.fori_loop(0, doc_count, step, jnp.int32(0))
-
-
-def fill_window(window_ref, rim, rows):
+
+
+def fill_rim(window_ref, rim):
     rim_rows = rim.shape[0]
     window_ref[0:PAD, :] = jnp.concatenate(
         [jnp.zeros((PAD - rim_rows, rim.shape[1]), jnp.float32), rim.astype(jnp.float32)], axis=0
     )
-    window_ref[PAD:, :] = rows.astype(jnp.float32)
+
+
+def fill_rows(window_ref, rows, first):
+    window_ref[PAD + first : PAD + first + rows.shape[0], :] = rows.astype(jnp.float32)
 
 
 def convolved(window_ref, taps, tile, distance):
@@ -152,7 +127,7 @@
 
 
 def per_tile(flag_ref, tiles, body):
-    for tile in range(tiles):
+    for tile in tiles:
         flagged = flag_ref[tile] == 1
 
         @pl.when(flagged)
@@ -168,17 +143,40 @@
     return pl.ds(pl.multiple_of(first, LANES), LANES)
 
 
-def key_value_kernel(
+def key_value_tile(
+    rim_ref, taps_ref, distance_ref, key_out_ref, value_out_ref, window_ref, head, slot, tile, masked
+):
+    width = taps_ref.shape[1] // 3
+    places = slice(tile * LANES, (tile + 1) * LANES)
+    distance = distance_ref[places, :] if masked else None
+    first = head * LANES
+    key_taps = taps_ref[:, columns(width + first)]
+    value_taps = taps_ref[:, columns(2 * width + first)]
+    grown = silu(convolved(window_ref.at[slot], key_taps, tile, distance))
+    square = jnp.sum(grown * grown, axis=1, keepdims=True)
+    key_out_ref[head, places, :] = (grown * lax.rsqrt(square + 1e-6)).astype(jnp.bfloat16)
+    values = silu(convolved(window_ref.at[slot + 1], value_taps, tile, distance))
+    value_out_ref[head, :, places] = values.T.astype(jnp.bfloat16)
+
+
+def kept_lanes(docs_ref, doc_count, first_pos, row_count, tiles):
+    last_pos = jnp.full((1, len(tiles) * LANES), first_pos + row_count - 1, jnp.int32)
+    last_start = start_at(docs_ref, doc_count, last_pos)
+    lanes = tiles[0] * LANES + lax.broadcasted_iota(jnp.int32, last_pos.shape, 1)
+    lanes_pos = first_pos + (lanes & -LANES) + row_at(lanes & (LANES - 1))
+    return jnp.where(lanes_pos >= last_start, 1.0, 0.0).astype(jnp.bfloat16)
+
+
+def later_rows_kernel(
     docs_ref,
-    flag_ref,
     key_ref,
     value_ref,
-    rim_ref,
     taps_ref,
-    distance_ref,
     key_out_ref,
     value_out_ref,
     state_ref,
+    distance_ref,
+    flag_ref,
     window_ref,
     *,
     doc_count,
@@ -186,56 +184,117 @@
 ):
     row_count, width = key_ref.shape
     head_count = width // LANES
-    steps = head_count // heads
-    tiles = row_count // LANES
-    index = lax.axis_index("seq")
-    first_pos = index * row_count
-
-    last_pos = jnp.full((1, row_count), first_pos + row_count - 1, jnp.int32)
-    last_start = start_at(docs_ref, doc_count, last_pos)
-    lanes = lax.broadcasted_iota(jnp.int32, (1, row_count), 1)
-    lanes_pos = first_pos + (lanes & -LANES) + row_at(lanes & (LANES - 1))
-    keep = jnp.where(lanes_pos >= last_start, 1.0, 0.0).astype(jnp.bfloat16)
-
-    def pair(step, carry):
+    tiles = list(range(1, row_count // LANES))
+    first_pos = lax.axis_index("seq") * row_count
+    keep = kept_lanes(docs_ref, doc_count, first_pos, row_count, tiles)
+    places = lax.broadcasted_iota(jnp.int32, (row_count, LANES), 0)
+    positions = first_pos + (places & -LANES) + row_at(places & (LANES - 1))
+    distance_ref[...] = positions - start_at(docs_ref, doc_count, positions)
+    for tile in range(row_count // LANES):
+        tile_first = first_pos + tile * LANES
+
+        def step(i, flag):
+            gap = docs_ref[i] - tile_first
+            return jnp.where((gap > -8) & (gap < LANES), 1, flag)
+
+        flag_ref[tile] = lax.fori_loop(0, doc_count, step, jnp.int32(0))
+    ahead = LANES - 16
+
+    def group(step, carry):
         for which in range(heads):
-            first = (step * heads + which) * LANES
-            fill_window(
-                window_ref.at[2 * which],
-                rim_ref[:, columns(width + first)],
-                key_ref[:, columns(first)],
-            )
-            fill_window(
-                window_ref.at[2 * which + 1],
-                rim_ref[:, columns(2 * width + first)],
-                value_ref[:, columns(first)],
-            )
+            cols = columns((step * heads + which) * LANES)
+            fill_rows(window_ref.at[2 * which], key_ref[ahead:, cols], ahead)
+            fill_rows(window_ref.at[2 * which + 1], value_ref[ahead:, cols], ahead)
 
         def body(tile, masked):
-            places = slice(tile * LANES, (tile + 1) * LANES)
-            distance = distance_ref[places, :] if masked else None
             for which in range(heads):
-                head = step * heads + which
-                first = head * LANES
-                key_taps = taps_ref[:, columns(width + first)]
-                value_taps = taps_ref[:, columns(2 * width + first)]
-                grown = silu(convolved(window_ref.at[2 * which], key_taps, tile, distance))
-                square = jnp.sum(grown * grown, axis=1, keepdims=True)
-                keys = (grown * lax.rsqrt(square + 1e-6)).astype(jnp.bfloat16)
-                key_out_ref[head, places, :] = keys
-                values = silu(convolved(window_ref.at[2 * which + 1], value_taps, tile, distance))
-                value_out_ref[head, :, places] = values.T.astype(jnp.bfloat16)
+                key_value_tile(
+                    None,
+                    taps_ref,
+                    distance_ref,
+                    key_out_ref,
+                    value_out_ref,
+                    window_ref,
+                    step * heads + which,
+                    2 * which,
+                    tile,
+                    masked,
+                )
 
         per_tile(flag_ref, tiles, body)
         for which in range(heads):
             head = step * heads + which
+            state_ref[head] = jnp.dot(
+                value_out_ref[head, :, LANES:] * keep,
+                key_out_ref[head, LANES:, :],
+                preferred_element_type=jnp.float32,
+            )
+        return carry
+
+    lax.fori_loop(0, head_count // heads, group, 0)
+
+
+def first_rows_kernel(
+    docs_ref,
+    flag_ref,
+    key_ref,
+    value_ref,
+    taps_ref,
+    rim_ref,
+    distance_ref,
+    later_state_ref,
+    key_in_ref,
+    value_in_ref,
+    key_out_ref,
+    value_out_ref,
+    state_ref,
+    window_ref,
+    *,
+    doc_count,
+    row_count,
+    heads,
+):
+    width = key_ref.shape[1]
+    head_count = width // LANES
+    index = lax.axis_index("seq")
+    keep = kept_lanes(docs_ref, doc_count, index * row_count, row_count, [0])
+
+    def group(step, carry):
+        for which in range(heads):
+            first = (step * heads + which) * LANES
+            fill_rim(window_ref.at[2 * which], rim_ref[:, columns(width + first)])
+            fill_rim(window_ref.at[2 * which + 1], rim_ref[:, columns(2 * width + first)])
+            fill_rows(window_ref.at[2 * which], key_ref[0:LANES, columns(first)], 0)
+            fill_rows(window_ref.at[2 * which + 1], value_ref[0:LANES, columns(first)], 0)
+
+        def body(tile, masked):
+            for which in range(heads):
+                key_value_tile(
+                    rim_ref,
+                    taps_ref,
+                    distance_ref,
+                    key_out_ref,
+                    value_out_ref,
+                    window_ref,
+                    step * heads + which,
+                    2 * which,
+                    tile,
+                    masked,
+                )
+
+        per_tile(flag_ref, [0], body)
+        for which in range(heads):
+            head = step * heads + which
+            total = later_state_ref[head] + jnp.dot(
+                value_out_ref[head, :, 0:LANES] * keep,
+                key_out_ref[head, 0:LANES, :],
+                preferred_element_type=jnp.float32,
+            )
             place = logical_place(head, index & 1, (index >> 1) & 1)
-            state_ref[place] = jnp.dot(
-                value_out_ref[head] * keep, key_out_ref[head], preferred_element_type=jnp.float32
-            ).astype(jnp.bfloat16)
+            state_ref[place] = total.astype(jnp.bfloat16)
         return carry
 
-    lax.fori_loop(0, steps, pair, 0)
+    lax.fori_loop(0, head_count // heads, group, 0)
 
 
 def join_kernel(docs_ref, mine_ref, theirs_ref, *out_refs, doc_count, row_count, bit, parts):
@@ -293,11 +352,8 @@
     def group(step, carry):
         for which in range(heads):
             head = first_head + step * heads + which
-            fill_window(
-                window_ref.at[which],
-                rim_ref[:, columns(head * LANES)],
-                query_ref[:, columns(head * LANES)],
-            )
+            fill_rim(window_ref.at[which], rim_ref[:, columns(head * LANES)])
+            fill_rows(window_ref.at[which], query_ref[:, columns(head * LANES)], 0)
 
         def body(tile, masked):
             places = slice(tile * LANES, (tile + 1) * LANES)
@@ -308,7 +364,7 @@
                 grown = silu(convolved(window_ref.at[which], taps, tile, distance))
                 query_out_ref[head, places, :] = grown.astype(jnp.bfloat16)
 
-        per_tile(flag_ref, tiles, body)
+        per_tile(flag_ref, range(tiles), body)
 
         for which in range(heads):
             head = first_head + step * heads + which
@@ -381,70 +437,69 @@
     query_ref,
     near_ref,
     table_ref,
+    gain_ref,
     first_state_ref,
-    own_state_ref,
-    other_state_ref,
-    gain_ref,
-    out_hbm_ref,
-    out_buffer,
-    sems,
-    *,
+    lower_ref,
+    *rest,
+    groups,
     dev_bits,
     heads,
+    skipped,
 ):
+    last_refs = rest[: len(groups)]
+    out_hbm_ref, out_buffer, sems = rest[len(groups) + skipped :]
     head_count, row_count, _ = query_ref.shape
     tiles = row_count // LANES
-    steps = head_count // heads
-    wide = heads * LANES
+    quarter = head_count // 4
     index = lax.axis_index("seq")
     core_bit = index & 1
     y_bit = (index >> 1) & 1
     tok_bits = row_count.bit_length() - 1
     select = selection(0, 1)
-
-    def copy(step):
-        cols = pl.ds(pl.multiple_of(step * wide, wide), wide)
-        return pltpu.make_async_copy(
-            out_buffer.at[:, cols], out_hbm_ref.at[:, cols], sems.at[step]
-        )
-
-    def group(step, carry):
-        for which in range(heads):
-            head = step * heads + which
-            first_place = logical_place(head, 1 - core_bit, y_bit)
-            place = logical_place(head, core_bit, y_bit)
-            is_own = place < 8
-            states = [first_state_ref[first_place]]
-            for level in range(dev_bits - 1):
-                states.append(
-                    jnp.where(
-                        is_own, own_state_ref[level, place & 7], other_state_ref[level, place & 7]
+    copies = []
+    for group, (last_ref, (other_half, other_quarter)) in enumerate(zip(last_refs, groups)):
+        first_head = (core_bit ^ other_half) * 2 * quarter + (y_bit ^ other_quarter) * quarter
+
+        def body(step, carry):
+            for which in range(heads):
+                local_head = step * heads + which
+                head = first_head + local_head
+                first_place = logical_place(head, 1 - core_bit, y_bit)
+                place = logical_place(head, core_bit, y_bit) & 7
+                states = [first_state_ref[first_place]]
+                for level in range(dev_bits - 2):
+                    states.append(lower_ref[level, place])
+                states.append(last_ref[local_head])
+                images = lax.dot_general(
+                    jnp.concatenate(states, axis=0),
+                    query_ref[head],
+                    NT,
+                    preferred_element_type=jnp.float32,
+                )
+                summed = near_ref[head]
+                for bit in range(dev_bits):
+                    coef = table_ref[tok_bits + 1 + bit, pl.ds(head, 1), :]
+                    summed = summed + coef * images[bit * LANES : (bit + 1) * LANES, :]
+                mean = jnp.mean(summed * summed, axis=0, keepdims=True)
+                normed = summed * lax.rsqrt(mean + 1e-6)
+                gain = gain_ref[head]
+                for tile in range(tiles):
+                    cols = slice(tile * LANES, (tile + 1) * LANES)
+                    done = (normed[:, cols] * gain).astype(jnp.bfloat16)
+                    turned = lax.dot_general(select, done, NT, preferred_element_type=jnp.float32)
+                    out_buffer[group, cols, columns(local_head * LANES)] = turned.astype(
+                        jnp.bfloat16
                     )
-                )
-            images = lax.dot_general(
-                jnp.concatenate(states, axis=0),
-                query_ref[head],
-                NT,
-                preferred_element_type=jnp.float32,
-            )
-            summed = near_ref[head]
-            for bit in range(dev_bits):
-                coef = table_ref[tok_bits + 1 + bit, pl.ds(head, 1), :]
-                summed = summed + coef * images[bit * LANES : (bit + 1) * LANES, :]
-            mean = jnp.mean(summed * summed, axis=0, keepdims=True)
-            normed = summed * lax.rsqrt(mean + 1e-6)
-            gain = gain_ref[head]
-            for tile in range(tiles):
-                cols = slice(tile * LANES, (tile + 1) * LANES)
-                done = (normed[:, cols] * gain).astype(jnp.bfloat16)
-                turned = lax.dot_general(select, done, NT, preferred_element_type=jnp.float32)
-                out_buffer[cols, columns(head * LANES)] = turned.astype(jnp.bfloat16)
-        copy(step).start()
-        return carry
-
-    lax.fori_loop(0, steps, group, 0)
-    for step in range(steps):
-        copy(step).wait()
+            return carry
+
+        lax.fori_loop(0, quarter // heads, body, 0)
+        wide = quarter * LANES
+        cols = pl.ds(pl.multiple_of(first_head * LANES, wide), wide)
+        copy = pltpu.make_async_copy(out_buffer.at[group], out_hbm_ref.at[:, cols], sems.at[group])
+        copy.start()
+        copies.append(copy)
+    for copy in copies:
+        copy.wait()
 
 
 def local(query_in, key_in, value_in, conv_weight, level_weight, out_gain, doc_starts):
@@ -476,41 +531,44 @@
     )(*(pltpu.with_memory_space_constraint(x, pltpu.HBM) for x in (query_in, key_in, value_in)))
     tails, docs = lax.optimization_barrier((tails, doc_starts))
     rims = exchange(tails, lambda i: i + 1 if i + 1 < dev_count else None)
-    table, starts, distance, gains, flags = pl.pallas_call(
-        functools.partial(tables_kernel, doc_count=doc_count),
-        in_specs=[smem, vmem, vmem],
-        out_specs=[vmem, vmem, vmem, vmem, smem],
+    heads = 2
+    keys, values_t, later_state, distance, flags = pl.pallas_call(
+        functools.partial(later_rows_kernel, doc_count=doc_count, heads=heads),
+        in_specs=[smem] + [vmem] * 3,
+        out_specs=[vmem] * 4 + [smem],
         out_shape=[
-            pltpu.VMEM((level_count, head_count, row_count), jnp.float32),
-            pltpu.VMEM((8, row_count), jnp.int32),
+            pltpu.VMEM((head_count, row_count, head_size), jnp.bfloat16),
+            pltpu.VMEM((head_count, head_size, row_count), jnp.bfloat16),
+            pltpu.VMEM((head_count, head_size, head_size), jnp.float32),
             pltpu.VMEM((row_count, LANES), jnp.int32),
-            pltpu.VMEM((head_count, head_size, LANES), jnp.float32),
             pltpu.SMEM((tiles,), jnp.int32),
         ],
-        compiler_params=limited(4),
-        name="tables",
-    )(docs, jnp.transpose(level_weight, (1, 0, 2)), out_gain.reshape(head_count, 1, head_size))
-    rims, table, starts, distance, gains, flags = lax.optimization_barrier(
-        (rims, table, starts, distance, gains, flags)
+        scratch_shapes=[pltpu.VMEM((2 * heads, row_count + PAD, LANES), jnp.float32)],
+        compiler_params=limited(3),
+        cost_estimate=pl.CostEstimate(
+            flops=500_000_000, bytes_accessed=4_000_000, transcendentals=1_500_000
+        ),
+        name="later_rows",
+    )(docs, key_in, value_in, conv_weight)
+    rims, keys, values_t, later_state, flags = lax.optimization_barrier(
+        (rims, keys, values_t, later_state, flags)
     )
-
-    heads = 2
-    steps = head_count // heads
     keys, values_t, state = pl.pallas_call(
-        functools.partial(key_value_kernel, doc_count=doc_count, heads=heads),
-        in_specs=[smem, smem] + [vmem] * 5,
+        functools.partial(
+            first_rows_kernel, doc_count=doc_count, row_count=row_count, heads=heads
+        ),
+        in_specs=[smem, smem] + [vmem] * 8,
         out_specs=[vmem] * 3,
         out_shape=[
             pltpu.VMEM((head_count, row_count, head_size), jnp.bfloat16),
             pltpu.VMEM((head_count, head_size, row_count), jnp.bfloat16),
             pltpu.VMEM((head_count, head_size, head_size), jnp.bfloat16),
         ],
-        scratch_shapes=[
-            pltpu.VMEM((2 * heads, row_count + PAD, LANES), jnp.float32),
-        ],
-        compiler_params=limited(4),
-        name="key_value",
-    )(docs, flags, key_in, value_in, rims, conv_weight, distance)
+        scratch_shapes=[pltpu.VMEM((2 * heads, LANES + PAD, LANES), jnp.float32)],
+        input_output_aliases={8: 0, 9: 1},
+        compiler_params=limited(2),
+        name="first_rows",
+    )(docs, flags, key_in, value_in, conv_weight, rims, distance, later_state, keys, values_t)
 
     def joined(mine, theirs, bit, parts=1):
         count = mine.shape[0] // (2 if parts == 2 else 1)
@@ -526,15 +584,12 @@
             name="join",
         )(doc_starts, mine, theirs)
 
-    buffers = None
-    piece_heads = head_count // 4
-
-    def near_piece(piece, buffers, flags):
+    def near_piece(first_head, piece_heads, buffers, flags):
         extra = [] if buffers is None else list(buffers)
         return pl.pallas_call(
             functools.partial(
                 near_kernel,
-                first_head=piece * piece_heads,
+                first_head=first_head,
                 head_count=piece_heads,
                 heads=heads,
                 skipped=len(extra),
@@ -553,55 +608,90 @@
             input_output_aliases={9: 0, 10: 1} if extra else {},
             compiler_params=limited(6),
             cost_estimate=pl.CostEstimate(
-                flops=500_000_000, bytes_accessed=3_500_000, transcendentals=300_000
+                flops=1_000_000, bytes_accessed=10_000, transcendentals=0
             ),
             name="near",
         )(flags, query_in, rims, conv_weight, distance, table, starts, keys, values_t, *extra)
 
-    def covered(payload, send, piece, buffers):
-        payload, tied = lax.optimization_barrier((payload, flags))
-        arrived = send(payload)
-        buffers = near_piece(piece, buffers, tied)
-        arrived, buffers = lax.optimization_barrier((arrived, buffers))
-        return arrived, buffers
-
+    def far_piece(groups, lower, last_states, out):
+        extra = [] if out is None else [out]
+        return pl.pallas_call(
+            functools.partial(
+                far_kernel, groups=groups, dev_bits=dev_bits, heads=heads, skipped=len(extra)
+            ),
+            in_specs=[vmem] * (6 + len(groups)) + [anywhere] * len(extra),
+            out_specs=anywhere,
+            out_shape=jax.ShapeDtypeStruct((row_count, width_all), jnp.bfloat16),
+            scratch_shapes=[
+                pltpu.VMEM((len(groups), row_count, quarter * head_size), jnp.bfloat16),
+                pltpu.SemaphoreType.DMA((len(groups),)),
+            ],
+            input_output_aliases={6 + len(groups): 0} if extra else {},
+            compiler_params=limited(4),
+            cost_estimate=pl.CostEstimate(
+                flops=1_000_000, bytes_accessed=10_000, transcendentals=0
+            ),
+            name="far",
+        )(queries, near, table, gains, first_state, lower, *last_states, *extra)
+
+    quarter = head_count // 4
+    state, docs = lax.optimization_barrier((state, docs))
     first_state = swapped(state, 0)
+    table, starts, gains = pl.pallas_call(
+        functools.partial(tables_kernel, doc_count=doc_count),
+        in_specs=[smem, vmem, vmem],
+        out_specs=[vmem] * 3,
+        out_shape=[
+            pltpu.VMEM((level_count, head_count, row_count), jnp.float32),
+            pltpu.VMEM((8, row_count), jnp.int32),
+            pltpu.VMEM((head_count, head_size, LANES), jnp.float32),
+        ],
+        compiler_params=limited(2),
+        name="tables",
+    )(docs, jnp.transpose(level_weight, (1, 0, 2)), out_gain.reshape(head_count, 1, head_size))
+    first_state, table, starts, gains = lax.optimization_barrier(
+        (first_state, table, starts, gains)
+    )
     pair_kept, pair_sent = joined(state, first_state, 0, parts=2)
-    pair_in, buffers = covered(pair_sent, lambda x: swapped(x, 1), 0, buffers)
+
+    pair_sent, tied = lax.optimization_barrier((pair_sent, flags))
+    pair_in = swapped(pair_sent, 1)
+    buffers = near_piece(0, quarter, None, tied)
+    pair_in, buffers = lax.optimization_barrier((pair_in, buffers))
     (carried,) = joined(pair_kept, pair_in, 1)
+
     received = []
-    for bit in range(2, dev_bits):
-        last = bit == dev_bits - 1
-        if last:
-            arrived, buffers = covered(carried, lambda x: sent_up(x, bit), 2, buffers)
-        elif bit == 2:
-            arrived, buffers = covered(carried, lambda x: swapped(x, bit), 1, buffers)
-        else:
-            arrived = swapped(carried, bit)
+    for bit in range(2, dev_bits - 1):
+        if bit == 2:
+            carried, tied = lax.optimization_barrier((carried, flags))
+        arrived = swapped(carried, bit)
+        if bit == 2:
+            buffers = near_piece(quarter, quarter, buffers, tied)
+            arrived, buffers = lax.optimization_barrier((arrived, buffers))
         received.append(arrived)
-        if not last:
-            (carried,) = joined(carried, arrived, bit)
+        (carried,) = joined(carried, arrived, bit)
 
     mine = jnp.stack([pair_kept] + received)
-    theirs, buffers = covered(mine, lambda x: swapped(x, 1), 3, buffers)
+    carried, mine, tied = lax.optimization_barrier((carried, mine, flags))
+    last_own = sent_up(carried, dev_bits - 1)
+    theirs = swapped(mine, 1)
+    buffers = near_piece(2 * quarter, 2 * quarter, buffers, tied)
+    last_own, theirs, buffers = lax.optimization_barrier((last_own, theirs, buffers))
     queries, near = buffers
-    own = jnp.concatenate(
-        [jnp.concatenate([pair_in[None], mine[1:]], axis=0), theirs], axis=1
-    )
+    own = jnp.concatenate([jnp.stack([pair_in] + received), theirs], axis=1)
+    own, last_own = lax.optimization_barrier((own, last_own))
+
+    last_next = swapped(last_own, 1)
     other = swapped(own, 0)
-
-    return pl.pallas_call(
-        functools.partial(far_kernel, dev_bits=dev_bits, heads=heads),
-        in_specs=[vmem] * 7,
-        out_specs=anywhere,
-        out_shape=jax.ShapeDtypeStruct((row_count, width_all), jnp.bfloat16),
-        scratch_shapes=[
-            pltpu.VMEM((row_count, width_all), jnp.bfloat16),
-            pltpu.SemaphoreType.DMA((steps,)),
-        ],
-        compiler_params=limited(8),
-        name="far",
-    )(queries, near, table, first_state, own, other, gains)
+    last_other = swapped(last_own, 0)
+    out = far_piece(((0, 0),), own, (last_own,), None)
+    other, last_other, out = lax.optimization_barrier((other, last_other, out))
+    out = far_piece(((1, 0),), other, (last_other,), out)
+    last_next, out = lax.optimization_barrier((last_next, out))
+    last_far = swapped(last_next, 0)
+    out = far_piece(((0, 1),), own, (last_next,), out)
+    last_far, out = lax.optimization_barrier((last_far, out))
+    return far_piece(((1, 1),), other, (last_far,), out)
 
 
 def solution(mesh):

time: 65 us -> 59.3 us (0.912)
  the two profiles are of different devices: /device:TPU:27 before, /device:TPU:0 now
where the time goes in v4:
time: 59.3 us; the launch traced here: 59.4 us
  Pallas kernels  42 us (71%)
  starting transfers between devices  15.4 us (26%)
  waiting for transfers between devices  1.69 us (3%)
    ppermute x10, starting transfers between devices, exchange(): return lax.ppermute(block, 'seq', route)  15.4 us
    pallas_call x3, Pallas kernels, near_piece(): pl.pallas_call(functools.partial(near_kernel, first_head=first_head, head...  13.1 us
    pallas_call x4, Pallas kernels, far_piece(): pl.pallas_call(functools.partial(far_kernel, groups=groups, dev_bits=dev_...  10.7 us
    pallas_call x1, Pallas kernels, local(): pl.pallas_call(functools.partial(later_rows_kernel, doc_count=doc_count,...  9.67 us
    pallas_call x1, Pallas kernels, local(): pl.pallas_call(functools.partial(first_rows_kernel, doc_count=doc_count,...  4.46 us
    pallas_call x3, Pallas kernels, joined(): pl.pallas_call(functools.partial(join_kernel, doc_count=doc_count, row_co...  2.04 us
    ppermute x10, waiting for transfers between devices, exchange(): return lax.ppermute(block, 'seq', route)  1.69 us
  transfers between devices with their start and end apart: 10, of which 3 were waited for; matrix products, arithmetic and copies ran while one was open for 0% of the time, Pallas kernels for 53%

profile of v4, /device:TPU:0, one launch (start us, length us, event | category | flops | bytes accessed | tf_op | source)
XLA Modules:
  0.0 59.4 jit_solution(7448499737994890439)
XLA Ops:
  0.0 1.1 %rim.1 = bf16[3,6144]{1,0:T(4,128)(2,1)S(1)} custom-call(bf16[512,2048]{1,0:T(8,128)(2,1)} %query_ref.7, bf16[512,2048]{1,0:T(8,128)(2,1)} %key_ref.5, bf16[512,2048]{1,0:T(8,128)(2,1)} %value_ref.5), custom_call_target="tpu_custom_call" | custom-call | tf_op jit(solution)/shard_map/rim/pallas_call | solution.py:520
  1.1 2.5 %collective-permute-start = (bf16[3,6144]{1,0:T(4,128)(2,1)S(1)}, bf16[3,6144]{1,0:T(4,128)(2,1)S(1)}, u32[]{:S(2)}, u32[]{:S(2)}) collective-permute-start(bf16[3,6144]{1,0:T(4,128)(2,1)S(1)} %rim.1), channel_id=1, source_target_pairs={{0,1},{1,2},{2,3},{3,4},{4,5},{5,6},{6,7},{7,8},{8,9},{9,10},{10,1... | collective-permute-start | bytes 110600 | tf_op jit(solution)/shard_map/ppermute | solution.py:18
  3.7 9.7 %later_rows.1 = (bf16[16,512,128]{2,1,0:T(8,128)(2,1)S(1)}, bf16[16,128,512]{2,1,0:T(8,128)(2,1)S(1)}, f32[16,128,128]{2,1,0:T(8,128)S(1)}, s32[512,128]{1,0:T(8,128)S(1)}, s32[4]{0:T(128)S(4)}) custom-call(s32[8]{0:T(128)S(1)} %copy-done.5, bf16[512,2048]{1,0:T(8,128)(2,1)S(1)} %copy-done.1, bf16[512,2048]{1,0:T(8,128)(2,1)S(1)} %copy-done.2, ...), custom_call_target="tpu_custom_call" | custom-call | flops 500000000 | bytes 4000000 | tf_op jit(solution)/shard_map/later_rows/pallas_call | solution.py:535
  13.3 0.0 collective-permute-done.rim_ref
  13.3 0.0 copy-start.4
  13.4 0.0 copy-start.6
  13.4 0.0 copy-start
  13.4 4.5 %first_rows.1 = (bf16[16,512,128]{2,1,0:T(8,128)(2,1)S(1)}, bf16[16,128,512]{2,1,0:T(8,128)(2,1)S(1)}, bf16[16,128,128]{2,1,0:T(8,128)(2,1)S(1)}) custom-call(s32[8]{0:T(128)S(1)} %copy-done.5, s32[4]{0:T(128)S(4)} %get-tuple-element.102.flag_ref, bf16[512,2048]{1,0:T(8,128)(2,1)S(1)} %copy-done.1, ...), custom_call_target="tpu_custom_call", output_to_operand_aliasing={{0}: (8, {}), {1}: (9, {})} | custom-call | tf_op jit(solution)/shard_map/first_rows/pallas_call | solution.py:556
  17.8 1.8 %collective-permute-start.1 = (bf16[16,128,128]{2,1,0:T(8,128)(2,1)S(1)}, bf16[16,128,128]{2,1,0:T(8,128)(2,1)S(1)}, u32[]{:S(2)}, u32[]{:S(2)}) collective-permute-start(bf16[16,128,128]{2,1,0:T(8,128)(2,1)S(1)} %get-tuple-element.76.mine_ref), channel_id=1, source_target_pairs={{0,1},{1,0},{2,3},{3,2},{4,5},{5,4},{6,7},{7,6},{8,9},{9,8},{10,11... | collective-permute-start | bytes 1572872 | tf_op jit(solution)/shard_map/ppermute | solution.py:18
  19.7 0.9 %tables.1 = (f32[14,16,512]{2,1,0:T(8,128)S(1)}, s32[8,512]{1,0:T(8,128)S(1)}, f32[16,128,128]{2,1,0:T(8,128)S(1)}) custom-call(s32[8]{0:T(128)S(1)} %copy-done.5, bf16[14,16,512]{2,1,0:T(8,128)(2,1)S(1)} %bitcast.9, f32[16,1,128]{2,1,0:T(1,128)S(1)} %bitcast.10), custom_call_target="tpu_custom_call" | custom-call | tf_op jit(solution)/shard_map/tables/pallas_call | solution.py:640
  20.6 0.6 collective-permute-done.1.theirs_ref.first_state_ref
  21.2 0.7 %join.3 = (bf16[4,128,128]{2,1,0:T(8,128)(2,1)S(1)}, bf16[4,128,128]{2,1,0:T(8,128)(2,1)S(1)}) custom-call(s32[8]{0:T(128)S(1)} %copy-done.5, bf16[16,128,128]{2,1,0:T(8,128)(2,1)S(1)} %get-tuple-element.76.mine_ref, bf16[16,128,128]{2,1,0:T(8,128)(2,1)S(1)} %collective-permute-done.1.theirs_ref.first_state_ref), custom_call_target="tpu_custom_call" | custom-call | tf_op jit(solution)/shard_map/join/pallas_call | solution.py:576
  21.9 1.6 %collective-permute-start.2 = (bf16[4,128,128]{2,1,0:T(8,128)(2,1)S(1)}, bf16[4,128,128]{2,1,0:T(8,128)(2,1)S(1)}, u32[]{:S(2)}, u32[]{:S(2)}) collective-permute-start(bf16[4,128,128]{2,1,0:T(8,128)(2,1)S(1)} %get-tuple-element.84), channel_id=1, source_target_pairs={{0,2},{1,3},{2,0},{3,1},{4,6},{5,7},{6,4},{7,5},{8,10},{9,11},{10,... | collective-permute-start | bytes 393224 | tf_op jit(solution)/shard_map/ppermute | solution.py:18
  23.5 3.3 %near.3 = (bf16[16,512,128]{2,1,0:T(8,128)(2,1)S(1)}, f32[16,128,512]{2,1,0:T(8,128)S(1)}) custom-call(s32[4]{0:T(128)S(4)} %get-tuple-element.102.flag_ref, bf16[512,2048]{1,0:T(8,128)(2,1)S(1)} %copy-done, bf16[3,6144]{1,0:T(4,128)(2,1)S(1)} %collective-permute-done.rim_ref, f32[4,6144]{1,0:T(4,128)S(1)} %copy-done.3, ...), custom_call_target="tpu_custom_call" | custom-call | flops 1000000 | bytes 10000 | tf_op jit(solution)/shard_map/near/pallas_call | solution.py:589
  26.8 1.0 %collective-permute-done.2.theirs_ref = bf16[4,128,128]{2,1,0:T(8,128)(2,1)S(1)} collective-permute-done((bf16[4,128,128]{2,1,0:T(8,128)(2,1)S(1)}, bf16[4,128,128]{2,1,0:T(8,128)(2,1)S(1)}, u32[]{:S(2)}, u32[]{:S(2)}) %collective-permute-start.2) | collective-permute-done | bytes 131104 | tf_op jit(solution)/shard_map/ppermute | solution.py:18
  27.7 0.7 %join.4.mine_ref = bf16[4,128,128]{2,1,0:T(8,128)(2,1)S(1)} custom-call(s32[8]{0:T(128)S(1)} %copy-done.5, bf16[4,128,128]{2,1,0:T(8,128)(2,1)S(1)} %get-tuple-element.82.mine_ref, bf16[4,128,128]{2,1,0:T(8,128)(2,1)S(1)} %collective-permute-done.2.theirs_ref), custom_call_target="tpu_custom_call" | custom-call | tf_op jit(solution)/shard_map/join/pallas_call | solution.py:576
  28.4 1.6 %collective-permute-start.3 = (bf16[4,128,128]{2,1,0:T(8,128)(2,1)S(1)}, bf16[4,128,128]{2,1,0:T(8,128)(2,1)S(1)}, u32[]{:S(2)}, u32[]{:S(2)}) collective-permute-start(bf16[4,128,128]{2,1,0:T(8,128)(2,1)S(1)} %join.4.mine_ref), channel_id=1, source_target_pairs={{0,4},{1,5},{2,6},{3,7},{4,0},{5,1},{6,2},{7,3},{8,12},{9,13},{10,... | collective-permute-start | bytes 393224 | tf_op jit(solution)/shard_map/ppermute | solution.py:18
  30.1 3.3 %near.4 = (bf16[16,512,128]{2,1,0:T(8,128)(2,1)S(1)}, f32[16,128,512]{2,1,0:T(8,128)S(1)}) custom-call(s32[4]{0:T(128)S(4)} %get-tuple-element.102.flag_ref, bf16[512,2048]{1,0:T(8,128)(2,1)S(1)} %copy-done, bf16[3,6144]{1,0:T(4,128)(2,1)S(1)} %collective-permute-done.rim_ref, ...), custom_call_target="tpu_custom_call", output_to_operand_aliasing={{0}: (9, {}), {1}: (10, {})} | custom-call | flops 1000000 | bytes 10000 | tf_op jit(solution)/shard_map/near/pallas_call | solution.py:589
  33.3 0.1 collective-permute-done.3.theirs_ref
  33.5 0.7 %join.5 = bf16[4,128,128]{2,1,0:T(8,128)(2,1)S(1)} custom-call(s32[8]{0:T(128)S(1)} %copy-done.5, bf16[4,128,128]{2,1,0:T(8,128)(2,1)S(1)} %join.4.mine_ref, bf16[4,128,128]{2,1,0:T(8,128)(2,1)S(1)} %collective-permute-done.3.theirs_ref), custom_call_target="tpu_custom_call" | custom-call | tf_op jit(solution)/shard_map/join/pallas_call | solution.py:576
  34.2 1.6 %collective-permute-start.5 = (bf16[2,4,128,128]{3,2,1,0:T(8,128)(2,1)S(1)}, bf16[2,4,128,128]{3,2,1,0:T(8,128)(2,1)S(1)}, u32[]{:S(2)}, u32[]{:S(2)}) collective-permute-start(bf16[2,4,128,128]{3,2,1,0:T(8,128)(2,1)S(1)} %pad_maximum_fusion.1), channel_id=1, source_target_pairs={{0,2},{1,3},{2,0},{3,1},{4,6},{5,7},{6,4},{7,5},{8,10},{9,11},{10,... | collective-permute-start | bytes 786440 | tf_op jit(solution)/shard_map/ppermute | solution.py:18
  35.7 4.5 %collective-permute-start.4 = (bf16[4,128,128]{2,1,0:T(8,128)(2,1)S(1)}, bf16[4,128,128]{2,1,0:T(8,128)(2,1)S(1)}, u32[]{:S(2)}, u32[]{:S(2)}) collective-permute-start(bf16[4,128,128]{2,1,0:T(8,128)(2,1)S(1)} %join.5), channel_id=1, source_target_pairs={{0,8},{1,9},{2,10},{3,11},{4,12},{5,13},{6,14},{7,15},{16,24},{17,... | collective-permute-start | bytes 393224 | tf_op jit(solution)/shard_map/ppermute | solution.py:18
  40.2 6.5 %near.5 = (bf16[16,512,128]{2,1,0:T(8,128)(2,1)S(1)}, f32[16,128,512]{2,1,0:T(8,128)S(1)}) custom-call(s32[4]{0:T(128)S(4)} %get-tuple-element.102.flag_ref, bf16[512,2048]{1,0:T(8,128)(2,1)S(1)} %copy-done, bf16[3,6144]{1,0:T(4,128)(2,1)S(1)} %collective-permute-done.rim_ref, ...), custom_call_target="tpu_custom_call", output_to_operand_aliasing={{0}: (9, {}), {1}: (10, {})} | custom-call | flops 1000000 | bytes 10000 | tf_op jit(solution)/shard_map/near/pallas_call | solution.py:589
  46.8 0.1 pad_maximum_fusion.lower_ref
  46.9 0.1 collective-permute-start.6
  46.9 0.5 collective-permute-start.7
  47.4 1.2 %collective-permute-start.8 = (bf16[4,128,128]{2,1,0:T(8,128)(2,1)S(1)}, bf16[4,128,128]{2,1,0:T(8,128)(2,1)S(1)}, u32[]{:S(2)}, u32[]{:S(2)}) collective-permute-start(bf16[4,128,128]{2,1,0:T(8,128)(2,1)S(1)} %collective-permute-done.4.rest_0_), channel_id=1, source_target_pairs={{0,2},{1,3},{2,0},{3,1},{4,6},{5,7},{6,4},{7,5},{8,10},{9,11},{10,... | collective-permute-start | bytes 393224 | tf_op jit(solution)/shard_map/ppermute | solution.py:18
  48.6 2.7 %far.4.rest_1_ = bf16[512,2048]{1,0:T(8,128)(2,1)} custom-call(bf16[16,512,128]{2,1,0:T(8,128)(2,1)S(1)} %get-tuple-element.107.query_ref, f32[16,128,512]{2,1,0:T(8,128)S(1)} %get-tuple-element.108.near_ref, f32[14,16,512]{2,1,0:T(8,128)S(1)} %get-tuple-element.86.table_ref, f32[16,128,128]{2,1,0:T(8,128)S(1)} %get-tuple-element.109.gain_ref, ...), custom_call_target="tpu_custom_call" | custom-call | flops 1000000 | bytes 10000 | tf_op jit(solution)/shard_map/far/pallas_call | solution.py:618
  51.3 2.7 %far.5.rest_1_ = bf16[512,2048]{1,0:T(8,128)(2,1)} custom-call(bf16[16,512,128]{2,1,0:T(8,128)(2,1)S(1)} %get-tuple-element.107.query_ref, f32[16,128,512]{2,1,0:T(8,128)S(1)} %get-tuple-element.108.near_ref, f32[14,16,512]{2,1,0:T(8,128)S(1)} %get-tuple-element.86.table_ref, ...), custom_call_target="tpu_custom_call", output_to_operand_aliasing={{}: (7, {})} | custom-call | flops 1000000 | bytes 10000 | tf_op jit(solution)/shard_map/far/pallas_call | solution.py:618
  54.0 0.1 collective-permute-start.9
  54.1 2.7 %far.6.rest_1_ = bf16[512,2048]{1,0:T(8,128)(2,1)} custom-call(bf16[16,512,128]{2,1,0:T(8,128)(2,1)S(1)} %get-tuple-element.107.query_ref, f32[16,128,512]{2,1,0:T(8,128)S(1)} %get-tuple-element.108.near_ref, f32[14,16,512]{2,1,0:T(8,128)S(1)} %get-tuple-element.86.table_ref, ...), custom_call_target="tpu_custom_call", output_to_operand_aliasing={{}: (7, {})} | custom-call | flops 1000000 | bytes 10000 | tf_op jit(solution)/shard_map/far/pallas_call | solution.py:618
  56.8 2.7 %far.7 = bf16[512,2048]{1,0:T(8,128)(2,1)} custom-call(bf16[16,512,128]{2,1,0:T(8,128)(2,1)S(1)} %get-tuple-element.107.query_ref, f32[16,128,512]{2,1,0:T(8,128)S(1)} %get-tuple-element.108.near_ref, f32[14,16,512]{2,1,0:T(8,128)S(1)} %get-tuple-element.86.table_ref, ...), custom_call_target="tpu_custom_call", output_to_operand_aliasing={{}: (7, {})} | custom-call | flops 1000000 | bytes 10000 | tf_op jit(solution)/shard_map/far/pallas_call | solution.py:618
  (18 shorter events, 0.1 us)
Async XLA Ops:
  0.0 3.6 %copy-start.2 = (bf16[512,2048]{1,0:T(8,128)(2,1)S(1)}, bf16[512,2048]{1,0:T(8,128)(2,1)}, u32[]{:S(2)}) copy-start(bf16[512,2048]{1,0:T(8,128)(2,1)} %value_ref.5) | copy-start | bytes 6291460
  0.0 3.6 %copy-start.1 = (bf16[512,2048]{1,0:T(8,128)(2,1)S(1)}, bf16[512,2048]{1,0:T(8,128)(2,1)}, u32[]{:S(2)}) copy-start(bf16[512,2048]{1,0:T(8,128)(2,1)} %key_ref.5) | copy-start | bytes 6291460
  0.0 3.6 %copy-start.5 = (s32[8]{0:T(128)S(1)}, s32[8]{0:T(128)}, u32[]{:S(2)}) copy-start(s32[8]{0:T(128)} %docs_ref.8) | copy-start | bytes 100
  0.0 3.6 %copy-start.3 = (f32[4,6144]{1,0:T(4,128)S(1)}, f32[4,6144]{1,0:T(4,128)}, u32[]{:S(2)}) copy-start(f32[4,6144]{1,0:T(4,128)} %taps_ref.9) | copy-start | bytes 294916
  1.1 12.2 %collective-permute-start = (bf16[3,6144]{1,0:T(4,128)(2,1)S(1)}, bf16[3,6144]{1,0:T(4,128)(2,1)S(1)}, u32[]{:S(2)}, u32[]{:S(2)}) collective-permute-start(bf16[3,6144]{1,0:T(4,128)(2,1)S(1)} %rim.1), channel_id=1, source_target_pairs={{0,1},{1,2},{2,3},{3,4},{4,5},{5,6},{6,7},{7,8},{8,9},{9,10},{10,1... | collective-permute-start | bytes 110600 | tf_op jit(solution)/shard_map/ppermute | solution.py:18
  13.3 6.3 %copy-start.4 = (bf16[16,14,512]{2,0,1:T(8,128)(2,1)S(1)}, bf16[16,14,512]{2,0,1:T(8,128)(2,1)}, u32[]{:S(2)}) copy-start(bf16[16,14,512]{2,0,1:T(8,128)(2,1)} %param.11) | copy-start | bytes 688132
  13.4 6.3 %copy-start.6 = (f32[2048]{0:T(1024)S(1)}, f32[2048]{0:T(1024)}, u32[]{:S(2)}) copy-start(f32[2048]{0:T(1024)} %param.12) | copy-start | bytes 24580
  13.4 10.1 %copy-start = (bf16[512,2048]{1,0:T(8,128)(2,1)S(1)}, bf16[512,2048]{1,0:T(8,128)(2,1)}, u32[]{:S(2)}) copy-start(bf16[512,2048]{1,0:T(8,128)(2,1)} %query_ref.7) | copy-start | bytes 6291460
  17.8 3.3 %collective-permute-start.1 = (bf16[16,128,128]{2,1,0:T(8,128)(2,1)S(1)}, bf16[16,128,128]{2,1,0:T(8,128)(2,1)S(1)}, u32[]{:S(2)}, u32[]{:S(2)}) collective-permute-start(bf16[16,128,128]{2,1,0:T(8,128)(2,1)S(1)} %get-tuple-element.76.mine_ref), channel_id=1, source_target_pairs={{0,1},{1,0},{2,3},{3,2},{4,5},{5,4},{6,7},{7,6},{8,9},{9,8},{10,11... | collective-permute-start | bytes 1572872 | tf_op jit(solution)/shard_map/ppermute | solution.py:18
  21.9 5.8 %collective-permute-start.2 = (bf16[4,128,128]{2,1,0:T(8,128)(2,1)S(1)}, bf16[4,128,128]{2,1,0:T(8,128)(2,1)S(1)}, u32[]{:S(2)}, u32[]{:S(2)}) collective-permute-start(bf16[4,128,128]{2,1,0:T(8,128)(2,1)S(1)} %get-tuple-element.84), channel_id=1, source_target_pairs={{0,2},{1,3},{2,0},{3,1},{4,6},{5,7},{6,4},{7,5},{8,10},{9,11},{10,... | collective-permute-start | bytes 393224 | tf_op jit(solution)/shard_map/ppermute | solution.py:18
  28.4 5.0 %collective-permute-start.3 = (bf16[4,128,128]{2,1,0:T(8,128)(2,1)S(1)}, bf16[4,128,128]{2,1,0:T(8,128)(2,1)S(1)}, u32[]{:S(2)}, u32[]{:S(2)}) collective-permute-start(bf16[4,128,128]{2,1,0:T(8,128)(2,1)S(1)} %join.4.mine_ref), channel_id=1, source_target_pairs={{0,4},{1,5},{2,6},{3,7},{4,0},{5,1},{6,2},{7,3},{8,12},{9,13},{10,... | collective-permute-start | bytes 393224 | tf_op jit(solution)/shard_map/ppermute | solution.py:18
  34.2 12.6 %collective-permute-start.5 = (bf16[2,4,128,128]{3,2,1,0:T(8,128)(2,1)S(1)}, bf16[2,4,128,128]{3,2,1,0:T(8,128)(2,1)S(1)}, u32[]{:S(2)}, u32[]{:S(2)}) collective-permute-start(bf16[2,4,128,128]{3,2,1,0:T(8,128)(2,1)S(1)} %pad_maximum_fusion.1), channel_id=1, source_target_pairs={{0,2},{1,3},{2,0},{3,1},{4,6},{5,7},{6,4},{7,5},{8,10},{9,11},{10,... | collective-permute-start | bytes 786440 | tf_op jit(solution)/shard_map/ppermute | solution.py:18
  35.7 11.0 %collective-permute-start.4 = (bf16[4,128,128]{2,1,0:T(8,128)(2,1)S(1)}, bf16[4,128,128]{2,1,0:T(8,128)(2,1)S(1)}, u32[]{:S(2)}, u32[]{:S(2)}) collective-permute-start(bf16[4,128,128]{2,1,0:T(8,128)(2,1)S(1)} %join.5), channel_id=1, source_target_pairs={{0,8},{1,9},{2,10},{3,11},{4,12},{5,13},{6,14},{7,15},{16,24},{17,... | collective-permute-start | bytes 393224 | tf_op jit(solution)/shard_map/ppermute | solution.py:18
  46.9 4.4 %collective-permute-start.6 = (bf16[2,8,128,128]{3,2,1,0:T(8,128)(2,1)S(1)}, bf16[2,8,128,128]{3,2,1,0:T(8,128)(2,1)S(1)}, u32[]{:S(2)}, u32[]{:S(2)}) collective-permute-start(bf16[2,8,128,128]{3,2,1,0:T(8,128)(2,1)S(1)} %pad_maximum_fusion.lower_ref), channel_id=1, source_target_pairs={{0,1},{1,0},{2,3},{3,2},{4,5},{5,4},{6,7},{7,6},{8,9},{9,8},{10,11... | collective-permute-start | bytes 1572872 | tf_op jit(solution)/shard_map/ppermute | solution.py:18
  46.9 4.3 %collective-permute-start.7 = (bf16[4,128,128]{2,1,0:T(8,128)(2,1)S(1)}, bf16[4,128,128]{2,1,0:T(8,128)(2,1)S(1)}, u32[]{:S(2)}, u32[]{:S(2)}) collective-permute-start(bf16[4,128,128]{2,1,0:T(8,128)(2,1)S(1)} %collective-permute-done.4.rest_0_), channel_id=1, source_target_pairs={{0,1},{1,0},{2,3},{3,2},{4,5},{5,4},{6,7},{7,6},{8,9},{9,8},{10,11... | collective-permute-start | bytes 393224 | tf_op jit(solution)/shard_map/ppermute | solution.py:18
  47.4 6.6 %collective-permute-start.8 = (bf16[4,128,128]{2,1,0:T(8,128)(2,1)S(1)}, bf16[4,128,128]{2,1,0:T(8,128)(2,1)S(1)}, u32[]{:S(2)}, u32[]{:S(2)}) collective-permute-start(bf16[4,128,128]{2,1,0:T(8,128)(2,1)S(1)} %collective-permute-done.4.rest_0_), channel_id=1, source_target_pairs={{0,2},{1,3},{2,0},{3,1},{4,6},{5,7},{6,4},{7,5},{8,10},{9,11},{10,... | collective-permute-start | bytes 393224 | tf_op jit(solution)/shard_map/ppermute | solution.py:18
  54.0 2.8 %collective-permute-start.9 = (bf16[4,128,128]{2,1,0:T(8,128)(2,1)S(1)}, bf16[4,128,128]{2,1,0:T(8,128)(2,1)S(1)}, u32[]{:S(2)}, u32[]{:S(2)}) collective-permute-start(bf16[4,128,128]{2,1,0:T(8,128)(2,1)S(1)} %collective-permute-done.8.rest_0_), channel_id=1, source_target_pairs={{0,1},{1,0},{2,3},{3,2},{4,5},{5,4},{6,7},{7,6},{8,9},{9,8},{10,11... | collective-permute-start | bytes 393224 | tf_op jit(solution)/shard_map/ppermute | solution.py:18

commit v5 on v4

--- a/solution.py
+++ b/solution.py
@@ -8,7 +8,8 @@
 from jax.sharding import PartitionSpec as P
 
 LANES = 128
-PAD = 8
+GROUP = 16
+PITCH = 24
 NT = (((1,), (1,)), ((), ()))
 
 
@@ -50,11 +51,11 @@
     return ((place & 7) << 4) | ((place >> 3) & 15)
 
 
-def selection(row_of, place_of):
-    shape = (LANES, LANES)
-    rows = lax.broadcasted_iota(jnp.int32, shape, row_of)
-    places = lax.broadcasted_iota(jnp.int32, shape, place_of)
-    return jnp.where(rows == row_at(places), 1.0, 0.0).astype(jnp.bfloat16)
+def selection(size):
+    rows = lax.broadcasted_iota(jnp.int32, (size, size), 0)
+    places = lax.broadcasted_iota(jnp.int32, (size, size), 1)
+    chosen = rows == (places & -LANES) + row_at(places & (LANES - 1))
+    return jnp.where(chosen, 1.0, 0.0).astype(jnp.bfloat16)
 
 
 def rim_kernel(query_ref, key_ref, value_ref, out_ref, buffer, sems):
@@ -83,7 +84,7 @@
     starts = start_at(docs_ref, doc_count, positions)
     start_ref[...] = starts - first_pos
     starts = jnp.concatenate([starts] * (head_count // 8), axis=0)
-    select = selection(0, 1)
+    select = selection(LANES)
     levels = level_ref[...].reshape(level_count * head_count, row_count)
     for tile in range(row_count // LANES):
         cols = slice(tile * LANES, (tile + 1) * LANES)
@@ -99,44 +100,56 @@
         gain_out_ref[head] = jnp.broadcast_to(gain_ref[head], (LANES, LANES)).T
 
 
+def window_rows(row_count):
+    return (row_count // GROUP + 1) * PITCH
+
+
 def fill_rim(window_ref, rim):
     rim_rows = rim.shape[0]
-    window_ref[0:PAD, :] = jnp.concatenate(
-        [jnp.zeros((PAD - rim_rows, rim.shape[1]), jnp.float32), rim.astype(jnp.float32)], axis=0
+    window_ref[GROUP - 8 : GROUP, :] = jnp.concatenate(
+        [jnp.zeros((8 - rim_rows, rim.shape[1]), jnp.float32), rim.astype(jnp.float32)], axis=0
     )
 
 
 def fill_rows(window_ref, rows, first):
-    window_ref[PAD + first : PAD + first + rows.shape[0], :] = rows.astype(jnp.float32)
-
-
-def convolved(window_ref, taps, tile, distance):
+    rows = rows.astype(jnp.float32)
+    for start in range(0, rows.shape[0], GROUP):
+        place = ((first + start) // GROUP + 1) * PITCH
+        window_ref[place : place + GROUP, :] = rows[start : start + GROUP, :]
+
+
+def convolved(window_ref, taps, inside_ref, tile):
     reach = taps.shape[0] - 1
-    rows = [
-        window_ref[pl.ds(PAD + tile * LANES + i, 8, stride=16), :] for i in range(-reach, 16)
-    ]
-    summed = taps[0:1, :] * jnp.concatenate(rows[reach:], axis=0)
-    for offset in range(1, reach + 1):
+    base = (tile * (LANES // GROUP) + 1) * PITCH
+    places = [base - PITCH + GROUP + i for i in range(-reach, 0)]
+    places += [base + i for i in range(GROUP)]
+    rows = [window_ref[pl.ds(place, 8, stride=PITCH), :] for place in places]
+    summed = None
+    for offset in range(reach, -1, -1):
         term = taps[offset : offset + 1, :] * jnp.concatenate(
             rows[reach - offset : reach - offset + 16], axis=0
         )
-        if distance is not None:
-            term = jnp.where(distance >= offset, term, 0.0)
-        summed = summed + term
+        summed = term if summed is None else term + summed
+        if offset:
+            first = (reach - offset) * 8
+            summed = summed * inside_ref[tile, first : first + LANES, :]
     return summed
 
 
-def per_tile(flag_ref, tiles, body):
-    for tile in tiles:
-        flagged = flag_ref[tile] == 1
-
-        @pl.when(flagged)
-        def _():
-            body(tile, True)
-
-        @pl.when(jnp.logical_not(flagged))
-        def _():
-            body(tile, False)
+def inside_masks(docs_ref, doc_count, first_pos, inside_ref):
+    tiles, places, _ = inside_ref.shape
+    ahead = (places - LANES) // 8
+    place = lax.broadcasted_iota(jnp.int32, (places, LANES), 0)
+    rows = ((place & 7) << 4) + (place >> 3) - ahead
+    for tile in range(tiles):
+        positions = rows + (first_pos + tile * LANES)
+
+        def step(i, inside):
+            return jnp.where(positions == docs_ref[i], 0.0, inside)
+
+        inside_ref[tile] = lax.fori_loop(
+            0, doc_count, step, jnp.ones((places, LANES), jnp.float32), unroll=8
+        )
 
 
 def columns(first):
@@ -144,18 +157,17 @@
 
 
 def key_value_tile(
-    rim_ref, taps_ref, distance_ref, key_out_ref, value_out_ref, window_ref, head, slot, tile, masked
+    taps_ref, inside_ref, key_out_ref, value_out_ref, window_ref, head, slot, tile
 ):
     width = taps_ref.shape[1] // 3
     places = slice(tile * LANES, (tile + 1) * LANES)
-    distance = distance_ref[places, :] if masked else None
     first = head * LANES
     key_taps = taps_ref[:, columns(width + first)]
     value_taps = taps_ref[:, columns(2 * width + first)]
-    grown = silu(convolved(window_ref.at[slot], key_taps, tile, distance))
+    grown = silu(convolved(window_ref.at[slot], key_taps, inside_ref, tile))
     square = jnp.sum(grown * grown, axis=1, keepdims=True)
     key_out_ref[head, places, :] = (grown * lax.rsqrt(square + 1e-6)).astype(jnp.bfloat16)
-    values = silu(convolved(window_ref.at[slot + 1], value_taps, tile, distance))
+    values = silu(convolved(window_ref.at[slot + 1], value_taps, inside_ref, tile))
     value_out_ref[head, :, places] = values.T.astype(jnp.bfloat16)
 
 
@@ -175,8 +187,7 @@
     key_out_ref,
     value_out_ref,
     state_ref,
-    distance_ref,
-    flag_ref,
+    inside_ref,
     window_ref,
     *,
     doc_count,
@@ -187,61 +198,55 @@
     tiles = list(range(1, row_count // LANES))
     first_pos = lax.axis_index("seq") * row_count
     keep = kept_lanes(docs_ref, doc_count, first_pos, row_count, tiles)
-    places = lax.broadcasted_iota(jnp.int32, (row_count, LANES), 0)
-    positions = first_pos + (places & -LANES) + row_at(places & (LANES - 1))
-    distance_ref[...] = positions - start_at(docs_ref, doc_count, positions)
-    for tile in range(row_count // LANES):
-        tile_first = first_pos + tile * LANES
-
-        def step(i, flag):
-            gap = docs_ref[i] - tile_first
-            return jnp.where((gap > -8) & (gap < LANES), 1, flag)
-
-        flag_ref[tile] = lax.fori_loop(0, doc_count, step, jnp.int32(0))
+    inside_masks(docs_ref, doc_count, first_pos, inside_ref)
     ahead = LANES - 16
 
-    def group(step, carry):
+    def add_state(head):
+        state_ref[head] = jnp.dot(
+            value_out_ref[head, :, LANES:] * keep,
+            key_out_ref[head, LANES:, :],
+            preferred_element_type=jnp.float32,
+        )
+
+    def group(step):
         for which in range(heads):
             cols = columns((step * heads + which) * LANES)
             fill_rows(window_ref.at[2 * which], key_ref[ahead:, cols], ahead)
             fill_rows(window_ref.at[2 * which + 1], value_ref[ahead:, cols], ahead)
-
-        def body(tile, masked):
+        for tile in tiles:
             for which in range(heads):
                 key_value_tile(
-                    None,
                     taps_ref,
-                    distance_ref,
+                    inside_ref,
                     key_out_ref,
                     value_out_ref,
                     window_ref,
                     step * heads + which,
                     2 * which,
                     tile,
-                    masked,
                 )
 
-        per_tile(flag_ref, tiles, body)
+    group(0)
+
+    def body(step, carry):
         for which in range(heads):
-            head = step * heads + which
-            state_ref[head] = jnp.dot(
-                value_out_ref[head, :, LANES:] * keep,
-                key_out_ref[head, LANES:, :],
-                preferred_element_type=jnp.float32,
-            )
+            add_state((step - 1) * heads + which)
+        group(step)
         return carry
 
-    lax.fori_loop(0, head_count // heads, group, 0)
+    steps = head_count // heads
+    lax.fori_loop(1, steps, body, 0)
+    for which in range(heads):
+        add_state((steps - 1) * heads + which)
 
 
 def first_rows_kernel(
     docs_ref,
-    flag_ref,
     key_ref,
     value_ref,
     taps_ref,
     rim_ref,
-    distance_ref,
+    inside_ref,
     later_state_ref,
     key_in_ref,
     value_in_ref,
@@ -259,42 +264,46 @@
     index = lax.axis_index("seq")
     keep = kept_lanes(docs_ref, doc_count, index * row_count, row_count, [0])
 
-    def group(step, carry):
+    def add_state(head):
+        total = later_state_ref[head] + jnp.dot(
+            value_out_ref[head, :, 0:LANES] * keep,
+            key_out_ref[head, 0:LANES, :],
+            preferred_element_type=jnp.float32,
+        )
+        place = logical_place(head, index & 1, (index >> 1) & 1)
+        state_ref[place] = total.astype(jnp.bfloat16)
+
+    def group(step):
         for which in range(heads):
             first = (step * heads + which) * LANES
             fill_rim(window_ref.at[2 * which], rim_ref[:, columns(width + first)])
             fill_rim(window_ref.at[2 * which + 1], rim_ref[:, columns(2 * width + first)])
             fill_rows(window_ref.at[2 * which], key_ref[0:LANES, columns(first)], 0)
             fill_rows(window_ref.at[2 * which + 1], value_ref[0:LANES, columns(first)], 0)
-
-        def body(tile, masked):
-            for which in range(heads):
-                key_value_tile(
-                    rim_ref,
-                    taps_ref,
-                    distance_ref,
-                    key_out_ref,
-                    value_out_ref,
-                    window_ref,
-                    step * heads + which,
-                    2 * which,
-                    tile,
-                    masked,
-                )
-
-        per_tile(flag_ref, [0], body)
         for which in range(heads):
-            head = step * heads + which
-            total = later_state_ref[head] + jnp.dot(
-                value_out_ref[head, :, 0:LANES] * keep,
-                key_out_ref[head, 0:LANES, :],
-                preferred_element_type=jnp.float32,
+            key_value_tile(
+                taps_ref,
+                inside_ref,
+                key_out_ref,
+                value_out_ref,
+                window_ref,
+                step * heads + which,
+                2 * which,
+                0,
             )
-            place = logical_place(head, index & 1, (index >> 1) & 1)
-            state_ref[place] = total.astype(jnp.bfloat16)
+
+    group(0)
+
+    def body(step, carry):
+        for which in range(heads):
+            add_state((step - 1) * heads + which)
+        group(step)
         return carry
 
-    lax.fori_loop(0, head_count // heads, group, 0)
+    steps = head_count // heads
+    lax.fori_loop(1, steps, body, 0)
+    for which in range(heads):
+        add_state((steps - 1) * heads + which)
 
 
 def join_kernel(docs_ref, mine_ref, theirs_ref, *out_refs, doc_count, row_count, bit, parts):
@@ -319,11 +328,11 @@
 
 
 def near_kernel(
-    flag_ref,
+    docs_ref,
     query_ref,
     rim_ref,
     taps_ref,
-    distance_ref,
+    inside_ref,
     table_ref,
     start_ref,
     key_ref,
@@ -355,16 +364,14 @@
             fill_rim(window_ref.at[which], rim_ref[:, columns(head * LANES)])
             fill_rows(window_ref.at[which], query_ref[:, columns(head * LANES)], 0)
 
-        def body(tile, masked):
-            places = slice(tile * LANES, (tile + 1) * LANES)
-            distance = distance_ref[places, :] if masked else None
-            for which in range(heads):
-                head = first_head + step * heads + which
-                taps = taps_ref[:, columns(head * LANES)]
-                grown = silu(convolved(window_ref.at[which], taps, tile, distance))
-                query_out_ref[head, places, :] = grown.astype(jnp.bfloat16)
-
-        per_tile(flag_ref, range(tiles), body)
+        for which in range(heads):
+            head = first_head + step * heads + which
+            taps = taps_ref[:, columns(head * LANES)]
+            for tile in range(tiles):
+                grown = silu(convolved(window_ref.at[which], taps, inside_ref, tile))
+                query_out_ref[head, tile * LANES : (tile + 1) * LANES, :] = grown.astype(
+                    jnp.bfloat16
+                )
 
         for which in range(heads):
             head = first_head + step * heads + which
@@ -440,66 +447,81 @@
     gain_ref,
     first_state_ref,
     lower_ref,
+    last_ref,
     *rest,
-    groups,
+    group,
+    previous,
+    writes_own,
     dev_bits,
-    heads,
-    skipped,
 ):
-    last_refs = rest[: len(groups)]
-    out_hbm_ref, out_buffer, sems = rest[len(groups) + skipped :]
     head_count, row_count, _ = query_ref.shape
-    tiles = row_count // LANES
     quarter = head_count // 4
+    wide = quarter * LANES
+    span = 2 * LANES
     index = lax.axis_index("seq")
     core_bit = index & 1
     y_bit = (index >> 1) & 1
     tok_bits = row_count.bit_length() - 1
-    select = selection(0, 1)
-    copies = []
-    for group, (last_ref, (other_half, other_quarter)) in enumerate(zip(last_refs, groups)):
-        first_head = (core_bit ^ other_half) * 2 * quarter + (y_bit ^ other_quarter) * quarter
-
-        def body(step, carry):
-            for which in range(heads):
-                local_head = step * heads + which
-                head = first_head + local_head
-                first_place = logical_place(head, 1 - core_bit, y_bit)
-                place = logical_place(head, core_bit, y_bit) & 7
-                states = [first_state_ref[first_place]]
-                for level in range(dev_bits - 2):
-                    states.append(lower_ref[level, place])
-                states.append(last_ref[local_head])
-                images = lax.dot_general(
-                    jnp.concatenate(states, axis=0),
-                    query_ref[head],
-                    NT,
-                    preferred_element_type=jnp.float32,
+
+    def first_head_of(group):
+        other_half, other_quarter = group
+        return (core_bit ^ other_half) * 2 * quarter + (y_bit ^ other_quarter) * quarter
+
+    def copy_out(result_ref, group, sem):
+        cols = pl.ds(pl.multiple_of(first_head_of(group) * LANES, wide), wide)
+        return pltpu.make_async_copy(result_ref, out_hbm_ref.at[:, cols], sem)
+
+    rest = list(rest)
+    previous_ref = rest.pop(0) if previous else None
+    sems = rest.pop() if previous or writes_own else None
+    result_ref = rest.pop()
+    out_hbm_ref = rest.pop() if previous or writes_own else None
+    copies = [copy_out(previous_ref, previous, sems.at[0])] if previous else []
+    for copy in copies:
+        copy.start()
+
+    first_head = first_head_of(group)
+    select = selection(span)
+    finished = []
+    for local_head in range(quarter):
+        head = first_head + local_head
+        first_place = logical_place(head, 1 - core_bit, y_bit)
+        place = logical_place(head, core_bit, y_bit) & 7
+        states = [first_state_ref[first_place]]
+        for level in range(dev_bits - 2):
+            states.append(lower_ref[level, place])
+        states.append(last_ref[local_head])
+        images = lax.dot_general(
+            jnp.concatenate(states, axis=0),
+            query_ref[head],
+            NT,
+            preferred_element_type=jnp.float32,
+        )
+        summed = near_ref[head]
+        for bit in range(dev_bits):
+            coef = table_ref[tok_bits + 1 + bit, pl.ds(head, 1), :]
+            summed = summed + coef * images[bit * LANES : (bit + 1) * LANES, :]
+        mean = jnp.mean(summed * summed, axis=0, keepdims=True)
+        normed = summed * lax.rsqrt(mean + 1e-6)
+        gain = jnp.concatenate([gain_ref[head]] * (row_count // LANES), axis=1)
+        finished.append((normed * gain).astype(jnp.bfloat16))
+        if local_head % 2 == 1:
+            both = jnp.concatenate(finished[-2:], axis=0)
+            cols = slice((local_head - 1) * LANES, (local_head + 1) * LANES)
+            for first in range(0, row_count, span):
+                turned = lax.dot_general(
+                    select, both[:, first : first + span], NT, preferred_element_type=jnp.float32
                 )
-                summed = near_ref[head]
-                for bit in range(dev_bits):
-                    coef = table_ref[tok_bits + 1 + bit, pl.ds(head, 1), :]
-                    summed = summed + coef * images[bit * LANES : (bit + 1) * LANES, :]
-                mean = jnp.mean(summed * summed, axis=0, keepdims=True)
-                normed = summed * lax.rsqrt(mean + 1e-6)
-                gain = gain_ref[head]
-                for tile in range(tiles):
-                    cols = slice(tile * LANES, (tile + 1) * LANES)
-                    done = (normed[:, cols] * gain).astype(jnp.bfloat16)
-                    turned = lax.dot_general(select, done, NT, preferred_element_type=jnp.float32)
-                    out_buffer[group, cols, columns(local_head * LANES)] = turned.astype(
-                        jnp.bfloat16
-                    )
-            return carry
-
-        lax.fori_loop(0, quarter // heads, body, 0)
-        wide = quarter * LANES
-        cols = pl.ds(pl.multiple_of(first_head * LANES, wide), wide)
-        copy = pltpu.make_async_copy(out_buffer.at[group], out_hbm_ref.at[:, cols], sems.at[group])
-        copy.start()
-        copies.append(copy)
+                result_ref[first : first + span, cols] = turned.astype(jnp.bfloat16)
+    if writes_own:
+        copies.append(copy_out(result_ref, group, sems.at[1]))
+        copies[-1].start()
     for copy in copies:
         copy.wait()
+
+
+def far_skip(*refs, **settings):
+    far_kernel(*refs[:8], *refs[9:], **settings)
 
 
 def local(query_in, key_in, value_in, conv_weight, level_weight, out_gain, doc_starts):
@@ -531,44 +553,43 @@
     )(*(pltpu.with_memory_space_constraint(x, pltpu.HBM) for x in (query_in, key_in, value_in)))
     tails, docs = lax.optimization_barrier((tails, doc_starts))
     rims = exchange(tails, lambda i: i + 1 if i + 1 < dev_count else None)
-    heads = 2
-    keys, values_t, later_state, distance, flags = pl.pallas_call(
+    heads = 4
+    keys, values_t, later_state, inside = pl.pallas_call(
         functools.partial(later_rows_kernel, doc_count=doc_count, heads=heads),
         in_specs=[smem] + [vmem] * 3,
-        out_specs=[vmem] * 4 + [smem],
+        out_specs=[vmem] * 4,
         out_shape=[
             pltpu.VMEM((head_count, row_count, head_size), jnp.bfloat16),
             pltpu.VMEM((head_count, head_size, row_count), jnp.bfloat16),
             pltpu.VMEM((head_count, head_size, head_size), jnp.float32),
-            pltpu.VMEM((row_count, LANES), jnp.int32),
-            pltpu.SMEM((tiles,), jnp.int32),
+            pltpu.VMEM((tiles, LANES + 8 * (rim_rows - 1), LANES), jnp.float32),
         ],
-        scratch_shapes=[pltpu.VMEM((2 * heads, row_count + PAD, LANES), jnp.float32)],
-        compiler_params=limited(3),
+        scratch_shapes=[pltpu.VMEM((2 * heads, window_rows(row_count), LANES), jnp.float32)],
+        compiler_params=limited(6),
         cost_estimate=pl.CostEstimate(
             flops=500_000_000, bytes_accessed=4_000_000, transcendentals=1_500_000
         ),
         name="later_rows",
     )(docs, key_in, value_in, conv_weight)
-    rims, keys, values_t, later_state, flags = lax.optimization_barrier(
-        (rims, keys, values_t, later_state, flags)
+    rims, keys, values_t, later_state = lax.optimization_barrier(
+        (rims, keys, values_t, later_state)
     )
     keys, values_t, state = pl.pallas_call(
         functools.partial(
             first_rows_kernel, doc_count=doc_count, row_count=row_count, heads=heads
         ),
-        in_specs=[smem, smem] + [vmem] * 8,
+        in_specs=[smem] + [vmem] * 8,
         out_specs=[vmem] * 3,
         out_shape=[
             pltpu.VMEM((head_count, row_count, head_size), jnp.bfloat16),
             pltpu.VMEM((head_count, head_size, row_count), jnp.bfloat16),
             pltpu.VMEM((head_count, head_size, head_size), jnp.bfloat16),
         ],
-        scratch_shapes=[pltpu.VMEM((2 * heads, LANES + PAD, LANES), jnp.float32)],
-        input_output_aliases={8: 0, 9: 1},
-        compiler_params=limited(2),
+        scratch_shapes=[pltpu.VMEM((2 * heads, window_rows(LANES), LANES), jnp.float32)],
+        input_output_aliases={7: 0, 8: 1},
+        compiler_params=limited(4),
         name="first_rows",
-    )(docs, flags, key_in, value_in, conv_weight, rims, distance, later_state, keys, values_t)
+    )(docs, key_in, value_in, conv_weight, rims, inside, later_state, keys, values_t)
 
     def joined(mine, theirs, bit, parts=1):
         count = mine.shape[0] // (2 if parts == 2 else 1)
@@ -584,7 +605,7 @@
             name="join",
         )(doc_starts, mine, theirs)
 
-    def near_piece(first_head, piece_heads, buffers, flags):
+    def near_piece(first_head, piece_heads, buffers, docs):
         extra = [] if buffers is None else list(buffers)
         return pl.pallas_call(
             functools.partial(
@@ -601,38 +622,43 @@
                 pltpu.VMEM((head_count, head_size, row_count), jnp.float32),
             ],
             scratch_shapes=[
-                pltpu.VMEM((heads, row_count + PAD, LANES), jnp.float32),
+                pltpu.VMEM((heads, window_rows(row_count), LANES), jnp.float32),
                 pltpu.VMEM((heads, tiles, 16, LANES), jnp.float32),
                 pltpu.VMEM((heads, row_count, row_count), jnp.bfloat16),
             ],
             input_output_aliases={9: 0, 10: 1} if extra else {},
             compiler_params=limited(6),
             cost_estimate=pl.CostEstimate(
-                flops=1_000_000, bytes_accessed=10_000, transcendentals=0
+                flops=5_000_000_000, bytes_accessed=35_000_000, transcendentals=300_000
             ),
             name="near",
-        )(flags, query_in, rims, conv_weight, distance, table, starts, keys, values_t, *extra)
-
-    def far_piece(groups, lower, last_states, out):
-        extra = [] if out is None else [out]
+        )(docs, query_in, rims, conv_weight, inside, table, starts, keys, values_t, *extra)
+
+    def far_piece(group, lower, last_state, previous=None, before=None, out=None, writes_own=False):
+        writes = previous or writes_own
+        extra = ([before] if previous else []) + ([] if out is None else [out])
+        out_type = jax.ShapeDtypeStruct((row_count, width_all), jnp.bfloat16)
+        result_type = pltpu.VMEM((row_count, width_all // 4), jnp.bfloat16)
         return pl.pallas_call(
             functools.partial(
-                far_kernel, groups=groups, dev_bits=dev_bits, heads=heads, skipped=len(extra)
+                far_skip if out is not None else far_kernel,
+                group=group,
+                previous=previous,
+                writes_own=writes_own,
+                dev_bits=dev_bits,
             ),
-            in_specs=[vmem] * (6 + len(groups)) + [anywhere] * len(extra),
-            out_specs=anywhere,
-            out_shape=jax.ShapeDtypeStruct((row_count, width_all), jnp.bfloat16),
-            scratch_shapes=[
-                pltpu.VMEM((len(groups), row_count, quarter * head_size), jnp.bfloat16),
-                pltpu.SemaphoreType.DMA((len(groups),)),
-            ],
-            input_output_aliases={6 + len(groups): 0} if extra else {},
+            in_specs=[vmem] * (8 if previous else 7) + ([] if out is None else [anywhere]),
+            out_specs=([anywhere] if writes else []) + ([] if writes_own else [vmem]),
+            out_shape=([out_type] if writes else []) + ([] if writes_own else [result_type]),
+            scratch_shapes=([result_type] if writes_own else [])
+            + ([pltpu.SemaphoreType.DMA((2,))] if writes else []),
+            input_output_aliases={} if out is None else {8: 0},
             compiler_params=limited(4),
             cost_estimate=pl.CostEstimate(
                 flops=1_000_000, bytes_accessed=10_000, transcendentals=0
             ),
             name="far",
-        )(queries, near, table, gains, first_state, lower, *last_states, *extra)
+        )(queries, near, table, gains, first_state, lower, last_state, *extra)
 
     quarter = head_count // 4
     state, docs = lax.optimization_barrier((state, docs))
@@ -654,7 +680,7 @@
     )
     pair_kept, pair_sent = joined(state, first_state, 0, parts=2)
 
-    pair_sent, tied = lax.optimization_barrier((pair_sent, flags))
+    pair_sent, tied = lax.optimization_barrier((pair_sent, docs))
     pair_in = swapped(pair_sent, 1)
     buffers = near_piece(0, quarter, None, tied)
     pair_in, buffers = lax.optimization_barrier((pair_in, buffers))
@@ -663,7 +689,7 @@
     received = []
     for bit in range(2, dev_bits - 1):
         if bit == 2:
-            carried, tied = lax.optimization_barrier((carried, flags))
+            carried, tied = lax.optimization_barrier((carried, docs))
         arrived = swapped(carried, bit)
         if bit == 2:
             buffers = near_piece(quarter, quarter, buffers, tied)
@@ -672,7 +698,7 @@
         (carried,) = joined(carried, arrived, bit)
 
     mine = jnp.stack([pair_kept] + received)
-    carried, mine, tied = lax.optimization_barrier((carried, mine, flags))
+    carried, mine, tied = lax.optimization_barrier((carried, mine, docs))
     last_own = sent_up(carried, dev_bits - 1)
     theirs = swapped(mine, 1)
     buffers = near_piece(2 * quarter, 2 * quarter, buffers, tied)
@@ -684,14 +710,15 @@
     last_next = swapped(last_own, 1)
     other = swapped(own, 0)
     last_other = swapped(last_own, 0)
-    out = far_piece(((0, 0),), own, (last_own,), None)
-    other, last_other, out = lax.optimization_barrier((other, last_other, out))
-    out = far_piece(((1, 0),), other, (last_other,), out)
+    (done,) = far_piece((0, 0), own, last_own)
+    other, last_other, done = lax.optimization_barrier((other, last_other, done))
+    (out,) = far_piece((1, 0), other, last_other, (0, 0), done, writes_own=True)
     last_next, out = lax.optimization_barrier((last_next, out))
     last_far = swapped(last_next, 0)
-    out = far_piece(((0, 1),), own, (last_next,), out)
-    last_far, out = lax.optimization_barrier((last_far, out))
-    return far_piece(((1, 1),), other, (last_far,), out)
+    (done,) = far_piece((0, 1), own, last_next)
+    last_far, out, done = lax.optimization_barrier((last_far, out, done))
+    (out,) = far_piece((1, 1), other, last_far, (0, 1), done, out, writes_own=True)
+    return out
 
 
 def solution(mesh):

time: 59.3 us -> 51.2 us (0.86)
  Pallas kernels: 42 us -> 30.3 us
  waiting for transfers between devices: 1.69 us -> 3.67 us
  starting transfers between devices: 15.4 us -> 16.5 us
    pallas_call x4, Pallas kernels: 10.7 us -> 6.52 us  [far_piece(): pl.pallas_call(functools.partial(far_skip if out is not None else far_ker...]
    pallas_call x1, Pallas kernels: 9.67 us -> 6.32 us  [local(): pl.pallas_call(functools.partial(later_rows_kernel, doc_count=doc_count,...]
    pallas_call x3, Pallas kernels: 13.1 us -> 10.7 us  [near_piece(): pl.pallas_call(functools.partial(near_kernel, first_head=first_head, head...]
    ppermute x10, waiting for transfers between devices: 1.69 us -> 3.67 us  [exchange(): return lax.ppermute(block, 'seq', route)]
    pallas_call x1, Pallas kernels: 4.46 us -> 2.67 us  [local(): pl.pallas_call(functools.partial(first_rows_kernel, doc_count=doc_count,...]
    ppermute x10, starting transfers between devices: 15.4 us -> 16.5 us  [exchange(): return lax.ppermute(block, 'seq', route)]
  transfers between devices with their start and end apart: 10 -> 10, of which waited for: 3 -> 5; matrix products, arithmetic and copies ran while one was open for 0% -> 0% of each run, Pallas kernels for 53% -> 44%
where the time goes in v5:
time: 51.2 us; the launch traced here: 51 us
  Pallas kernels  30.3 us (59%)
  starting transfers between devices  16.5 us (32%)
  waiting for transfers between devices  3.67 us (7%)
    ppermute x10, starting transfers between devices, exchange(): return lax.ppermute(block, 'seq', route)  16.5 us
    pallas_call x3, Pallas kernels, near_piece(): pl.pallas_call(functools.partial(near_kernel, first_head=first_head, head...  10.7 us
    pallas_call x4, Pallas kernels, far_piece(): pl.pallas_call(functools.partial(far_skip if out is not None else far_ker...  6.52 us
    pallas_call x1, Pallas kernels, local(): pl.pallas_call(functools.partial(later_rows_kernel, doc_count=doc_count,...  6.32 us
    ppermute x10, waiting for transfers between devices, exchange(): return lax.ppermute(block, 'seq', route)  3.67 us
    pallas_call x1, Pallas kernels, local(): pl.pallas_call(functools.partial(first_rows_kernel, doc_count=doc_count,...  2.67 us
    pallas_call x3, Pallas kernels, joined(): pl.pallas_call(functools.partial(join_kernel, doc_count=doc_count, row_co...  2.04 us
    pallas_call x1, Pallas kernels, local(): pl.pallas_call(rim_kernel, in_specs=[pl.BlockSpec(memory_space=pltpu.HBM)...  1.09 us
  transfers between devices with their start and end apart: 10, of which 5 were waited for; matrix products, arithmetic and copies ran while one was open for 0% of the time, Pallas kernels for 44%

profile of v5, /device:TPU:0, one launch (start us, length us, event | category | flops | bytes accessed | tf_op | source)
XLA Modules:
  0.0 51.0 jit_solution(12687627862786397309)
XLA Ops:
  0.0 1.1 %rim.1 = bf16[3,6144]{1,0:T(4,128)(2,1)S(1)} custom-call(bf16[512,2048]{1,0:T(8,128)(2,1)} %query_ref.7, bf16[512,2048]{1,0:T(8,128)(2,1)} %key_ref.5, bf16[512,2048]{1,0:T(8,128)(2,1)} %value_ref.5), custom_call_target="tpu_custom_call" | custom-call | tf_op jit(solution)/shard_map/rim/pallas_call | solution.py:542
  1.1 2.5 %collective-permute-start = (bf16[3,6144]{1,0:T(4,128)(2,1)S(1)}, bf16[3,6144]{1,0:T(4,128)(2,1)S(1)}, u32[]{:S(2)}, u32[]{:S(2)}) collective-permute-start(bf16[3,6144]{1,0:T(4,128)(2,1)S(1)} %rim.1), channel_id=1, source_target_pairs={{0,1},{1,2},{2,3},{3,4},{4,5},{5,6},{6,7},{7,8},{8,9},{9,10},{10,1... | collective-permute-start | bytes 110600 | tf_op jit(solution)/shard_map/ppermute | solution.py:19
  3.7 6.3 %later_rows.1 = (bf16[16,512,128]{2,1,0:T(8,128)(2,1)S(1)}, bf16[16,128,512]{2,1,0:T(8,128)(2,1)S(1)}, f32[16,128,128]{2,1,0:T(8,128)S(1)}, f32[4,144,128]{2,1,0:T(8,128)S(1)}) custom-call(s32[8]{0:T(128)S(1)} %copy-done.5, bf16[512,2048]{1,0:T(8,128)(2,1)S(1)} %copy-done, bf16[512,2048]{1,0:T(8,128)(2,1)S(1)} %copy-done.1, f32[4,6144]{1,0:T(4,128)S(1)} %copy-done.3), custom_call_target="tpu_custom_call" | custom-call | flops 500000000 | bytes 4000000 | tf_op jit(solution)/shard_map/later_rows/pallas_call | solution.py:557
  10.0 0.0 copy-start.4
  10.0 0.0 copy-start.6
  10.0 0.0 copy-start.2
  10.0 2.7 %first_rows.1 = (bf16[16,512,128]{2,1,0:T(8,128)(2,1)S(1)}, bf16[16,128,512]{2,1,0:T(8,128)(2,1)S(1)}, bf16[16,128,128]{2,1,0:T(8,128)(2,1)S(1)}) custom-call(s32[8]{0:T(128)S(1)} %copy-done.5, bf16[512,2048]{1,0:T(8,128)(2,1)S(1)} %copy-done, bf16[512,2048]{1,0:T(8,128)(2,1)S(1)} %copy-done.1, ...), custom_call_target="tpu_custom_call", output_to_operand_aliasing={{0}: (7, {}), {1}: (8, {})} | custom-call | tf_op jit(solution)/shard_map/first_rows/pallas_call | solution.py:577
  12.7 2.7 %collective-permute-start.1 = (bf16[16,128,128]{2,1,0:T(8,128)(2,1)S(1)}, bf16[16,128,128]{2,1,0:T(8,128)(2,1)S(1)}, u32[]{:S(2)}, u32[]{:S(2)}) collective-permute-start(bf16[16,128,128]{2,1,0:T(8,128)(2,1)S(1)} %get-tuple-element.73.mine_ref), channel_id=1, source_target_pairs={{0,1},{1,0},{2,3},{3,2},{4,5},{5,4},{6,7},{7,6},{8,9},{9,8},{10,11... | collective-permute-start | bytes 1572872 | tf_op jit(solution)/shard_map/ppermute | solution.py:19
  15.4 0.9 %tables.1 = (f32[14,16,512]{2,1,0:T(8,128)S(1)}, s32[8,512]{1,0:T(8,128)S(1)}, f32[16,128,128]{2,1,0:T(8,128)S(1)}) custom-call(s32[8]{0:T(128)S(1)} %copy-done.5, bf16[14,16,512]{2,1,0:T(8,128)(2,1)S(1)} %bitcast.9, f32[16,1,128]{2,1,0:T(1,128)S(1)} %bitcast.10), custom_call_target="tpu_custom_call" | custom-call | tf_op jit(solution)/shard_map/tables/pallas_call | solution.py:666
  16.4 0.6 %collective-permute-done.1.theirs_ref.first_state_ref.refs_4_ = bf16[16,128,128]{2,1,0:T(8,128)(2,1)S(1)} collective-permute-done((bf16[16,128,128]{2,1,0:T(8,128)(2,1)S(1)}, bf16[16,128,128]{2,1,0:T(8,128)(2,1)S(1)}, u32[]{:S(2)}, u32[]{:S(2)}) %collective-permute-start.1) | collective-permute-done | bytes 524320 | tf_op jit(solution)/shard_map/ppermute | solution.py:19
  16.9 0.7 %join.3 = (bf16[4,128,128]{2,1,0:T(8,128)(2,1)S(1)}, bf16[4,128,128]{2,1,0:T(8,128)(2,1)S(1)}) custom-call(s32[8]{0:T(128)S(1)} %copy-done.5, bf16[16,128,128]{2,1,0:T(8,128)(2,1)S(1)} %get-tuple-element.73.mine_ref, bf16[16,128,128]{2,1,0:T(8,128)(2,1)S(1)} %collective-permute-done.1.theirs_ref.first_state_ref.refs_4_), custom_call_target="tpu_custom_call" | custom-call | tf_op jit(solution)/shard_map/join/pallas_call | solution.py:597
  17.7 1.6 %collective-permute-start.2 = (bf16[4,128,128]{2,1,0:T(8,128)(2,1)S(1)}, bf16[4,128,128]{2,1,0:T(8,128)(2,1)S(1)}, u32[]{:S(2)}, u32[]{:S(2)}) collective-permute-start(bf16[4,128,128]{2,1,0:T(8,128)(2,1)S(1)} %get-tuple-element.81), channel_id=1, source_target_pairs={{0,2},{1,3},{2,0},{3,1},{4,6},{5,7},{6,4},{7,5},{8,10},{9,11},{10,... | collective-permute-start | bytes 393224 | tf_op jit(solution)/shard_map/ppermute | solution.py:19
  19.3 2.8 %near.3 = (bf16[16,512,128]{2,1,0:T(8,128)(2,1)S(1)}, f32[16,128,512]{2,1,0:T(8,128)S(1)}) custom-call(s32[8]{0:T(128)S(1)} %copy-done.5, bf16[512,2048]{1,0:T(8,128)(2,1)S(1)} %copy-done.2, bf16[3,6144]{1,0:T(4,128)(2,1)S(1)} %collective-permute-done.rim_ref, f32[4,6144]{1,0:T(4,128)S(1)} %copy-done.3, f32[4,144,128]{2,1,0:T(8,128)S(1)} %get-tuple-element.68.inside_ref, ...), custom_call_target="tpu_custom_call" | custom-call | flops 5000000000 | bytes 35000000 | tf_op jit(solution)/shard_map/near/pallas_call | solution.py:610
  22.1 1.4 %collective-permute-done.2.theirs_ref = bf16[4,128,128]{2,1,0:T(8,128)(2,1)S(1)} collective-permute-done((bf16[4,128,128]{2,1,0:T(8,128)(2,1)S(1)}, bf16[4,128,128]{2,1,0:T(8,128)(2,1)S(1)}, u32[]{:S(2)}, u32[]{:S(2)}) %collective-permute-start.2) | collective-permute-done | bytes 131104 | tf_op jit(solution)/shard_map/ppermute | solution.py:19
  23.5 0.7 %join.4.mine_ref = bf16[4,128,128]{2,1,0:T(8,128)(2,1)S(1)} custom-call(s32[8]{0:T(128)S(1)} %copy-done.5, bf16[4,128,128]{2,1,0:T(8,128)(2,1)S(1)} %get-tuple-element.79.mine_ref, bf16[4,128,128]{2,1,0:T(8,128)(2,1)S(1)} %collective-permute-done.2.theirs_ref), custom_call_target="tpu_custom_call" | custom-call | tf_op jit(solution)/shard_map/join/pallas_call | solution.py:597
  24.2 1.6 %collective-permute-start.3 = (bf16[4,128,128]{2,1,0:T(8,128)(2,1)S(1)}, bf16[4,128,128]{2,1,0:T(8,128)(2,1)S(1)}, u32[]{:S(2)}, u32[]{:S(2)}) collective-permute-start(bf16[4,128,128]{2,1,0:T(8,128)(2,1)S(1)} %join.4.mine_ref), channel_id=1, source_target_pairs={{0,4},{1,5},{2,6},{3,7},{4,0},{5,1},{6,2},{7,3},{8,12},{9,13},{10,... | collective-permute-start | bytes 393224 | tf_op jit(solution)/shard_map/ppermute | solution.py:19
  25.8 2.8 %near.4 = (bf16[16,512,128]{2,1,0:T(8,128)(2,1)S(1)}, f32[16,128,512]{2,1,0:T(8,128)S(1)}) custom-call(s32[8]{0:T(128)S(1)} %copy-done.5, bf16[512,2048]{1,0:T(8,128)(2,1)S(1)} %copy-done.2, bf16[3,6144]{1,0:T(4,128)(2,1)S(1)} %collective-permute-done.rim_ref, f32[4,6144]{1,0:T(4,128)S(1)} %copy-done.3, ...), custom_call_target="tpu_custom_call", output_to_operand_aliasing={{0}: (9, {}), {1}: (10, {})} | custom-call | flops 5000000000 | bytes 35000000 | tf_op jit(solution)/shard_map/near/pallas_call | solution.py:610
  28.6 0.6 %collective-permute-done.3.theirs_ref = bf16[4,128,128]{2,1,0:T(8,128)(2,1)S(1)} collective-permute-done((bf16[4,128,128]{2,1,0:T(8,128)(2,1)S(1)}, bf16[4,128,128]{2,1,0:T(8,128)(2,1)S(1)}, u32[]{:S(2)}, u32[]{:S(2)}) %collective-permute-start.3) | collective-permute-done | bytes 131104 | tf_op jit(solution)/shard_map/ppermute | solution.py:19
  29.2 0.7 %join.5 = bf16[4,128,128]{2,1,0:T(8,128)(2,1)S(1)} custom-call(s32[8]{0:T(128)S(1)} %copy-done.5, bf16[4,128,128]{2,1,0:T(8,128)(2,1)S(1)} %join.4.mine_ref, bf16[4,128,128]{2,1,0:T(8,128)(2,1)S(1)} %collective-permute-done.3.theirs_ref), custom_call_target="tpu_custom_call" | custom-call | tf_op jit(solution)/shard_map/join/pallas_call | solution.py:597
  29.9 4.7 %collective-permute-start.4 = (bf16[4,128,128]{2,1,0:T(8,128)(2,1)S(1)}, bf16[4,128,128]{2,1,0:T(8,128)(2,1)S(1)}, u32[]{:S(2)}, u32[]{:S(2)}) collective-permute-start(bf16[4,128,128]{2,1,0:T(8,128)(2,1)S(1)} %join.5), channel_id=1, source_target_pairs={{0,8},{1,9},{2,10},{3,11},{4,12},{5,13},{6,14},{7,15},{16,24},{17,... | collective-permute-start | bytes 393224 | tf_op jit(solution)/shard_map/ppermute | solution.py:19
  34.6 1.6 %collective-permute-start.5 = (bf16[2,4,128,128]{3,2,1,0:T(8,128)(2,1)S(1)}, bf16[2,4,128,128]{3,2,1,0:T(8,128)(2,1)S(1)}, u32[]{:S(2)}, u32[]{:S(2)}) collective-permute-start(bf16[2,4,128,128]{3,2,1,0:T(8,128)(2,1)S(1)} %pad_maximum_fusion.1), channel_id=1, source_target_pairs={{0,2},{1,3},{2,0},{3,1},{4,6},{5,7},{6,4},{7,5},{8,10},{9,11},{10,... | collective-permute-start | bytes 786440 | tf_op jit(solution)/shard_map/ppermute | solution.py:19
  36.2 5.1 %near.5 = (bf16[16,512,128]{2,1,0:T(8,128)(2,1)S(1)}, f32[16,128,512]{2,1,0:T(8,128)S(1)}) custom-call(s32[8]{0:T(128)S(1)} %copy-done.5, bf16[512,2048]{1,0:T(8,128)(2,1)S(1)} %copy-done.2, bf16[3,6144]{1,0:T(4,128)(2,1)S(1)} %collective-permute-done.rim_ref, f32[4,6144]{1,0:T(4,128)S(1)} %copy-done.3, ...), custom_call_target="tpu_custom_call", output_to_operand_aliasing={{0}: (9, {}), {1}: (10, {})} | custom-call | flops 5000000000 | bytes 35000000 | tf_op jit(solution)/shard_map/near/pallas_call | solution.py:610
  41.3 0.1 pad_maximum_fusion.lower_ref
  41.4 0.1 collective-permute-start.6
  41.5 0.5 collective-permute-start.7
  42.0 1.2 %collective-permute-start.8 = (bf16[4,128,128]{2,1,0:T(8,128)(2,1)S(1)}, bf16[4,128,128]{2,1,0:T(8,128)(2,1)S(1)}, u32[]{:S(2)}, u32[]{:S(2)}) collective-permute-start(bf16[4,128,128]{2,1,0:T(8,128)(2,1)S(1)} %collective-permute-done.4.last_ref), channel_id=1, source_target_pairs={{0,2},{1,3},{2,0},{3,1},{4,6},{5,7},{6,4},{7,5},{8,10},{9,11},{10,... | collective-permute-start | bytes 393224 | tf_op jit(solution)/shard_map/ppermute | solution.py:19
  43.2 1.2 %far.4.rest_0_ = bf16[512,512]{1,0:T(8,128)(2,1)S(1)} custom-call(bf16[16,512,128]{2,1,0:T(8,128)(2,1)S(1)} %get-tuple-element.104.query_ref.refs_0_, f32[16,128,512]{2,1,0:T(8,128)S(1)} %get-tuple-element.105.near_ref.refs_1_, f32[14,16,512]{2,1,0:T(8,128)S(1)} %get-tuple-element.83.table_ref.refs_2_, ...), custom_call_target="tpu_custom_call" | custom-call | flops 1000000 | bytes 10000 | tf_op jit(solution)/shard_map/far/pallas_call | solution.py:642
  44.4 2.0 %far.5.refs_8_ = bf16[512,2048]{1,0:T(8,128)(2,1)} custom-call(bf16[16,512,128]{2,1,0:T(8,128)(2,1)S(1)} %get-tuple-element.104.query_ref.refs_0_, f32[16,128,512]{2,1,0:T(8,128)S(1)} %get-tuple-element.105.near_ref.refs_1_, f32[14,16,512]{2,1,0:T(8,128)S(1)} %get-tuple-element.83.table_ref.refs_2_, f32[16,128,128]{2,1,0:T(8,128)S(1)} %get-tuple-element.106.gain_ref.refs_3_, ...), custom_call_target="tpu_custom_call" | custom-call | flops 1000000 | bytes 10000 | tf_op jit(solution)/shard_map/far/pallas_call | solution.py:642
  46.5 1.0 %collective-permute-done.8.last_ref = bf16[4,128,128]{2,1,0:T(8,128)(2,1)S(1)} collective-permute-done((bf16[4,128,128]{2,1,0:T(8,128)(2,1)S(1)}, bf16[4,128,128]{2,1,0:T(8,128)(2,1)S(1)}, u32[]{:S(2)}, u32[]{:S(2)}) %collective-permute-start.8) | collective-permute-done | bytes 131104 | tf_op jit(solution)/shard_map/ppermute | solution.py:19
  47.5 1.2 %far.6.refs_7_ = bf16[512,512]{1,0:T(8,128)(2,1)S(1)} custom-call(bf16[16,512,128]{2,1,0:T(8,128)(2,1)S(1)} %get-tuple-element.104.query_ref.refs_0_, f32[16,128,512]{2,1,0:T(8,128)S(1)} %get-tuple-element.105.near_ref.refs_1_, f32[14,16,512]{2,1,0:T(8,128)S(1)} %get-tuple-element.83.table_ref.refs_2_, ...), custom_call_target="tpu_custom_call" | custom-call | flops 1000000 | bytes 10000 | tf_op jit(solution)/shard_map/far/pallas_call | solution.py:642
  48.7 0.1 collective-permute-done.9.refs_6_
  48.8 2.0 %far.7 = bf16[512,2048]{1,0:T(8,128)(2,1)} custom-call(bf16[16,512,128]{2,1,0:T(8,128)(2,1)S(1)} %get-tuple-element.104.query_ref.refs_0_, f32[16,128,512]{2,1,0:T(8,128)S(1)} %get-tuple-element.105.near_ref.refs_1_, f32[14,16,512]{2,1,0:T(8,128)S(1)} %get-tuple-element.83.table_ref.refs_2_, ...), custom_call_target="tpu_custom_call", output_to_operand_aliasing={{}: (8, {})} | custom-call | flops 1000000 | bytes 10000 | tf_op jit(solution)/shard_map/far/pallas_call | solution.py:642
  (18 shorter events, 0.1 us)
Async XLA Ops:
  0.0 3.6 %copy-start.1 = (bf16[512,2048]{1,0:T(8,128)(2,1)S(1)}, bf16[512,2048]{1,0:T(8,128)(2,1)}, u32[]{:S(2)}) copy-start(bf16[512,2048]{1,0:T(8,128)(2,1)} %value_ref.5) | copy-start | bytes 6291460
  0.0 3.6 %copy-start = (bf16[512,2048]{1,0:T(8,128)(2,1)S(1)}, bf16[512,2048]{1,0:T(8,128)(2,1)}, u32[]{:S(2)}) copy-start(bf16[512,2048]{1,0:T(8,128)(2,1)} %key_ref.5) | copy-start | bytes 6291460
  0.0 3.6 %copy-start.5 = (s32[8]{0:T(128)S(1)}, s32[8]{0:T(128)}, u32[]{:S(2)}) copy-start(s32[8]{0:T(128)} %docs_ref.11) | copy-start | bytes 100
  0.0 3.6 %copy-start.3 = (f32[4,6144]{1,0:T(4,128)S(1)}, f32[4,6144]{1,0:T(4,128)}, u32[]{:S(2)}) copy-start(f32[4,6144]{1,0:T(4,128)} %taps_ref.9) | copy-start | bytes 294916
  1.1 8.9 %collective-permute-start = (bf16[3,6144]{1,0:T(4,128)(2,1)S(1)}, bf16[3,6144]{1,0:T(4,128)(2,1)S(1)}, u32[]{:S(2)}, u32[]{:S(2)}) collective-permute-start(bf16[3,6144]{1,0:T(4,128)(2,1)S(1)} %rim.1), channel_id=1, source_target_pairs={{0,1},{1,2},{2,3},{3,4},{4,5},{5,6},{6,7},{7,8},{8,9},{9,10},{10,1... | collective-permute-start | bytes 110600 | tf_op jit(solution)/shard_map/ppermute | solution.py:19
  10.0 5.4 %copy-start.4 = (bf16[16,14,512]{2,0,1:T(8,128)(2,1)S(1)}, bf16[16,14,512]{2,0,1:T(8,128)(2,1)}, u32[]{:S(2)}) copy-start(bf16[16,14,512]{2,0,1:T(8,128)(2,1)} %param.11) | copy-start | bytes 688132
  10.0 5.4 %copy-start.6 = (f32[2048]{0:T(1024)S(1)}, f32[2048]{0:T(1024)}, u32[]{:S(2)}) copy-start(f32[2048]{0:T(1024)} %param.12) | copy-start | bytes 24580
  10.0 9.2 %copy-start.2 = (bf16[512,2048]{1,0:T(8,128)(2,1)S(1)}, bf16[512,2048]{1,0:T(8,128)(2,1)}, u32[]{:S(2)}) copy-start(bf16[512,2048]{1,0:T(8,128)(2,1)} %query_ref.7) | copy-start | bytes 6291460
  12.7 4.2 %collective-permute-start.1 = (bf16[16,128,128]{2,1,0:T(8,128)(2,1)S(1)}, bf16[16,128,128]{2,1,0:T(8,128)(2,1)S(1)}, u32[]{:S(2)}, u32[]{:S(2)}) collective-permute-start(bf16[16,128,128]{2,1,0:T(8,128)(2,1)S(1)} %get-tuple-element.73.mine_ref), channel_id=1, source_target_pairs={{0,1},{1,0},{2,3},{3,2},{4,5},{5,4},{6,7},{7,6},{8,9},{9,8},{10,11... | collective-permute-start | bytes 1572872 | tf_op jit(solution)/shard_map/ppermute | solution.py:19
  17.7 5.8 %collective-permute-start.2 = (bf16[4,128,128]{2,1,0:T(8,128)(2,1)S(1)}, bf16[4,128,128]{2,1,0:T(8,128)(2,1)S(1)}, u32[]{:S(2)}, u32[]{:S(2)}) collective-permute-start(bf16[4,128,128]{2,1,0:T(8,128)(2,1)S(1)} %get-tuple-element.81), channel_id=1, source_target_pairs={{0,2},{1,3},{2,0},{3,1},{4,6},{5,7},{6,4},{7,5},{8,10},{9,11},{10,... | collective-permute-start | bytes 393224 | tf_op jit(solution)/shard_map/ppermute | solution.py:19
  24.2 5.0 %collective-permute-start.3 = (bf16[4,128,128]{2,1,0:T(8,128)(2,1)S(1)}, bf16[4,128,128]{2,1,0:T(8,128)(2,1)S(1)}, u32[]{:S(2)}, u32[]{:S(2)}) collective-permute-start(bf16[4,128,128]{2,1,0:T(8,128)(2,1)S(1)} %join.4.mine_ref), channel_id=1, source_target_pairs={{0,4},{1,5},{2,6},{3,7},{4,0},{5,1},{6,2},{7,3},{8,12},{9,13},{10,... | collective-permute-start | bytes 393224 | tf_op jit(solution)/shard_map/ppermute | solution.py:19
  29.9 11.4 %collective-permute-start.4 = (bf16[4,128,128]{2,1,0:T(8,128)(2,1)S(1)}, bf16[4,128,128]{2,1,0:T(8,128)(2,1)S(1)}, u32[]{:S(2)}, u32[]{:S(2)}) collective-permute-start(bf16[4,128,128]{2,1,0:T(8,128)(2,1)S(1)} %join.5), channel_id=1, source_target_pairs={{0,8},{1,9},{2,10},{3,11},{4,12},{5,13},{6,14},{7,15},{16,24},{17,... | collective-permute-start | bytes 393224 | tf_op jit(solution)/shard_map/ppermute | solution.py:19
  34.6 6.7 %collective-permute-start.5 = (bf16[2,4,128,128]{3,2,1,0:T(8,128)(2,1)S(1)}, bf16[2,4,128,128]{3,2,1,0:T(8,128)(2,1)S(1)}, u32[]{:S(2)}, u32[]{:S(2)}) collective-permute-start(bf16[2,4,128,128]{3,2,1,0:T(8,128)(2,1)S(1)} %pad_maximum_fusion.1), channel_id=1, source_target_pairs={{0,2},{1,3},{2,0},{3,1},{4,6},{5,7},{6,4},{7,5},{8,10},{9,11},{10,... | collective-permute-start | bytes 786440 | tf_op jit(solution)/shard_map/ppermute | solution.py:19
  41.4 3.0 %collective-permute-start.6 = (bf16[2,8,128,128]{3,2,1,0:T(8,128)(2,1)S(1)}, bf16[2,8,128,128]{3,2,1,0:T(8,128)(2,1)S(1)}, u32[]{:S(2)}, u32[]{:S(2)}) collective-permute-start(bf16[2,8,128,128]{3,2,1,0:T(8,128)(2,1)S(1)} %pad_maximum_fusion.lower_ref), channel_id=1, source_target_pairs={{0,1},{1,0},{2,3},{3,2},{4,5},{5,4},{6,7},{7,6},{8,9},{9,8},{10,11... | collective-permute-start | bytes 1572872 | tf_op jit(solution)/shard_map/ppermute | solution.py:19
  41.5 2.9 %collective-permute-start.7 = (bf16[4,128,128]{2,1,0:T(8,128)(2,1)S(1)}, bf16[4,128,128]{2,1,0:T(8,128)(2,1)S(1)}, u32[]{:S(2)}, u32[]{:S(2)}) collective-permute-start(bf16[4,128,128]{2,1,0:T(8,128)(2,1)S(1)} %collective-permute-done.4.last_ref), channel_id=1, source_target_pairs={{0,1},{1,0},{2,3},{3,2},{4,5},{5,4},{6,7},{7,6},{8,9},{9,8},{10,11... | collective-permute-start | bytes 393224 | tf_op jit(solution)/shard_map/ppermute | solution.py:19
  42.0 5.5 %collective-permute-start.8 = (bf16[4,128,128]{2,1,0:T(8,128)(2,1)S(1)}, bf16[4,128,128]{2,1,0:T(8,128)(2,1)S(1)}, u32[]{:S(2)}, u32[]{:S(2)}) collective-permute-start(bf16[4,128,128]{2,1,0:T(8,128)(2,1)S(1)} %collective-permute-done.4.last_ref), channel_id=1, source_target_pairs={{0,2},{1,3},{2,0},{3,1},{4,6},{5,7},{6,4},{7,5},{8,10},{9,11},{10,... | collective-permute-start | bytes 393224 | tf_op jit(solution)/shard_map/ppermute | solution.py:19
  47.5 1.3 %collective-permute-start.9 = (bf16[4,128,128]{2,1,0:T(8,128)(2,1)S(1)}, bf16[4,128,128]{2,1,0:T(8,128)(2,1)S(1)}, u32[]{:S(2)}, u32[]{:S(2)}) collective-permute-start(bf16[4,128,128]{2,1,0:T(8,128)(2,1)S(1)} %collective-permute-done.8.last_ref), channel_id=1, source_target_pairs={{0,1},{1,0},{2,3},{3,2},{4,5},{5,4},{6,7},{7,6},{8,9},{9,8},{10,11... | collective-permute-start | bytes 393224 | tf_op jit(solution)/shard_map/ppermute | solution.py:19

commit v6 on v5

--- a/solution.py
+++ b/solution.py
@@ -23,10 +23,6 @@
     return exchange(block, lambda i: i ^ (1 << bit))
 
 
-def sent_up(block, bit):
-    return exchange(block, lambda i: None if i >> bit & 1 else i | 1 << bit)
-
-
 def limited(mebibytes):
     return pltpu.CompilerParams(vmem_limit_bytes=mebibytes * 1024 * 1024)
 
@@ -39,8 +35,8 @@
     return lax.fori_loop(0, doc_count, step, jnp.zeros_like(positions))
 
 
-def silu(values):
-    return values * (0.5 + 0.5 * jnp.tanh(0.5 * values))
+def silu_of_twice(half):
+    return half + half * jnp.tanh(half)
 
 
 def logical_place(head, core_bit, y_bit):
@@ -74,7 +70,10 @@
         out_ref[:, part * width : (part + 1) * width] = buffer[part, edge - rim_rows : edge, :]
 
 
-def tables_kernel(docs_ref, level_ref, gain_ref, table_ref, start_ref, gain_out_ref, *, doc_count):
+def tables_kernel(
+    docs_ref, level_ref, gain_ref, table_ref, start_ref, gain_out_ref, factor_ref, *, doc_count
+):
+    join_factors(docs_ref, doc_count, level_ref.shape[2], factor_ref)
     level_count, head_count, row_count = level_ref.shape
     tok_bits = row_count.bit_length() - 1
     index = lax.axis_index("seq")
@@ -162,12 +161,12 @@
     width = taps_ref.shape[1] // 3
     places = slice(tile * LANES, (tile + 1) * LANES)
     first = head * LANES
-    key_taps = taps_ref[:, columns(width + first)]
-    value_taps = taps_ref[:, columns(2 * width + first)]
-    grown = silu(convolved(window_ref.at[slot], key_taps, inside_ref, tile))
+    key_taps = 0.5 * taps_ref[:, columns(width + first)]
+    value_taps = 0.5 * taps_ref[:, columns(2 * width + first)]
+    grown = silu_of_twice(convolved(window_ref.at[slot], key_taps, inside_ref, tile))
     square = jnp.sum(grown * grown, axis=1, keepdims=True)
     key_out_ref[head, places, :] = (grown * lax.rsqrt(square + 1e-6)).astype(jnp.bfloat16)
-    values = silu(convolved(window_ref.at[slot + 1], value_taps, inside_ref, tile))
+    values = silu_of_twice(convolved(window_ref.at[slot + 1], value_taps, inside_ref, tile))
     value_out_ref[head, :, places] = values.T.astype(jnp.bfloat16)
 
 
@@ -306,25 +305,22 @@
         add_state((steps - 1) * heads + which)
 
 
-def join_kernel(docs_ref, mine_ref, theirs_ref, *out_refs, doc_count, row_count, bit, parts):
+def join_factors(docs_ref, doc_count, row_count, factor_ref):
     index = lax.axis_index("seq")
-    stride = 1 << bit
-    upper_first = (((index >> (bit + 1)) << (bit + 1)) + stride) * row_count
-
-    def step(i, found):
-        gap = docs_ref[i] - upper_first
-        return jnp.where((gap >= 0) & (gap < stride * row_count), 1, found)
-
-    upper_has = lax.fori_loop(0, doc_count, step, jnp.int32(0))
-    is_upper = (index >> bit) & 1
-    keep_mine = jnp.where((upper_has == 1) & (is_upper == 0), 0.0, 1.0)
-    keep_theirs = jnp.where((upper_has == 1) & (is_upper == 1), 0.0, 1.0)
-    skip = theirs_ref.shape[0] // 2 if parts == 2 else 0
-    count = out_refs[0].shape[0]
-    for part, out_ref in enumerate(out_refs):
-        mine = mine_ref[part * count : (part + 1) * count].astype(jnp.float32)
-        theirs = theirs_ref[skip + part * count : skip + (part + 1) * count].astype(jnp.float32)
-        out_ref[...] = (mine * keep_mine + theirs * keep_theirs).astype(jnp.bfloat16)
+    for bit in range(factor_ref.shape[0] // 2):
+        stride = 1 << bit
+        upper_first = (((index >> (bit + 1)) << (bit + 1)) + stride) * row_count
+
+        def step(i, found):
+            gap = docs_ref[i] - upper_first
+            return jnp.where((gap >= 0) & (gap < stride * row_count), 1, found)
+
+        upper_has = lax.fori_loop(0, doc_count, step, jnp.int32(0), unroll=8)
+        is_upper = (index >> bit) & 1
+        keep_mine = jnp.where((upper_has == 1) & (is_upper == 0), 0.0, 1.0)
+        keep_theirs = jnp.where((upper_has == 1) & (is_upper == 1), 0.0, 1.0)
+        factor_ref[2 * bit : 2 * bit + 1, :] = jnp.full((1, LANES), keep_mine, jnp.float32)
+        factor_ref[2 * bit + 1 : 2 * bit + 2, :] = jnp.full((1, LANES), keep_theirs, jnp.float32)
 
 
 def near_kernel(
@@ -366,9 +362,9 @@
 
         for which in range(heads):
             head = first_head + step * heads + which
-            taps = taps_ref[:, columns(head * LANES)]
+            taps = 0.5 * taps_ref[:, columns(head * LANES)]
             for tile in range(tiles):
-                grown = silu(convolved(window_ref.at[which], taps, inside_ref, tile))
+                grown = silu_of_twice(convolved(window_ref.at[which], taps, inside_ref, tile))
                 query_out_ref[head, tile * LANES : (tile + 1) * LANES, :] = grown.astype(
                     jnp.bfloat16
                 )
@@ -591,19 +587,10 @@
         name="first_rows",
     )(docs, key_in, value_in, conv_weight, rims, inside, later_state, keys, values_t)
 
-    def joined(mine, theirs, bit, parts=1):
-        count = mine.shape[0] // (2 if parts == 2 else 1)
-        shape = (count // parts, head_size, head_size)
-        return pl.pallas_call(
-            functools.partial(
-                join_kernel, doc_count=doc_count, row_count=row_count, bit=bit, parts=parts
-            ),
-            in_specs=[smem, vmem, vmem],
-            out_specs=[vmem] * parts,
-            out_shape=[pltpu.VMEM(shape, jnp.bfloat16)] * parts,
-            compiler_params=limited(1),
-            name="join",
-        )(doc_starts, mine, theirs)
+    def joined(mine, theirs, bit):
+        mine = mine.astype(jnp.float32) * factors[2 * bit]
+        theirs = theirs.astype(jnp.float32) * factors[2 * bit + 1]
+        return (mine + theirs).astype(jnp.bfloat16)
 
     def near_piece(first_head, piece_heads, buffers, docs):
         extra = [] if buffers is None else list(buffers)
@@ -663,28 +650,31 @@
     quarter = head_count // 4
     state, docs = lax.optimization_barrier((state, docs))
     first_state = swapped(state, 0)
-    table, starts, gains = pl.pallas_call(
+    table, starts, gains, factors = pl.pallas_call(
         functools.partial(tables_kernel, doc_count=doc_count),
         in_specs=[smem, vmem, vmem],
-        out_specs=[vmem] * 3,
+        out_specs=[vmem] * 4,
         out_shape=[
             pltpu.VMEM((level_count, head_count, row_count), jnp.float32),
             pltpu.VMEM((8, row_count), jnp.int32),
             pltpu.VMEM((head_count, head_size, LANES), jnp.float32),
+            pltpu.VMEM((2 * (dev_bits - 1), LANES), jnp.float32),
         ],
         compiler_params=limited(2),
         name="tables",
     )(docs, jnp.transpose(level_weight, (1, 0, 2)), out_gain.reshape(head_count, 1, head_size))
-    first_state, table, starts, gains = lax.optimization_barrier(
-        (first_state, table, starts, gains)
+    first_state, table, starts, gains, factors = lax.optimization_barrier(
+        (first_state, table, starts, gains, factors)
     )
-    pair_kept, pair_sent = joined(state, first_state, 0, parts=2)
+    half = 2 * quarter
+    pair_kept = joined(state[:quarter], first_state[half : half + quarter], 0)
+    pair_sent = joined(state[quarter:half], first_state[half + quarter :], 0)
 
     pair_sent, tied = lax.optimization_barrier((pair_sent, docs))
     pair_in = swapped(pair_sent, 1)
     buffers = near_piece(0, quarter, None, tied)
     pair_in, buffers = lax.optimization_barrier((pair_in, buffers))
-    (carried,) = joined(pair_kept, pair_in, 1)
+    carried = joined(pair_kept, pair_in, 1)
 
     received = []
     for bit in range(2, dev_bits - 1):
@@ -695,11 +685,11 @@
             buffers = near_piece(quarter, quarter, buffers, tied)
             arrived, buffers = lax.optimization_barrier((arrived, buffers))
         received.append(arrived)
-        (carried,) = joined(carried, arrived, bit)
+        carried = joined(carried, arrived, bit)
 
     mine = jnp.stack([pair_kept] + received)
     carried, mine, tied = lax.optimization_barrier((carried, mine, docs))
-    last_own = sent_up(carried, dev_bits - 1)
+    last_own = swapped(carried, dev_bits - 1)
     theirs = swapped(mine, 1)
     buffers = near_piece(2 * quarter, 2 * quarter, buffers, tied)
     last_own, theirs, buffers = lax.optimization_barrier((last_own, theirs, buffers))

time: 51.2 us -> 46.9 us (0.916)
  Pallas kernels: 30.3 us -> 27.9 us
  starting transfers between devices: 16.5 us -> 14.3 us
    ppermute x10, starting transfers between devices: 16.5 us -> 14.3 us  [exchange(): return lax.ppermute(block, 'seq', route)]
    pallas_call x3 -> x0, Pallas kernels: 2.04 us -> none  [joined(): pl.pallas_call(functools.partial(join_kernel, doc_count=doc_count, row_co...]
  transfers between devices with their start and end apart: 10 -> 10, of which waited for: 5 -> 5; matrix products, arithmetic and copies ran while one was open for 0% -> 0% of each run, Pallas kernels for 44% -> 48%
where the time goes in v6:
time: 46.9 us; the launch traced here: 46.8 us
  Pallas kernels  27.9 us (59%)
  starting transfers between devices  14.3 us (30%)
  waiting for transfers between devices  3.79 us (8%)
    ppermute x10, starting transfers between devices, exchange(): return lax.ppermute(block, 'seq', route)  14.3 us
    pallas_call x3, Pallas kernels, near_piece(): pl.pallas_call(functools.partial(near_kernel, first_head=first_head, head...  10.8 us
    pallas_call x4, Pallas kernels, far_piece(): pl.pallas_call(functools.partial(far_skip if out is not None else far_ker...  6.53 us
    pallas_call x1, Pallas kernels, local(): pl.pallas_call(functools.partial(later_rows_kernel, doc_count=doc_count,...  5.99 us
    ppermute x10, waiting for transfers between devices, exchange(): return lax.ppermute(block, 'seq', route)  3.79 us
    pallas_call x1, Pallas kernels, local(): pl.pallas_call(functools.partial(first_rows_kernel, doc_count=doc_count,...  2.54 us
    pallas_call x1, Pallas kernels, local(): pl.pallas_call(rim_kernel, in_specs=[pl.BlockSpec(memory_space=pltpu.HBM)...  1.09 us
    pallas_call x1, Pallas kernels, local(): pl.pallas_call(functools.partial(tables_kernel, doc_count=doc_count), in_...  0.99 us
  transfers between devices with their start and end apart: 10, of which 5 were waited for; matrix products, arithmetic and copies ran while one was open for 0% of the time, Pallas kernels for 48%

profile of v6, /device:TPU:0, one launch (start us, length us, event | category | flops | bytes accessed | tf_op | source)
XLA Modules:
  0.0 46.8 jit_solution(12941423232373301304)
XLA Ops:
  0.0 1.1 %rim.1 = bf16[3,6144]{1,0:T(4,128)(2,1)S(1)} custom-call(bf16[512,2048]{1,0:T(8,128)(2,1)} %query_ref.7, bf16[512,2048]{1,0:T(8,128)(2,1)} %key_ref.5, bf16[512,2048]{1,0:T(8,128)(2,1)} %value_ref.5), custom_call_target="tpu_custom_call" | custom-call | tf_op jit(solution)/shard_map/rim/pallas_call | solution.py:538
  1.1 2.5 %collective-permute-start = (bf16[3,6144]{1,0:T(4,128)(2,1)S(1)}, bf16[3,6144]{1,0:T(4,128)(2,1)S(1)}, u32[]{:S(2)}, u32[]{:S(2)}) collective-permute-start(bf16[3,6144]{1,0:T(4,128)(2,1)S(1)} %rim.1), channel_id=1, source_target_pairs={{0,1},{1,2},{2,3},{3,4},{4,5},{5,6},{6,7},{7,8},{8,9},{9,10},{10,1... | collective-permute-start | bytes 110600 | tf_op jit(solution)/shard_map/ppermute | solution.py:19
  3.7 6.0 %later_rows.1 = (bf16[16,512,128]{2,1,0:T(8,128)(2,1)S(1)}, bf16[16,128,512]{2,1,0:T(8,128)(2,1)S(1)}, f32[16,128,128]{2,1,0:T(8,128)S(1)}, f32[4,144,128]{2,1,0:T(8,128)S(1)}) custom-call(s32[8]{0:T(128)S(1)} %copy-done.6, bf16[512,2048]{1,0:T(8,128)(2,1)S(1)} %copy-done, bf16[512,2048]{1,0:T(8,128)(2,1)S(1)} %copy-done.1, f32[4,6144]{1,0:T(4,128)S(1)} %copy-done.3), custom_call_target="tpu_custom_call" | custom-call | flops 500000000 | bytes 4000000 | tf_op jit(solution)/shard_map/later_rows/pallas_call | solution.py:553
  9.7 0.0 copy-start.4
  9.7 0.0 copy-start.5
  9.7 0.0 copy-start.2
  9.7 2.5 %first_rows.1 = (bf16[16,512,128]{2,1,0:T(8,128)(2,1)S(1)}, bf16[16,128,512]{2,1,0:T(8,128)(2,1)S(1)}, bf16[16,128,128]{2,1,0:T(8,128)(2,1)S(1)}) custom-call(s32[8]{0:T(128)S(1)} %copy-done.6, bf16[512,2048]{1,0:T(8,128)(2,1)S(1)} %copy-done, bf16[512,2048]{1,0:T(8,128)(2,1)S(1)} %copy-done.1, ...), custom_call_target="tpu_custom_call", output_to_operand_aliasing={{0}: (7, {}), {1}: (8, {})} | custom-call | tf_op jit(solution)/shard_map/first_rows/pallas_call | solution.py:573
  12.3 2.7 %collective-permute-start.1 = (bf16[16,128,128]{2,1,0:T(8,128)(2,1)S(1)}, bf16[16,128,128]{2,1,0:T(8,128)(2,1)S(1)}, u32[]{:S(2)}, u32[]{:S(2)}) collective-permute-start(bf16[16,128,128]{2,1,0:T(8,128)(2,1)S(1)} %get-tuple-element.73), channel_id=1, source_target_pairs={{0,1},{1,0},{2,3},{3,2},{4,5},{5,4},{6,7},{7,6},{8,9},{9,8},{10,11... | collective-permute-start | bytes 1572872 | tf_op jit(solution)/shard_map/ppermute | solution.py:19
  15.0 1.0 %tables.1 = (f32[14,16,512]{2,1,0:T(8,128)S(1)}, s32[8,512]{1,0:T(8,128)S(1)}, f32[16,128,128]{2,1,0:T(8,128)S(1)}, f32[6,128]{1,0:T(8,128)S(1)}) custom-call(s32[8]{0:T(128)S(1)} %copy-done.6, bf16[14,16,512]{2,1,0:T(8,128)(2,1)S(1)} %bitcast.18, f32[16,1,128]{2,1,0:T(1,128)S(1)} %bitcast.19), custom_call_target="tpu_custom_call" | custom-call | tf_op jit(solution)/shard_map/tables/pallas_call | solution.py:653
  15.9 0.5 %collective-permute-done.1.first_state_ref.refs_4_ = bf16[16,128,128]{2,1,0:T(8,128)(2,1)S(1)} collective-permute-done((bf16[16,128,128]{2,1,0:T(8,128)(2,1)S(1)}, bf16[16,128,128]{2,1,0:T(8,128)(2,1)S(1)}, u32[]{:S(2)}, u32[]{:S(2)}) %collective-permute-start.1) | collective-permute-done | bytes 524320 | tf_op jit(solution)/shard_map/ppermute | solution.py:19
  16.5 0.1 fusion
  16.6 1.6 %collective-permute-start.2 = (bf16[4,128,128]{2,1,0:T(8,128)(2,1)S(1)}, bf16[4,128,128]{2,1,0:T(8,128)(2,1)S(1)}, u32[]{:S(2)}, u32[]{:S(2)}) collective-permute-start(bf16[4,128,128]{2,1,0:T(8,128)(2,1)S(1)} %get-tuple-element.81), channel_id=1, source_target_pairs={{0,2},{1,3},{2,0},{3,1},{4,6},{5,7},{6,4},{7,5},{8,10},{9,11},{10,... | collective-permute-start | bytes 393224 | tf_op jit(solution)/shard_map/ppermute | solution.py:19
  18.2 2.8 %near.3 = (bf16[16,512,128]{2,1,0:T(8,128)(2,1)S(1)}, f32[16,128,512]{2,1,0:T(8,128)S(1)}) custom-call(s32[8]{0:T(128)S(1)} %copy-done.6, bf16[512,2048]{1,0:T(8,128)(2,1)S(1)} %copy-done.2, bf16[3,6144]{1,0:T(4,128)(2,1)S(1)} %collective-permute-done.rim_ref, f32[4,6144]{1,0:T(4,128)S(1)} %copy-done.3, f32[4,144,128]{2,1,0:T(8,128)S(1)} %get-tuple-element.68.inside_ref, ...), custom_call_target="tpu_custom_call" | custom-call | flops 5000000000 | bytes 35000000 | tf_op jit(solution)/shard_map/near/pallas_call | solution.py:597
  21.0 1.5 %collective-permute-done.2 = bf16[4,128,128]{2,1,0:T(8,128)(2,1)S(1)} collective-permute-done((bf16[4,128,128]{2,1,0:T(8,128)(2,1)S(1)}, bf16[4,128,128]{2,1,0:T(8,128)(2,1)S(1)}, u32[]{:S(2)}, u32[]{:S(2)}) %collective-permute-start.2) | collective-permute-done | bytes 131104 | tf_op jit(solution)/shard_map/ppermute | solution.py:19
  22.4 0.1 add_convert_fusion.1
  22.5 1.6 %collective-permute-start.3 = (bf16[4,128,128]{2,1,0:T(8,128)(2,1)S(1)}, bf16[4,128,128]{2,1,0:T(8,128)(2,1)S(1)}, u32[]{:S(2)}, u32[]{:S(2)}) collective-permute-start(bf16[4,128,128]{2,1,0:T(8,128)(2,1)S(1)} %add_convert_fusion.1), channel_id=1, source_target_pairs={{0,4},{1,5},{2,6},{3,7},{4,0},{5,1},{6,2},{7,3},{8,12},{9,13},{10,... | collective-permute-start | bytes 393224 | tf_op jit(solution)/shard_map/ppermute | solution.py:19
  24.2 2.8 %near.4 = (bf16[16,512,128]{2,1,0:T(8,128)(2,1)S(1)}, f32[16,128,512]{2,1,0:T(8,128)S(1)}) custom-call(s32[8]{0:T(128)S(1)} %copy-done.6, bf16[512,2048]{1,0:T(8,128)(2,1)S(1)} %copy-done.2, bf16[3,6144]{1,0:T(4,128)(2,1)S(1)} %collective-permute-done.rim_ref, f32[4,6144]{1,0:T(4,128)S(1)} %copy-done.3, ...), custom_call_target="tpu_custom_call", output_to_operand_aliasing={{0}: (9, {}), {1}: (10, {})} | custom-call | flops 5000000000 | bytes 35000000 | tf_op jit(solution)/shard_map/near/pallas_call | solution.py:597
  27.0 0.6 %collective-permute-done.3 = bf16[4,128,128]{2,1,0:T(8,128)(2,1)S(1)} collective-permute-done((bf16[4,128,128]{2,1,0:T(8,128)(2,1)S(1)}, bf16[4,128,128]{2,1,0:T(8,128)(2,1)S(1)}, u32[]{:S(2)}, u32[]{:S(2)}) %collective-permute-start.3) | collective-permute-done | bytes 131104 | tf_op jit(solution)/shard_map/ppermute | solution.py:19
  27.6 0.1 add_convert_fusion
  27.7 2.7 %collective-permute-start.4 = (bf16[4,128,128]{2,1,0:T(8,128)(2,1)S(1)}, bf16[4,128,128]{2,1,0:T(8,128)(2,1)S(1)}, u32[]{:S(2)}, u32[]{:S(2)}) collective-permute-start(bf16[4,128,128]{2,1,0:T(8,128)(2,1)S(1)} %add_convert_fusion), channel_id=1, source_target_pairs={{0,8},{1,9},{2,10},{3,11},{4,12},{5,13},{6,14},{7,15},{8,0},{9,1},... | collective-permute-start | bytes 393224 | tf_op jit(solution)/shard_map/ppermute | solution.py:19
  30.3 1.5 %collective-permute-start.5 = (bf16[2,4,128,128]{3,2,1,0:T(8,128)(2,1)S(1)}, bf16[2,4,128,128]{3,2,1,0:T(8,128)(2,1)S(1)}, u32[]{:S(2)}, u32[]{:S(2)}) collective-permute-start(bf16[2,4,128,128]{3,2,1,0:T(8,128)(2,1)S(1)} %pad_maximum_fusion.1), channel_id=1, source_target_pairs={{0,2},{1,3},{2,0},{3,1},{4,6},{5,7},{6,4},{7,5},{8,10},{9,11},{10,... | collective-permute-start | bytes 786440 | tf_op jit(solution)/shard_map/ppermute | solution.py:19
  31.8 5.2 %near.5 = (bf16[16,512,128]{2,1,0:T(8,128)(2,1)S(1)}, f32[16,128,512]{2,1,0:T(8,128)S(1)}) custom-call(s32[8]{0:T(128)S(1)} %copy-done.6, bf16[512,2048]{1,0:T(8,128)(2,1)S(1)} %copy-done.2, bf16[3,6144]{1,0:T(4,128)(2,1)S(1)} %collective-permute-done.rim_ref, f32[4,6144]{1,0:T(4,128)S(1)} %copy-done.3, ...), custom_call_target="tpu_custom_call", output_to_operand_aliasing={{0}: (9, {}), {1}: (10, {})} | custom-call | flops 5000000000 | bytes 35000000 | tf_op jit(solution)/shard_map/near/pallas_call | solution.py:597
  37.1 0.1 pad_maximum_fusion.lower_ref
  37.2 0.1 collective-permute-start.6
  37.2 0.5 %collective-permute-start.7 = (bf16[4,128,128]{2,1,0:T(8,128)(2,1)S(1)}, bf16[4,128,128]{2,1,0:T(8,128)(2,1)S(1)}, u32[]{:S(2)}, u32[]{:S(2)}) collective-permute-start(bf16[4,128,128]{2,1,0:T(8,128)(2,1)S(1)} %collective-permute-done.4.last_ref), channel_id=1, source_target_pairs={{0,1},{1,0},{2,3},{3,2},{4,5},{5,4},{6,7},{7,6},{8,9},{9,8},{10,11... | collective-permute-start | bytes 393224 | tf_op jit(solution)/shard_map/ppermute | solution.py:19
  37.7 1.1 %collective-permute-start.8 = (bf16[4,128,128]{2,1,0:T(8,128)(2,1)S(1)}, bf16[4,128,128]{2,1,0:T(8,128)(2,1)S(1)}, u32[]{:S(2)}, u32[]{:S(2)}) collective-permute-start(bf16[4,128,128]{2,1,0:T(8,128)(2,1)S(1)} %collective-permute-done.4.last_ref), channel_id=1, source_target_pairs={{0,2},{1,3},{2,0},{3,1},{4,6},{5,7},{6,4},{7,5},{8,10},{9,11},{10,... | collective-permute-start | bytes 393224 | tf_op jit(solution)/shard_map/ppermute | solution.py:19
  38.8 1.2 %far.4.rest_0_ = bf16[512,512]{1,0:T(8,128)(2,1)S(1)} custom-call(bf16[16,512,128]{2,1,0:T(8,128)(2,1)S(1)} %get-tuple-element.104.query_ref.refs_0_, f32[16,128,512]{2,1,0:T(8,128)S(1)} %get-tuple-element.105.near_ref.refs_1_, f32[14,16,512]{2,1,0:T(8,128)S(1)} %get-tuple-element.83.table_ref.refs_2_, ...), custom_call_target="tpu_custom_call" | custom-call | flops 1000000 | bytes 10000 | tf_op jit(solution)/shard_map/far/pallas_call | solution.py:629
  40.1 2.0 %far.5.refs_8_ = bf16[512,2048]{1,0:T(8,128)(2,1)} custom-call(bf16[16,512,128]{2,1,0:T(8,128)(2,1)S(1)} %get-tuple-element.104.query_ref.refs_0_, f32[16,128,512]{2,1,0:T(8,128)S(1)} %get-tuple-element.105.near_ref.refs_1_, f32[14,16,512]{2,1,0:T(8,128)S(1)} %get-tuple-element.83.table_ref.refs_2_, f32[16,128,128]{2,1,0:T(8,128)S(1)} %get-tuple-element.106.gain_ref.refs_3_, ...), custom_call_target="tpu_custom_call" | custom-call | flops 1000000 | bytes 10000 | tf_op jit(solution)/shard_map/far/pallas_call | solution.py:629
  42.2 1.1 %collective-permute-done.8.last_ref = bf16[4,128,128]{2,1,0:T(8,128)(2,1)S(1)} collective-permute-done((bf16[4,128,128]{2,1,0:T(8,128)(2,1)S(1)}, bf16[4,128,128]{2,1,0:T(8,128)(2,1)S(1)}, u32[]{:S(2)}, u32[]{:S(2)}) %collective-permute-start.8) | collective-permute-done | bytes 131104 | tf_op jit(solution)/shard_map/ppermute | solution.py:19
  43.2 1.2 %far.6.refs_7_ = bf16[512,512]{1,0:T(8,128)(2,1)S(1)} custom-call(bf16[16,512,128]{2,1,0:T(8,128)(2,1)S(1)} %get-tuple-element.104.query_ref.refs_0_, f32[16,128,512]{2,1,0:T(8,128)S(1)} %get-tuple-element.105.near_ref.refs_1_, f32[14,16,512]{2,1,0:T(8,128)S(1)} %get-tuple-element.83.table_ref.refs_2_, ...), custom_call_target="tpu_custom_call" | custom-call | flops 1000000 | bytes 10000 | tf_op jit(solution)/shard_map/far/pallas_call | solution.py:629
  44.5 0.1 collective-permute-done.9.refs_6_
  44.6 2.0 %far.7 = bf16[512,2048]{1,0:T(8,128)(2,1)} custom-call(bf16[16,512,128]{2,1,0:T(8,128)(2,1)S(1)} %get-tuple-element.104.query_ref.refs_0_, f32[16,128,512]{2,1,0:T(8,128)S(1)} %get-tuple-element.105.near_ref.refs_1_, f32[14,16,512]{2,1,0:T(8,128)S(1)} %get-tuple-element.83.table_ref.refs_2_, ...), custom_call_target="tpu_custom_call", output_to_operand_aliasing={{}: (8, {})} | custom-call | flops 1000000 | bytes 10000 | tf_op jit(solution)/shard_map/far/pallas_call | solution.py:629
  (19 shorter events, 0.1 us)
Async XLA Ops:
  0.0 3.6 %copy-start.1 = (bf16[512,2048]{1,0:T(8,128)(2,1)S(1)}, bf16[512,2048]{1,0:T(8,128)(2,1)}, u32[]{:S(2)}) copy-start(bf16[512,2048]{1,0:T(8,128)(2,1)} %value_ref.5) | copy-start | bytes 6291460
  0.0 3.6 %copy-start = (bf16[512,2048]{1,0:T(8,128)(2,1)S(1)}, bf16[512,2048]{1,0:T(8,128)(2,1)}, u32[]{:S(2)}) copy-start(bf16[512,2048]{1,0:T(8,128)(2,1)} %key_ref.5) | copy-start | bytes 6291460
  0.0 3.6 %copy-start.6 = (s32[8]{0:T(128)S(1)}, s32[8]{0:T(128)}, u32[]{:S(2)}) copy-start(s32[8]{0:T(128)} %docs_ref.5) | copy-start | bytes 100
  0.0 3.6 %copy-start.3 = (f32[4,6144]{1,0:T(4,128)S(1)}, f32[4,6144]{1,0:T(4,128)}, u32[]{:S(2)}) copy-start(f32[4,6144]{1,0:T(4,128)} %taps_ref.9) | copy-start | bytes 294916
  1.1 8.6 %collective-permute-start = (bf16[3,6144]{1,0:T(4,128)(2,1)S(1)}, bf16[3,6144]{1,0:T(4,128)(2,1)S(1)}, u32[]{:S(2)}, u32[]{:S(2)}) collective-permute-start(bf16[3,6144]{1,0:T(4,128)(2,1)S(1)} %rim.1), channel_id=1, source_target_pairs={{0,1},{1,2},{2,3},{3,4},{4,5},{5,6},{6,7},{7,8},{8,9},{9,10},{10,1... | collective-permute-start | bytes 110600 | tf_op jit(solution)/shard_map/ppermute | solution.py:19
  9.7 5.3 %copy-start.4 = (bf16[16,14,512]{2,0,1:T(8,128)(2,1)S(1)}, bf16[16,14,512]{2,0,1:T(8,128)(2,1)}, u32[]{:S(2)}) copy-start(bf16[16,14,512]{2,0,1:T(8,128)(2,1)} %param.11) | copy-start | bytes 688132
  9.7 5.3 %copy-start.5 = (f32[2048]{0:T(1024)S(1)}, f32[2048]{0:T(1024)}, u32[]{:S(2)}) copy-start(f32[2048]{0:T(1024)} %param.12) | copy-start | bytes 24580
  9.7 8.5 %copy-start.2 = (bf16[512,2048]{1,0:T(8,128)(2,1)S(1)}, bf16[512,2048]{1,0:T(8,128)(2,1)}, u32[]{:S(2)}) copy-start(bf16[512,2048]{1,0:T(8,128)(2,1)} %query_ref.7) | copy-start | bytes 6291460
  12.3 4.2 %collective-permute-start.1 = (bf16[16,128,128]{2,1,0:T(8,128)(2,1)S(1)}, bf16[16,128,128]{2,1,0:T(8,128)(2,1)S(1)}, u32[]{:S(2)}, u32[]{:S(2)}) collective-permute-start(bf16[16,128,128]{2,1,0:T(8,128)(2,1)S(1)} %get-tuple-element.73), channel_id=1, source_target_pairs={{0,1},{1,0},{2,3},{3,2},{4,5},{5,4},{6,7},{7,6},{8,9},{9,8},{10,11... | collective-permute-start | bytes 1572872 | tf_op jit(solution)/shard_map/ppermute | solution.py:19
  16.6 5.8 %collective-permute-start.2 = (bf16[4,128,128]{2,1,0:T(8,128)(2,1)S(1)}, bf16[4,128,128]{2,1,0:T(8,128)(2,1)S(1)}, u32[]{:S(2)}, u32[]{:S(2)}) collective-permute-start(bf16[4,128,128]{2,1,0:T(8,128)(2,1)S(1)} %get-tuple-element.81), channel_id=1, source_target_pairs={{0,2},{1,3},{2,0},{3,1},{4,6},{5,7},{6,4},{7,5},{8,10},{9,11},{10,... | collective-permute-start | bytes 393224 | tf_op jit(solution)/shard_map/ppermute | solution.py:19
  22.5 5.0 %collective-permute-start.3 = (bf16[4,128,128]{2,1,0:T(8,128)(2,1)S(1)}, bf16[4,128,128]{2,1,0:T(8,128)(2,1)S(1)}, u32[]{:S(2)}, u32[]{:S(2)}) collective-permute-start(bf16[4,128,128]{2,1,0:T(8,128)(2,1)S(1)} %add_convert_fusion.1), channel_id=1, source_target_pairs={{0,4},{1,5},{2,6},{3,7},{4,0},{5,1},{6,2},{7,3},{8,12},{9,13},{10,... | collective-permute-start | bytes 393224 | tf_op jit(solution)/shard_map/ppermute | solution.py:19
  27.7 9.4 %collective-permute-start.4 = (bf16[4,128,128]{2,1,0:T(8,128)(2,1)S(1)}, bf16[4,128,128]{2,1,0:T(8,128)(2,1)S(1)}, u32[]{:S(2)}, u32[]{:S(2)}) collective-permute-start(bf16[4,128,128]{2,1,0:T(8,128)(2,1)S(1)} %add_convert_fusion), channel_id=1, source_target_pairs={{0,8},{1,9},{2,10},{3,11},{4,12},{5,13},{6,14},{7,15},{8,0},{9,1},... | collective-permute-start | bytes 393224 | tf_op jit(solution)/shard_map/ppermute | solution.py:19
  30.3 6.8 %collective-permute-start.5 = (bf16[2,4,128,128]{3,2,1,0:T(8,128)(2,1)S(1)}, bf16[2,4,128,128]{3,2,1,0:T(8,128)(2,1)S(1)}, u32[]{:S(2)}, u32[]{:S(2)}) collective-permute-start(bf16[2,4,128,128]{3,2,1,0:T(8,128)(2,1)S(1)} %pad_maximum_fusion.1), channel_id=1, source_target_pairs={{0,2},{1,3},{2,0},{3,1},{4,6},{5,7},{6,4},{7,5},{8,10},{9,11},{10,... | collective-permute-start | bytes 786440 | tf_op jit(solution)/shard_map/ppermute | solution.py:19
  37.2 2.9 %collective-permute-start.6 = (bf16[2,8,128,128]{3,2,1,0:T(8,128)(2,1)S(1)}, bf16[2,8,128,128]{3,2,1,0:T(8,128)(2,1)S(1)}, u32[]{:S(2)}, u32[]{:S(2)}) collective-permute-start(bf16[2,8,128,128]{3,2,1,0:T(8,128)(2,1)S(1)} %pad_maximum_fusion.lower_ref), channel_id=1, source_target_pairs={{0,1},{1,0},{2,3},{3,2},{4,5},{5,4},{6,7},{7,6},{8,9},{9,8},{10,11... | collective-permute-start | bytes 1572872 | tf_op jit(solution)/shard_map/ppermute | solution.py:19
  37.2 2.8 %collective-permute-start.7 = (bf16[4,128,128]{2,1,0:T(8,128)(2,1)S(1)}, bf16[4,128,128]{2,1,0:T(8,128)(2,1)S(1)}, u32[]{:S(2)}, u32[]{:S(2)}) collective-permute-start(bf16[4,128,128]{2,1,0:T(8,128)(2,1)S(1)} %collective-permute-done.4.last_ref), channel_id=1, source_target_pairs={{0,1},{1,0},{2,3},{3,2},{4,5},{5,4},{6,7},{7,6},{8,9},{9,8},{10,11... | collective-permute-start | bytes 393224 | tf_op jit(solution)/shard_map/ppermute | solution.py:19
  37.7 5.5 %collective-permute-start.8 = (bf16[4,128,128]{2,1,0:T(8,128)(2,1)S(1)}, bf16[4,128,128]{2,1,0:T(8,128)(2,1)S(1)}, u32[]{:S(2)}, u32[]{:S(2)}) collective-permute-start(bf16[4,128,128]{2,1,0:T(8,128)(2,1)S(1)} %collective-permute-done.4.last_ref), channel_id=1, source_target_pairs={{0,2},{1,3},{2,0},{3,1},{4,6},{5,7},{6,4},{7,5},{8,10},{9,11},{10,... | collective-permute-start | bytes 393224 | tf_op jit(solution)/shard_map/ppermute | solution.py:19
  43.2 1.3 %collective-permute-start.9 = (bf16[4,128,128]{2,1,0:T(8,128)(2,1)S(1)}, bf16[4,128,128]{2,1,0:T(8,128)(2,1)S(1)}, u32[]{:S(2)}, u32[]{:S(2)}) collective-permute-start(bf16[4,128,128]{2,1,0:T(8,128)(2,1)S(1)} %collective-permute-done.8.last_ref), channel_id=1, source_target_pairs={{0,1},{1,0},{2,3},{3,2},{4,5},{5,4},{6,7},{7,6},{8,9},{9,8},{10,11... | collective-permute-start | bytes 393224 | tf_op jit(solution)/shard_map/ppermute | solution.py:19

commit v7 on v6

--- a/solution.py
+++ b/solution.py
@@ -386,7 +386,7 @@
             )
             fine = jnp.where(sub16 > low_row, 0.0, fine)
             for tile in range(tiles):
-                fine_ref[which, tile] = fine[:, tile * LANES : (tile + 1) * LANES]
+                fine_ref[which, tile, 0:16, :] = fine[:, tile * LANES : (tile + 1) * LANES]
             for part in range(row_count // span):
                 rows = (part + 1) * span
                 scores = lax.dot_general(
@@ -551,7 +551,7 @@
     rims = exchange(tails, lambda i: i + 1 if i + 1 < dev_count else None)
     heads = 4
     keys, values_t, later_state, inside = pl.pallas_call(
-        functools.partial(later_rows_kernel, doc_count=doc_count, heads=heads),
+        functools.partial(later_rows_kernel, doc_count=doc_count, heads=2 * heads),
         in_specs=[smem] + [vmem] * 3,
         out_specs=[vmem] * 4,
         out_shape=[
@@ -560,8 +560,8 @@
             pltpu.VMEM((head_count, head_size, head_size), jnp.float32),
             pltpu.VMEM((tiles, LANES + 8 * (rim_rows - 1), LANES), jnp.float32),
         ],
-        scratch_shapes=[pltpu.VMEM((2 * heads, window_rows(row_count), LANES), jnp.float32)],
-        compiler_params=limited(6),
+        scratch_shapes=[pltpu.VMEM((4 * heads, window_rows(row_count), LANES), jnp.float32)],
+        compiler_params=limited(14),
         cost_estimate=pl.CostEstimate(
             flops=500_000_000, bytes_accessed=4_000_000, transcendentals=1_500_000
         ),
@@ -572,7 +572,7 @@
     )
     keys, values_t, state = pl.pallas_call(
         functools.partial(
-            first_rows_kernel, doc_count=doc_count, row_count=row_count, heads=heads
+            first_rows_kernel, doc_count=doc_count, row_count=row_count, heads=2 * heads
         ),
         in_specs=[smem] + [vmem] * 8,
         out_specs=[vmem] * 3,
@@ -581,9 +581,9 @@
             pltpu.VMEM((head_count, head_size, row_count), jnp.bfloat16),
             pltpu.VMEM((head_count, head_size, head_size), jnp.bfloat16),
         ],
-        scratch_shapes=[pltpu.VMEM((2 * heads, window_rows(LANES), LANES), jnp.float32)],
+        scratch_shapes=[pltpu.VMEM((4 * heads, window_rows(LANES), LANES), jnp.float32)],
         input_output_aliases={7: 0, 8: 1},
-        compiler_params=limited(4),
+        compiler_params=limited(6),
         name="first_rows",
     )(docs, key_in, value_in, conv_weight, rims, inside, later_state, keys, values_t)
 
@@ -593,6 +593,7 @@
         return (mine + theirs).astype(jnp.bfloat16)
 
     def near_piece(first_head, piece_heads, buffers, docs):
+        heads = piece_heads
         extra = [] if buffers is None else list(buffers)
         return pl.pallas_call(
             functools.partial(
@@ -610,11 +611,11 @@
             ],
             scratch_shapes=[
                 pltpu.VMEM((heads, window_rows(row_count), LANES), jnp.float32),
-                pltpu.VMEM((heads, tiles, 16, LANES), jnp.float32),
+                pltpu.VMEM((heads, tiles, 24, LANES), jnp.float32),
                 pltpu.VMEM((heads, row_count, row_count), jnp.bfloat16),
             ],
             input_output_aliases={9: 0, 10: 1} if extra else {},
-            compiler_params=limited(6),
+            compiler_params=limited(10),
             cost_estimate=pl.CostEstimate(
                 flops=5_000_000_000, bytes_accessed=35_000_000, transcendentals=300_000
             ),
@@ -642,7 +643,7 @@
             input_output_aliases={} if out is None else {8: 0},
             compiler_params=limited(4),
             cost_estimate=pl.CostEstimate(
-                flops=1_000_000, bytes_accessed=10_000, transcendentals=0
+                flops=5_000_000_000, bytes_accessed=35_000_000, transcendentals=0
             ),
             name="far",
         )(queries, near, table, gains, first_state, lower, last_state, *extra)

time: 46.9 us -> 45.9 us (0.979)
  Pallas kernels: 27.9 us -> 26.8 us
    pallas_call x1, Pallas kernels: 5.99 us -> 5.48 us  [local(): pl.pallas_call(functools.partial(later_rows_kernel, doc_count=doc_count,...]
    pallas_call x3, Pallas kernels: 10.8 us -> 10.3 us  [near_piece(): pl.pallas_call(functools.partial(near_kernel, first_head=first_head, head...]
  transfers between devices with their start and end apart: 10 -> 10, of which waited for: 5 -> 6; matrix products, arithmetic and copies ran while one was open for 0% -> 0% of each run, Pallas kernels for 48% -> 47%
where the time goes in v7:
time: 45.9 us; the launch traced here: 45.7 us
  Pallas kernels  26.8 us (58%)
  starting transfers between devices  14.2 us (31%)
  waiting for transfers between devices  3.94 us (9%)
    ppermute x10, starting transfers between devices, exchange(): return lax.ppermute(block, 'seq', route)  14.2 us
    pallas_call x3, Pallas kernels, near_piece(): pl.pallas_call(functools.partial(near_kernel, first_head=first_head, head...  10.3 us
    pallas_call x4, Pallas kernels, far_piece(): pl.pallas_call(functools.partial(far_skip if out is not None else far_ker...  6.58 us
    pallas_call x1, Pallas kernels, local(): pl.pallas_call(functools.partial(later_rows_kernel, doc_count=doc_count,...  5.48 us
    ppermute x10, waiting for transfers between devices, exchange(): return lax.ppermute(block, 'seq', route)  3.94 us
    pallas_call x1, Pallas kernels, local(): pl.pallas_call(functools.partial(first_rows_kernel, doc_count=doc_count,...  2.23 us
    pallas_call x1, Pallas kernels, local(): pl.pallas_call(functools.partial(tables_kernel, doc_count=doc_count), in_...  1.17 us
    pallas_call x1, Pallas kernels, local(): pl.pallas_call(rim_kernel, in_specs=[pl.BlockSpec(memory_space=pltpu.HBM)...  1.09 us
  transfers between devices with their start and end apart: 10, of which 6 were waited for; matrix products, arithmetic and copies ran while one was open for 0% of the time, Pallas kernels for 47%

profile of v7, /device:TPU:0, one launch (start us, length us, event | category | flops | bytes accessed | tf_op | source)
XLA Modules:
  0.0 45.7 jit_solution(3113888027037735763)
XLA Ops:
  0.0 1.1 %rim.1 = bf16[3,6144]{1,0:T(4,128)(2,1)S(1)} custom-call(bf16[512,2048]{1,0:T(8,128)(2,1)} %query_ref.7, bf16[512,2048]{1,0:T(8,128)(2,1)} %key_ref.5, bf16[512,2048]{1,0:T(8,128)(2,1)} %value_ref.5), custom_call_target="tpu_custom_call" | custom-call | tf_op jit(solution)/shard_map/rim/pallas_call | solution.py:538
  1.1 2.5 %collective-permute-start = (bf16[3,6144]{1,0:T(4,128)(2,1)S(1)}, bf16[3,6144]{1,0:T(4,128)(2,1)S(1)}, u32[]{:S(2)}, u32[]{:S(2)}) collective-permute-start(bf16[3,6144]{1,0:T(4,128)(2,1)S(1)} %rim.1), channel_id=1, source_target_pairs={{0,1},{1,2},{2,3},{3,4},{4,5},{5,6},{6,7},{7,8},{8,9},{9,10},{10,1... | collective-permute-start | bytes 110600 | tf_op jit(solution)/shard_map/ppermute | solution.py:19
  3.7 5.5 %later_rows.1 = (bf16[16,512,128]{2,1,0:T(8,128)(2,1)S(1)}, bf16[16,128,512]{2,1,0:T(8,128)(2,1)S(1)}, f32[16,128,128]{2,1,0:T(8,128)S(1)}, f32[4,144,128]{2,1,0:T(8,128)S(1)}) custom-call(s32[8]{0:T(128)S(1)} %copy-done.6, bf16[512,2048]{1,0:T(8,128)(2,1)S(1)} %copy-done, bf16[512,2048]{1,0:T(8,128)(2,1)S(1)} %copy-done.1, f32[4,6144]{1,0:T(4,128)S(1)} %copy-done.3), custom_call_target="tpu_custom_call" | custom-call | flops 500000000 | bytes 4000000 | tf_op jit(solution)/shard_map/later_rows/pallas_call | solution.py:553
  9.1 0.0 copy-start.4
  9.2 0.0 copy-start.5
  9.2 2.2 %first_rows.1 = (bf16[16,512,128]{2,1,0:T(8,128)(2,1)S(1)}, bf16[16,128,512]{2,1,0:T(8,128)(2,1)S(1)}, bf16[16,128,128]{2,1,0:T(8,128)(2,1)S(1)}) custom-call(s32[8]{0:T(128)S(1)} %copy-done.6, bf16[512,2048]{1,0:T(8,128)(2,1)S(1)} %copy-done, bf16[512,2048]{1,0:T(8,128)(2,1)S(1)} %copy-done.1, ...), custom_call_target="tpu_custom_call", output_to_operand_aliasing={{0}: (7, {}), {1}: (8, {})} | custom-call | tf_op jit(solution)/shard_map/first_rows/pallas_call | solution.py:573
  11.4 2.7 %collective-permute-start.1 = (bf16[16,128,128]{2,1,0:T(8,128)(2,1)S(1)}, bf16[16,128,128]{2,1,0:T(8,128)(2,1)S(1)}, u32[]{:S(2)}, u32[]{:S(2)}) collective-permute-start(bf16[16,128,128]{2,1,0:T(8,128)(2,1)S(1)} %get-tuple-element.73), channel_id=1, source_target_pairs={{0,1},{1,0},{2,3},{3,2},{4,5},{5,4},{6,7},{7,6},{8,9},{9,8},{10,11... | collective-permute-start | bytes 1572872 | tf_op jit(solution)/shard_map/ppermute | solution.py:19
  14.1 1.2 %tables.1 = (f32[14,16,512]{2,1,0:T(8,128)S(1)}, s32[8,512]{1,0:T(8,128)S(1)}, f32[16,128,128]{2,1,0:T(8,128)S(1)}, f32[6,128]{1,0:T(8,128)S(1)}) custom-call(s32[8]{0:T(128)S(1)} %copy-done.6, bf16[14,16,512]{2,1,0:T(8,128)(2,1)S(1)} %bitcast.18, f32[16,1,128]{2,1,0:T(1,128)S(1)} %bitcast.19), custom_call_target="tpu_custom_call" | custom-call | tf_op jit(solution)/shard_map/tables/pallas_call | solution.py:654
  15.3 0.4 collective-permute-done.1.first_state_ref.refs_4_
  15.7 0.1 fusion
  15.8 1.6 %collective-permute-start.2 = (bf16[4,128,128]{2,1,0:T(8,128)(2,1)S(1)}, bf16[4,128,128]{2,1,0:T(8,128)(2,1)S(1)}, u32[]{:S(2)}, u32[]{:S(2)}) collective-permute-start(bf16[4,128,128]{2,1,0:T(8,128)(2,1)S(1)} %get-tuple-element.81), channel_id=1, source_target_pairs={{0,2},{1,3},{2,0},{3,1},{4,6},{5,7},{6,4},{7,5},{8,10},{9,11},{10,... | collective-permute-start | bytes 393224 | tf_op jit(solution)/shard_map/ppermute | solution.py:19
  17.4 2.8 %near.3 = (bf16[16,512,128]{2,1,0:T(8,128)(2,1)S(1)}, f32[16,128,512]{2,1,0:T(8,128)S(1)}) custom-call(s32[8]{0:T(128)S(1)} %copy-done.6, bf16[512,2048]{1,0:T(8,128)(2,1)S(1)} %copy-done.2, bf16[3,6144]{1,0:T(4,128)(2,1)S(1)} %collective-permute-done.rim_ref, f32[4,6144]{1,0:T(4,128)S(1)} %copy-done.3, f32[4,144,128]{2,1,0:T(8,128)S(1)} %get-tuple-element.68.inside_ref, ...), custom_call_target="tpu_custom_call" | custom-call | flops 5000000000 | bytes 35000000 | tf_op jit(solution)/shard_map/near/pallas_call | solution.py:598
  20.2 1.5 %collective-permute-done.2 = bf16[4,128,128]{2,1,0:T(8,128)(2,1)S(1)} collective-permute-done((bf16[4,128,128]{2,1,0:T(8,128)(2,1)S(1)}, bf16[4,128,128]{2,1,0:T(8,128)(2,1)S(1)}, u32[]{:S(2)}, u32[]{:S(2)}) %collective-permute-start.2) | collective-permute-done | bytes 131104 | tf_op jit(solution)/shard_map/ppermute | solution.py:19
  21.6 0.1 add_convert_fusion.1
  21.7 1.6 %collective-permute-start.3 = (bf16[4,128,128]{2,1,0:T(8,128)(2,1)S(1)}, bf16[4,128,128]{2,1,0:T(8,128)(2,1)S(1)}, u32[]{:S(2)}, u32[]{:S(2)}) collective-permute-start(bf16[4,128,128]{2,1,0:T(8,128)(2,1)S(1)} %add_convert_fusion.1), channel_id=1, source_target_pairs={{0,4},{1,5},{2,6},{3,7},{4,0},{5,1},{6,2},{7,3},{8,12},{9,13},{10,... | collective-permute-start | bytes 393224 | tf_op jit(solution)/shard_map/ppermute | solution.py:19
  23.4 2.8 %near.4 = (bf16[16,512,128]{2,1,0:T(8,128)(2,1)S(1)}, f32[16,128,512]{2,1,0:T(8,128)S(1)}) custom-call(s32[8]{0:T(128)S(1)} %copy-done.6, bf16[512,2048]{1,0:T(8,128)(2,1)S(1)} %copy-done.2, bf16[3,6144]{1,0:T(4,128)(2,1)S(1)} %collective-permute-done.rim_ref, f32[4,6144]{1,0:T(4,128)S(1)} %copy-done.3, ...), custom_call_target="tpu_custom_call", output_to_operand_aliasing={{0}: (9, {}), {1}: (10, {})} | custom-call | flops 5000000000 | bytes 35000000 | tf_op jit(solution)/shard_map/near/pallas_call | solution.py:598
  26.1 0.6 %collective-permute-done.3 = bf16[4,128,128]{2,1,0:T(8,128)(2,1)S(1)} collective-permute-done((bf16[4,128,128]{2,1,0:T(8,128)(2,1)S(1)}, bf16[4,128,128]{2,1,0:T(8,128)(2,1)S(1)}, u32[]{:S(2)}, u32[]{:S(2)}) %collective-permute-start.3) | collective-permute-done | bytes 131104 | tf_op jit(solution)/shard_map/ppermute | solution.py:19
  26.7 0.1 add_convert_fusion
  26.8 2.7 %collective-permute-start.4 = (bf16[4,128,128]{2,1,0:T(8,128)(2,1)S(1)}, bf16[4,128,128]{2,1,0:T(8,128)(2,1)S(1)}, u32[]{:S(2)}, u32[]{:S(2)}) collective-permute-start(bf16[4,128,128]{2,1,0:T(8,128)(2,1)S(1)} %add_convert_fusion), channel_id=1, source_target_pairs={{0,8},{1,9},{2,10},{3,11},{4,12},{5,13},{6,14},{7,15},{8,0},{9,1},... | collective-permute-start | bytes 393224 | tf_op jit(solution)/shard_map/ppermute | solution.py:19
  29.5 1.5 %collective-permute-start.5 = (bf16[2,4,128,128]{3,2,1,0:T(8,128)(2,1)S(1)}, bf16[2,4,128,128]{3,2,1,0:T(8,128)(2,1)S(1)}, u32[]{:S(2)}, u32[]{:S(2)}) collective-permute-start(bf16[2,4,128,128]{3,2,1,0:T(8,128)(2,1)S(1)} %pad_maximum_fusion.1), channel_id=1, source_target_pairs={{0,2},{1,3},{2,0},{3,1},{4,6},{5,7},{6,4},{7,5},{8,10},{9,11},{10,... | collective-permute-start | bytes 786440 | tf_op jit(solution)/shard_map/ppermute | solution.py:19
  31.0 4.7 %near.5 = (bf16[16,512,128]{2,1,0:T(8,128)(2,1)S(1)}, f32[16,128,512]{2,1,0:T(8,128)S(1)}) custom-call(s32[8]{0:T(128)S(1)} %copy-done.6, bf16[512,2048]{1,0:T(8,128)(2,1)S(1)} %copy-done.2, bf16[3,6144]{1,0:T(4,128)(2,1)S(1)} %collective-permute-done.rim_ref, f32[4,6144]{1,0:T(4,128)S(1)} %copy-done.3, ...), custom_call_target="tpu_custom_call", output_to_operand_aliasing={{0}: (9, {}), {1}: (10, {})} | custom-call | flops 5000000000 | bytes 35000000 | tf_op jit(solution)/shard_map/near/pallas_call | solution.py:598
  35.8 0.3 collective-permute-done.5
  36.1 0.1 pad_maximum_fusion.lower_ref
  36.2 0.1 collective-permute-start.6
  36.2 1.3 %collective-permute-start.8 = (bf16[4,128,128]{2,1,0:T(8,128)(2,1)S(1)}, bf16[4,128,128]{2,1,0:T(8,128)(2,1)S(1)}, u32[]{:S(2)}, u32[]{:S(2)}) collective-permute-start(bf16[4,128,128]{2,1,0:T(8,128)(2,1)S(1)} %collective-permute-done.4.last_ref), channel_id=1, source_target_pairs={{0,2},{1,3},{2,0},{3,1},{4,6},{5,7},{6,4},{7,5},{8,10},{9,11},{10,... | collective-permute-start | bytes 393224 | tf_op jit(solution)/shard_map/ppermute | solution.py:19
  37.6 0.2 collective-permute-start.7
  37.8 1.2 %far.4.rest_0_ = bf16[512,512]{1,0:T(8,128)(2,1)S(1)} custom-call(bf16[16,512,128]{2,1,0:T(8,128)(2,1)S(1)} %get-tuple-element.104.query_ref.refs_0_, f32[16,128,512]{2,1,0:T(8,128)S(1)} %get-tuple-element.105.near_ref.refs_1_, f32[14,16,512]{2,1,0:T(8,128)S(1)} %get-tuple-element.83.table_ref.refs_2_, ...), custom_call_target="tpu_custom_call" | custom-call | flops 5000000000 | bytes 35000000 | tf_op jit(solution)/shard_map/far/pallas_call | solution.py:630
  39.0 2.1 %far.5.refs_8_ = bf16[512,2048]{1,0:T(8,128)(2,1)} custom-call(bf16[16,512,128]{2,1,0:T(8,128)(2,1)S(1)} %get-tuple-element.104.query_ref.refs_0_, f32[16,128,512]{2,1,0:T(8,128)S(1)} %get-tuple-element.105.near_ref.refs_1_, f32[14,16,512]{2,1,0:T(8,128)S(1)} %get-tuple-element.83.table_ref.refs_2_, f32[16,128,128]{2,1,0:T(8,128)S(1)} %get-tuple-element.106.gain_ref.refs_3_, ...), custom_call_target="tpu_custom_call" | custom-call | flops 5000000000 | bytes 35000000 | tf_op jit(solution)/shard_map/far/pallas_call | solution.py:630
  41.1 1.1 %collective-permute-done.8.last_ref = bf16[4,128,128]{2,1,0:T(8,128)(2,1)S(1)} collective-permute-done((bf16[4,128,128]{2,1,0:T(8,128)(2,1)S(1)}, bf16[4,128,128]{2,1,0:T(8,128)(2,1)S(1)}, u32[]{:S(2)}, u32[]{:S(2)}) %collective-permute-start.8) | collective-permute-done | bytes 131104 | tf_op jit(solution)/shard_map/ppermute | solution.py:19
  42.2 1.2 %far.6.refs_7_ = bf16[512,512]{1,0:T(8,128)(2,1)S(1)} custom-call(bf16[16,512,128]{2,1,0:T(8,128)(2,1)S(1)} %get-tuple-element.104.query_ref.refs_0_, f32[16,128,512]{2,1,0:T(8,128)S(1)} %get-tuple-element.105.near_ref.refs_1_, f32[14,16,512]{2,1,0:T(8,128)S(1)} %get-tuple-element.83.table_ref.refs_2_, ...), custom_call_target="tpu_custom_call" | custom-call | flops 5000000000 | bytes 35000000 | tf_op jit(solution)/shard_map/far/pallas_call | solution.py:630
  43.4 0.1 collective-permute-done.9.refs_6_
  43.5 2.1 %far.7 = bf16[512,2048]{1,0:T(8,128)(2,1)} custom-call(bf16[16,512,128]{2,1,0:T(8,128)(2,1)S(1)} %get-tuple-element.104.query_ref.refs_0_, f32[16,128,512]{2,1,0:T(8,128)S(1)} %get-tuple-element.105.near_ref.refs_1_, f32[14,16,512]{2,1,0:T(8,128)S(1)} %get-tuple-element.83.table_ref.refs_2_, ...), custom_call_target="tpu_custom_call", output_to_operand_aliasing={{}: (8, {})} | custom-call | flops 5000000000 | bytes 35000000 | tf_op jit(solution)/shard_map/far/pallas_call | solution.py:630
  (19 shorter events, 0.1 us)
Async XLA Ops:
  0.0 3.6 %copy-start.1 = (bf16[512,2048]{1,0:T(8,128)(2,1)S(1)}, bf16[512,2048]{1,0:T(8,128)(2,1)}, u32[]{:S(2)}) copy-start(bf16[512,2048]{1,0:T(8,128)(2,1)} %value_ref.5) | copy-start | bytes 6291460
  0.0 3.6 %copy-start = (bf16[512,2048]{1,0:T(8,128)(2,1)S(1)}, bf16[512,2048]{1,0:T(8,128)(2,1)}, u32[]{:S(2)}) copy-start(bf16[512,2048]{1,0:T(8,128)(2,1)} %key_ref.5) | copy-start | bytes 6291460
  0.0 3.6 %copy-start.6 = (s32[8]{0:T(128)S(1)}, s32[8]{0:T(128)}, u32[]{:S(2)}) copy-start(s32[8]{0:T(128)} %docs_ref.5) | copy-start | bytes 100
  0.0 3.6 %copy-start.3 = (f32[4,6144]{1,0:T(4,128)S(1)}, f32[4,6144]{1,0:T(4,128)}, u32[]{:S(2)}) copy-start(f32[4,6144]{1,0:T(4,128)} %taps_ref.9) | copy-start | bytes 294916
  1.1 8.0 %collective-permute-start = (bf16[3,6144]{1,0:T(4,128)(2,1)S(1)}, bf16[3,6144]{1,0:T(4,128)(2,1)S(1)}, u32[]{:S(2)}, u32[]{:S(2)}) collective-permute-start(bf16[3,6144]{1,0:T(4,128)(2,1)S(1)} %rim.1), channel_id=1, source_target_pairs={{0,1},{1,2},{2,3},{3,4},{4,5},{5,6},{6,7},{7,8},{8,9},{9,10},{10,1... | collective-permute-start | bytes 110600 | tf_op jit(solution)/shard_map/ppermute | solution.py:19
  9.1 5.0 %copy-start.4 = (bf16[16,14,512]{2,0,1:T(8,128)(2,1)S(1)}, bf16[16,14,512]{2,0,1:T(8,128)(2,1)}, u32[]{:S(2)}) copy-start(bf16[16,14,512]{2,0,1:T(8,128)(2,1)} %param.11) | copy-start | bytes 688132
  9.2 5.0 %copy-start.5 = (f32[2048]{0:T(1024)S(1)}, f32[2048]{0:T(1024)}, u32[]{:S(2)}) copy-start(f32[2048]{0:T(1024)} %param.12) | copy-start | bytes 24580
  9.2 8.2 %copy-start.2 = (bf16[512,2048]{1,0:T(8,128)(2,1)S(1)}, bf16[512,2048]{1,0:T(8,128)(2,1)}, u32[]{:S(2)}) copy-start(bf16[512,2048]{1,0:T(8,128)(2,1)} %query_ref.7) | copy-start | bytes 6291460
  11.4 4.2 %collective-permute-start.1 = (bf16[16,128,128]{2,1,0:T(8,128)(2,1)S(1)}, bf16[16,128,128]{2,1,0:T(8,128)(2,1)S(1)}, u32[]{:S(2)}, u32[]{:S(2)}) collective-permute-start(bf16[16,128,128]{2,1,0:T(8,128)(2,1)S(1)} %get-tuple-element.73), channel_id=1, source_target_pairs={{0,1},{1,0},{2,3},{3,2},{4,5},{5,4},{6,7},{7,6},{8,9},{9,8},{10,11... | collective-permute-start | bytes 1572872 | tf_op jit(solution)/shard_map/ppermute | solution.py:19
  15.8 5.8 %collective-permute-start.2 = (bf16[4,128,128]{2,1,0:T(8,128)(2,1)S(1)}, bf16[4,128,128]{2,1,0:T(8,128)(2,1)S(1)}, u32[]{:S(2)}, u32[]{:S(2)}) collective-permute-start(bf16[4,128,128]{2,1,0:T(8,128)(2,1)S(1)} %get-tuple-element.81), channel_id=1, source_target_pairs={{0,2},{1,3},{2,0},{3,1},{4,6},{5,7},{6,4},{7,5},{8,10},{9,11},{10,... | collective-permute-start | bytes 393224 | tf_op jit(solution)/shard_map/ppermute | solution.py:19
  21.7 5.0 %collective-permute-start.3 = (bf16[4,128,128]{2,1,0:T(8,128)(2,1)S(1)}, bf16[4,128,128]{2,1,0:T(8,128)(2,1)S(1)}, u32[]{:S(2)}, u32[]{:S(2)}) collective-permute-start(bf16[4,128,128]{2,1,0:T(8,128)(2,1)S(1)} %add_convert_fusion.1), channel_id=1, source_target_pairs={{0,4},{1,5},{2,6},{3,7},{4,0},{5,1},{6,2},{7,3},{8,12},{9,13},{10,... | collective-permute-start | bytes 393224 | tf_op jit(solution)/shard_map/ppermute | solution.py:19
  26.8 8.9 %collective-permute-start.4 = (bf16[4,128,128]{2,1,0:T(8,128)(2,1)S(1)}, bf16[4,128,128]{2,1,0:T(8,128)(2,1)S(1)}, u32[]{:S(2)}, u32[]{:S(2)}) collective-permute-start(bf16[4,128,128]{2,1,0:T(8,128)(2,1)S(1)} %add_convert_fusion), channel_id=1, source_target_pairs={{0,8},{1,9},{2,10},{3,11},{4,12},{5,13},{6,14},{7,15},{8,0},{9,1},... | collective-permute-start | bytes 393224 | tf_op jit(solution)/shard_map/ppermute | solution.py:19
  29.5 6.6 %collective-permute-start.5 = (bf16[2,4,128,128]{3,2,1,0:T(8,128)(2,1)S(1)}, bf16[2,4,128,128]{3,2,1,0:T(8,128)(2,1)S(1)}, u32[]{:S(2)}, u32[]{:S(2)}) collective-permute-start(bf16[2,4,128,128]{3,2,1,0:T(8,128)(2,1)S(1)} %pad_maximum_fusion.1), channel_id=1, source_target_pairs={{0,2},{1,3},{2,0},{3,1},{4,6},{5,7},{6,4},{7,5},{8,10},{9,11},{10,... | collective-permute-start | bytes 786440 | tf_op jit(solution)/shard_map/ppermute | solution.py:19
  36.2 2.8 %collective-permute-start.6 = (bf16[2,8,128,128]{3,2,1,0:T(8,128)(2,1)S(1)}, bf16[2,8,128,128]{3,2,1,0:T(8,128)(2,1)S(1)}, u32[]{:S(2)}, u32[]{:S(2)}) collective-permute-start(bf16[2,8,128,128]{3,2,1,0:T(8,128)(2,1)S(1)} %pad_maximum_fusion.lower_ref), channel_id=1, source_target_pairs={{0,1},{1,0},{2,3},{3,2},{4,5},{5,4},{6,7},{7,6},{8,9},{9,8},{10,11... | collective-permute-start | bytes 1572872 | tf_op jit(solution)/shard_map/ppermute | solution.py:19
  36.2 5.9 %collective-permute-start.8 = (bf16[4,128,128]{2,1,0:T(8,128)(2,1)S(1)}, bf16[4,128,128]{2,1,0:T(8,128)(2,1)S(1)}, u32[]{:S(2)}, u32[]{:S(2)}) collective-permute-start(bf16[4,128,128]{2,1,0:T(8,128)(2,1)S(1)} %collective-permute-done.4.last_ref), channel_id=1, source_target_pairs={{0,2},{1,3},{2,0},{3,1},{4,6},{5,7},{6,4},{7,5},{8,10},{9,11},{10,... | collective-permute-start | bytes 393224 | tf_op jit(solution)/shard_map/ppermute | solution.py:19
  37.6 1.4 %collective-permute-start.7 = (bf16[4,128,128]{2,1,0:T(8,128)(2,1)S(1)}, bf16[4,128,128]{2,1,0:T(8,128)(2,1)S(1)}, u32[]{:S(2)}, u32[]{:S(2)}) collective-permute-start(bf16[4,128,128]{2,1,0:T(8,128)(2,1)S(1)} %collective-permute-done.4.last_ref), channel_id=1, source_target_pairs={{0,1},{1,0},{2,3},{3,2},{4,5},{5,4},{6,7},{7,6},{8,9},{9,8},{10,11... | collective-permute-start | bytes 393224 | tf_op jit(solution)/shard_map/ppermute | solution.py:19
  42.2 1.3 %collective-permute-start.9 = (bf16[4,128,128]{2,1,0:T(8,128)(2,1)S(1)}, bf16[4,128,128]{2,1,0:T(8,128)(2,1)S(1)}, u32[]{:S(2)}, u32[]{:S(2)}) collective-permute-start(bf16[4,128,128]{2,1,0:T(8,128)(2,1)S(1)} %collective-permute-done.8.last_ref), channel_id=1, source_target_pairs={{0,1},{1,0},{2,3},{3,2},{4,5},{5,4},{6,7},{7,6},{8,9},{9,8},{10,11... | collective-permute-start | bytes 393224 | tf_op jit(solution)/shard_map/ppermute | solution.py:19

commit v8 on v7

--- a/solution.py
+++ b/solution.py
@@ -548,7 +548,7 @@
         name="rim",
     )(*(pltpu.with_memory_space_constraint(x, pltpu.HBM) for x in (query_in, key_in, value_in)))
     tails, docs = lax.optimization_barrier((tails, doc_starts))
-    rims = exchange(tails, lambda i: i + 1 if i + 1 < dev_count else None)
+    rims = exchange(tails, lambda i: (i + 1) % dev_count)
     heads = 4
     keys, values_t, later_state, inside = pl.pallas_call(
         functools.partial(later_rows_kernel, doc_count=doc_count, heads=2 * heads),

time: 45.9 us -> 43.8 us (0.954)
  starting transfers between devices: 14.2 us -> 11 us
  local copies, waits for them, and re-layouts: 0.04 us -> 0.72 us
  waiting for transfers between devices: 3.94 us -> 4.54 us
    ppermute x10, starting transfers between devices: 14.2 us -> 11 us  [exchange(): return lax.ppermute(block, 'seq', route)]
    unnamed x14, local copies, waits for them, and re-layouts: 0.03 us -> 0.71 us
    ppermute x10, waiting for transfers between devices: 3.94 us -> 4.54 us  [exchange(): return lax.ppermute(block, 'seq', route)]
  transfers between devices with their start and end apart: 10 -> 10, of which waited for: 6 -> 7; matrix products, arithmetic and copies ran while one was open for 0% -> 0% of each run, Pallas kernels for 47% -> 49%
where the time goes in v8:
time: 43.8 us; the launch traced here: 43.7 us
  Pallas kernels  26.8 us (61%)
  starting transfers between devices  11 us (25%)
  waiting for transfers between devices  4.54 us (10%)
  local copies, waits for them, and re-layouts  0.72 us (2%)
    ppermute x10, starting transfers between devices, exchange(): return lax.ppermute(block, 'seq', route)  11 us
    pallas_call x3, Pallas kernels, near_piece(): pl.pallas_call(functools.partial(near_kernel, first_head=first_head, head...  10.3 us
    pallas_call x4, Pallas kernels, far_piece(): pl.pallas_call(functools.partial(far_skip if out is not None else far_ker...  6.58 us
    pallas_call x1, Pallas kernels, local(): pl.pallas_call(functools.partial(later_rows_kernel, doc_count=doc_count,...  5.48 us
    ppermute x10, waiting for transfers between devices, exchange(): return lax.ppermute(block, 'seq', route)  4.54 us
    pallas_call x1, Pallas kernels, local(): pl.pallas_call(functools.partial(first_rows_kernel, doc_count=doc_count,...  2.23 us
    pallas_call x1, Pallas kernels, local(): pl.pallas_call(functools.partial(tables_kernel, doc_count=doc_count), in_...  1.17 us
    pallas_call x1, Pallas kernels, local(): pl.pallas_call(rim_kernel, in_specs=[pl.BlockSpec(memory_space=pltpu.HBM)...  1.09 us
  transfers between devices with their start and end apart: 10, of which 7 were waited for; matrix products, arithmetic and copies ran while one was open for 0% of the time, Pallas kernels for 49%

profile of v8, /device:TPU:0, one launch (start us, length us, event | category | flops | bytes accessed | tf_op | source)
XLA Modules:
  0.0 43.7 jit_solution(4802256676029074131)
XLA Ops:
  0.0 1.1 %rim.1 = bf16[3,6144]{1,0:T(4,128)(2,1)S(1)} custom-call(bf16[512,2048]{1,0:T(8,128)(2,1)} %query_ref.7, bf16[512,2048]{1,0:T(8,128)(2,1)} %key_ref.5, bf16[512,2048]{1,0:T(8,128)(2,1)} %value_ref.5), custom_call_target="tpu_custom_call" | custom-call | tf_op jit(solution)/shard_map/rim/pallas_call | solution.py:538
  1.1 0.5 %collective-permute-start = (bf16[3,6144]{1,0:T(4,128)(2,1)S(1)}, bf16[3,6144]{1,0:T(4,128)(2,1)S(1)}, u32[]{:S(2)}, u32[]{:S(2)}) collective-permute-start(bf16[3,6144]{1,0:T(4,128)(2,1)S(1)} %rim.1), channel_id=1, source_target_pairs={{0,1},{1,2},{2,3},{3,4},{4,5},{5,6},{6,7},{7,8},{8,9},{9,10},{10,1... | collective-permute-start | bytes 110600 | tf_op jit(solution)/shard_map/ppermute | solution.py:19
  1.6 0.1 copy-done.1
  1.7 0.6 %copy-done = bf16[512,2048]{1,0:T(8,128)(2,1)S(1)} copy-done((bf16[512,2048]{1,0:T(8,128)(2,1)S(1)}, bf16[512,2048]{1,0:T(8,128)(2,1)}, u32[]{:S(2)}) %copy-start) | copy-done | bytes 2097176
  2.3 5.5 %later_rows.1 = (bf16[16,512,128]{2,1,0:T(8,128)(2,1)S(1)}, bf16[16,128,512]{2,1,0:T(8,128)(2,1)S(1)}, f32[16,128,128]{2,1,0:T(8,128)S(1)}, f32[4,144,128]{2,1,0:T(8,128)S(1)}) custom-call(s32[8]{0:T(128)S(1)} %copy-done.6, bf16[512,2048]{1,0:T(8,128)(2,1)S(1)} %copy-done, bf16[512,2048]{1,0:T(8,128)(2,1)S(1)} %copy-done.1, f32[4,6144]{1,0:T(4,128)S(1)} %copy-done.3), custom_call_target="tpu_custom_call" | custom-call | flops 500000000 | bytes 4000000 | tf_op jit(solution)/shard_map/later_rows/pallas_call | solution.py:553
  7.8 0.6 %collective-permute-done.rim_ref = bf16[3,6144]{1,0:T(4,128)(2,1)S(1)} collective-permute-done((bf16[3,6144]{1,0:T(4,128)(2,1)S(1)}, bf16[3,6144]{1,0:T(4,128)(2,1)S(1)}, u32[]{:S(2)}, u32[]{:S(2)}) %collective-permute-start) | collective-permute-done | bytes 36896 | tf_op jit(solution)/shard_map/ppermute | solution.py:19
  8.4 2.2 %first_rows.1 = (bf16[16,512,128]{2,1,0:T(8,128)(2,1)S(1)}, bf16[16,128,512]{2,1,0:T(8,128)(2,1)S(1)}, bf16[16,128,128]{2,1,0:T(8,128)(2,1)S(1)}) custom-call(s32[8]{0:T(128)S(1)} %copy-done.6, bf16[512,2048]{1,0:T(8,128)(2,1)S(1)} %copy-done, bf16[512,2048]{1,0:T(8,128)(2,1)S(1)} %copy-done.1, ...), custom_call_target="tpu_custom_call", output_to_operand_aliasing={{0}: (7, {}), {1}: (8, {})} | custom-call | tf_op jit(solution)/shard_map/first_rows/pallas_call | solution.py:573
  10.6 1.5 %collective-permute-start.1 = (bf16[16,128,128]{2,1,0:T(8,128)(2,1)S(1)}, bf16[16,128,128]{2,1,0:T(8,128)(2,1)S(1)}, u32[]{:S(2)}, u32[]{:S(2)}) collective-permute-start(bf16[16,128,128]{2,1,0:T(8,128)(2,1)S(1)} %get-tuple-element.73), channel_id=1, source_target_pairs={{0,1},{1,0},{2,3},{3,2},{4,5},{5,4},{6,7},{7,6},{8,9},{9,8},{10,11... | collective-permute-start | bytes 1572872 | tf_op jit(solution)/shard_map/ppermute | solution.py:19
  12.1 1.2 %tables.1 = (f32[14,16,512]{2,1,0:T(8,128)S(1)}, s32[8,512]{1,0:T(8,128)S(1)}, f32[16,128,128]{2,1,0:T(8,128)S(1)}, f32[6,128]{1,0:T(8,128)S(1)}) custom-call(s32[8]{0:T(128)S(1)} %copy-done.6, bf16[14,16,512]{2,1,0:T(8,128)(2,1)S(1)} %bitcast.18, f32[16,1,128]{2,1,0:T(1,128)S(1)} %bitcast.19), custom_call_target="tpu_custom_call" | custom-call | tf_op jit(solution)/shard_map/tables/pallas_call | solution.py:654
  13.3 0.4 collective-permute-done.1.first_state_ref.refs_4_
  13.6 0.1 fusion
  13.7 1.6 %collective-permute-start.2 = (bf16[4,128,128]{2,1,0:T(8,128)(2,1)S(1)}, bf16[4,128,128]{2,1,0:T(8,128)(2,1)S(1)}, u32[]{:S(2)}, u32[]{:S(2)}) collective-permute-start(bf16[4,128,128]{2,1,0:T(8,128)(2,1)S(1)} %get-tuple-element.81), channel_id=1, source_target_pairs={{0,2},{1,3},{2,0},{3,1},{4,6},{5,7},{6,4},{7,5},{8,10},{9,11},{10,... | collective-permute-start | bytes 393224 | tf_op jit(solution)/shard_map/ppermute | solution.py:19
  15.4 2.8 %near.3 = (bf16[16,512,128]{2,1,0:T(8,128)(2,1)S(1)}, f32[16,128,512]{2,1,0:T(8,128)S(1)}) custom-call(s32[8]{0:T(128)S(1)} %copy-done.6, bf16[512,2048]{1,0:T(8,128)(2,1)S(1)} %copy-done.2, bf16[3,6144]{1,0:T(4,128)(2,1)S(1)} %collective-permute-done.rim_ref, f32[4,6144]{1,0:T(4,128)S(1)} %copy-done.3, f32[4,144,128]{2,1,0:T(8,128)S(1)} %get-tuple-element.68.inside_ref, ...), custom_call_target="tpu_custom_call" | custom-call | flops 5000000000 | bytes 35000000 | tf_op jit(solution)/shard_map/near/pallas_call | solution.py:598
  18.1 1.5 %collective-permute-done.2 = bf16[4,128,128]{2,1,0:T(8,128)(2,1)S(1)} collective-permute-done((bf16[4,128,128]{2,1,0:T(8,128)(2,1)S(1)}, bf16[4,128,128]{2,1,0:T(8,128)(2,1)S(1)}, u32[]{:S(2)}, u32[]{:S(2)}) %collective-permute-start.2) | collective-permute-done | bytes 131104 | tf_op jit(solution)/shard_map/ppermute | solution.py:19
  19.6 0.1 add_convert_fusion.1
  19.7 1.6 %collective-permute-start.3 = (bf16[4,128,128]{2,1,0:T(8,128)(2,1)S(1)}, bf16[4,128,128]{2,1,0:T(8,128)(2,1)S(1)}, u32[]{:S(2)}, u32[]{:S(2)}) collective-permute-start(bf16[4,128,128]{2,1,0:T(8,128)(2,1)S(1)} %add_convert_fusion.1), channel_id=1, source_target_pairs={{0,4},{1,5},{2,6},{3,7},{4,0},{5,1},{6,2},{7,3},{8,12},{9,13},{10,... | collective-permute-start | bytes 393224 | tf_op jit(solution)/shard_map/ppermute | solution.py:19
  21.3 2.8 %near.4 = (bf16[16,512,128]{2,1,0:T(8,128)(2,1)S(1)}, f32[16,128,512]{2,1,0:T(8,128)S(1)}) custom-call(s32[8]{0:T(128)S(1)} %copy-done.6, bf16[512,2048]{1,0:T(8,128)(2,1)S(1)} %copy-done.2, bf16[3,6144]{1,0:T(4,128)(2,1)S(1)} %collective-permute-done.rim_ref, f32[4,6144]{1,0:T(4,128)S(1)} %copy-done.3, ...), custom_call_target="tpu_custom_call", output_to_operand_aliasing={{0}: (9, {}), {1}: (10, {})} | custom-call | flops 5000000000 | bytes 35000000 | tf_op jit(solution)/shard_map/near/pallas_call | solution.py:598
  24.1 0.6 %collective-permute-done.3 = bf16[4,128,128]{2,1,0:T(8,128)(2,1)S(1)} collective-permute-done((bf16[4,128,128]{2,1,0:T(8,128)(2,1)S(1)}, bf16[4,128,128]{2,1,0:T(8,128)(2,1)S(1)}, u32[]{:S(2)}, u32[]{:S(2)}) %collective-permute-start.3) | collective-permute-done | bytes 131104 | tf_op jit(solution)/shard_map/ppermute | solution.py:19
  24.7 0.1 add_convert_fusion
  24.8 2.7 %collective-permute-start.4 = (bf16[4,128,128]{2,1,0:T(8,128)(2,1)S(1)}, bf16[4,128,128]{2,1,0:T(8,128)(2,1)S(1)}, u32[]{:S(2)}, u32[]{:S(2)}) collective-permute-start(bf16[4,128,128]{2,1,0:T(8,128)(2,1)S(1)} %add_convert_fusion), channel_id=1, source_target_pairs={{0,8},{1,9},{2,10},{3,11},{4,12},{5,13},{6,14},{7,15},{8,0},{9,1},... | collective-permute-start | bytes 393224 | tf_op jit(solution)/shard_map/ppermute | solution.py:19
  27.5 1.5 %collective-permute-start.5 = (bf16[2,4,128,128]{3,2,1,0:T(8,128)(2,1)S(1)}, bf16[2,4,128,128]{3,2,1,0:T(8,128)(2,1)S(1)}, u32[]{:S(2)}, u32[]{:S(2)}) collective-permute-start(bf16[2,4,128,128]{3,2,1,0:T(8,128)(2,1)S(1)} %pad_maximum_fusion.1), channel_id=1, source_target_pairs={{0,2},{1,3},{2,0},{3,1},{4,6},{5,7},{6,4},{7,5},{8,10},{9,11},{10,... | collective-permute-start | bytes 786440 | tf_op jit(solution)/shard_map/ppermute | solution.py:19
  29.0 4.7 %near.5 = (bf16[16,512,128]{2,1,0:T(8,128)(2,1)S(1)}, f32[16,128,512]{2,1,0:T(8,128)S(1)}) custom-call(s32[8]{0:T(128)S(1)} %copy-done.6, bf16[512,2048]{1,0:T(8,128)(2,1)S(1)} %copy-done.2, bf16[3,6144]{1,0:T(4,128)(2,1)S(1)} %collective-permute-done.rim_ref, f32[4,6144]{1,0:T(4,128)S(1)} %copy-done.3, ...), custom_call_target="tpu_custom_call", output_to_operand_aliasing={{0}: (9, {}), {1}: (10, {})} | custom-call | flops 5000000000 | bytes 35000000 | tf_op jit(solution)/shard_map/near/pallas_call | solution.py:598
  33.7 0.3 collective-permute-done.5
  34.1 0.1 collective-permute-start.6
  34.2 1.3 %collective-permute-start.8 = (bf16[4,128,128]{2,1,0:T(8,128)(2,1)S(1)}, bf16[4,128,128]{2,1,0:T(8,128)(2,1)S(1)}, u32[]{:S(2)}, u32[]{:S(2)}) collective-permute-start(bf16[4,128,128]{2,1,0:T(8,128)(2,1)S(1)} %collective-permute-done.4.last_ref), channel_id=1, source_target_pairs={{0,2},{1,3},{2,0},{3,1},{4,6},{5,7},{6,4},{7,5},{8,10},{9,11},{10,... | collective-permute-start | bytes 393224 | tf_op jit(solution)/shard_map/ppermute | solution.py:19
  35.6 0.2 collective-permute-start.7
  35.7 1.2 %far.4.rest_0_ = bf16[512,512]{1,0:T(8,128)(2,1)S(1)} custom-call(bf16[16,512,128]{2,1,0:T(8,128)(2,1)S(1)} %get-tuple-element.104.query_ref.refs_0_, f32[16,128,512]{2,1,0:T(8,128)S(1)} %get-tuple-element.105.near_ref.refs_1_, f32[14,16,512]{2,1,0:T(8,128)S(1)} %get-tuple-element.83.table_ref.refs_2_, ...), custom_call_target="tpu_custom_call" | custom-call | flops 5000000000 | bytes 35000000 | tf_op jit(solution)/shard_map/far/pallas_call | solution.py:630
  37.0 2.1 %far.5.refs_8_ = bf16[512,2048]{1,0:T(8,128)(2,1)} custom-call(bf16[16,512,128]{2,1,0:T(8,128)(2,1)S(1)} %get-tuple-element.104.query_ref.refs_0_, f32[16,128,512]{2,1,0:T(8,128)S(1)} %get-tuple-element.105.near_ref.refs_1_, f32[14,16,512]{2,1,0:T(8,128)S(1)} %get-tuple-element.83.table_ref.refs_2_, f32[16,128,128]{2,1,0:T(8,128)S(1)} %get-tuple-element.106.gain_ref.refs_3_, ...), custom_call_target="tpu_custom_call" | custom-call | flops 5000000000 | bytes 35000000 | tf_op jit(solution)/shard_map/far/pallas_call | solution.py:630
  39.1 1.1 %collective-permute-done.8.last_ref = bf16[4,128,128]{2,1,0:T(8,128)(2,1)S(1)} collective-permute-done((bf16[4,128,128]{2,1,0:T(8,128)(2,1)S(1)}, bf16[4,128,128]{2,1,0:T(8,128)(2,1)S(1)}, u32[]{:S(2)}, u32[]{:S(2)}) %collective-permute-start.8) | collective-permute-done | bytes 131104 | tf_op jit(solution)/shard_map/ppermute | solution.py:19
  40.1 1.2 %far.6.refs_7_ = bf16[512,512]{1,0:T(8,128)(2,1)S(1)} custom-call(bf16[16,512,128]{2,1,0:T(8,128)(2,1)S(1)} %get-tuple-element.104.query_ref.refs_0_, f32[16,128,512]{2,1,0:T(8,128)S(1)} %get-tuple-element.105.near_ref.refs_1_, f32[14,16,512]{2,1,0:T(8,128)S(1)} %get-tuple-element.83.table_ref.refs_2_, ...), custom_call_target="tpu_custom_call" | custom-call | flops 5000000000 | bytes 35000000 | tf_op jit(solution)/shard_map/far/pallas_call | solution.py:630
  41.4 0.1 collective-permute-done.9.refs_6_
  41.5 2.0 %far.7 = bf16[512,2048]{1,0:T(8,128)(2,1)} custom-call(bf16[16,512,128]{2,1,0:T(8,128)(2,1)S(1)} %get-tuple-element.104.query_ref.refs_0_, f32[16,128,512]{2,1,0:T(8,128)S(1)} %get-tuple-element.105.near_ref.refs_1_, f32[14,16,512]{2,1,0:T(8,128)S(1)} %get-tuple-element.83.table_ref.refs_2_, ...), custom_call_target="tpu_custom_call", output_to_operand_aliasing={{}: (8, {})} | custom-call | flops 5000000000 | bytes 35000000 | tf_op jit(solution)/shard_map/far/pallas_call | solution.py:630
  (19 shorter events, 0.1 us)
Async XLA Ops:
  0.0 1.7 %copy-start.1 = (bf16[512,2048]{1,0:T(8,128)(2,1)S(1)}, bf16[512,2048]{1,0:T(8,128)(2,1)}, u32[]{:S(2)}) copy-start(bf16[512,2048]{1,0:T(8,128)(2,1)} %value_ref.5) | copy-start | bytes 6291460
  0.0 2.3 %copy-start = (bf16[512,2048]{1,0:T(8,128)(2,1)S(1)}, bf16[512,2048]{1,0:T(8,128)(2,1)}, u32[]{:S(2)}) copy-start(bf16[512,2048]{1,0:T(8,128)(2,1)} %key_ref.5) | copy-start | bytes 6291460
  0.0 2.3 %copy-start.6 = (s32[8]{0:T(128)S(1)}, s32[8]{0:T(128)}, u32[]{:S(2)}) copy-start(s32[8]{0:T(128)} %docs_ref.5) | copy-start | bytes 100
  0.0 2.3 %copy-start.3 = (f32[4,6144]{1,0:T(4,128)S(1)}, f32[4,6144]{1,0:T(4,128)}, u32[]{:S(2)}) copy-start(f32[4,6144]{1,0:T(4,128)} %taps_ref.9) | copy-start | bytes 294916
  1.1 7.3 %collective-permute-start = (bf16[3,6144]{1,0:T(4,128)(2,1)S(1)}, bf16[3,6144]{1,0:T(4,128)(2,1)S(1)}, u32[]{:S(2)}, u32[]{:S(2)}) collective-permute-start(bf16[3,6144]{1,0:T(4,128)(2,1)S(1)} %rim.1), channel_id=1, source_target_pairs={{0,1},{1,2},{2,3},{3,4},{4,5},{5,6},{6,7},{7,8},{8,9},{9,10},{10,1... | collective-permute-start | bytes 110600 | tf_op jit(solution)/shard_map/ppermute | solution.py:19
  8.4 3.7 %copy-start.4 = (bf16[16,14,512]{2,0,1:T(8,128)(2,1)S(1)}, bf16[16,14,512]{2,0,1:T(8,128)(2,1)}, u32[]{:S(2)}) copy-start(bf16[16,14,512]{2,0,1:T(8,128)(2,1)} %param.11) | copy-start | bytes 688132
  8.4 3.7 %copy-start.5 = (f32[2048]{0:T(1024)S(1)}, f32[2048]{0:T(1024)}, u32[]{:S(2)}) copy-start(f32[2048]{0:T(1024)} %param.12) | copy-start | bytes 24580
  8.4 7.0 %copy-start.2 = (bf16[512,2048]{1,0:T(8,128)(2,1)S(1)}, bf16[512,2048]{1,0:T(8,128)(2,1)}, u32[]{:S(2)}) copy-start(bf16[512,2048]{1,0:T(8,128)(2,1)} %query_ref.7) | copy-start | bytes 6291460
  10.6 3.0 %collective-permute-start.1 = (bf16[16,128,128]{2,1,0:T(8,128)(2,1)S(1)}, bf16[16,128,128]{2,1,0:T(8,128)(2,1)S(1)}, u32[]{:S(2)}, u32[]{:S(2)}) collective-permute-start(bf16[16,128,128]{2,1,0:T(8,128)(2,1)S(1)} %get-tuple-element.73), channel_id=1, source_target_pairs={{0,1},{1,0},{2,3},{3,2},{4,5},{5,4},{6,7},{7,6},{8,9},{9,8},{10,11... | collective-permute-start | bytes 1572872 | tf_op jit(solution)/shard_map/ppermute | solution.py:19
  13.7 5.8 %collective-permute-start.2 = (bf16[4,128,128]{2,1,0:T(8,128)(2,1)S(1)}, bf16[4,128,128]{2,1,0:T(8,128)(2,1)S(1)}, u32[]{:S(2)}, u32[]{:S(2)}) collective-permute-start(bf16[4,128,128]{2,1,0:T(8,128)(2,1)S(1)} %get-tuple-element.81), channel_id=1, source_target_pairs={{0,2},{1,3},{2,0},{3,1},{4,6},{5,7},{6,4},{7,5},{8,10},{9,11},{10,... | collective-permute-start | bytes 393224 | tf_op jit(solution)/shard_map/ppermute | solution.py:19
  19.7 5.0 %collective-permute-start.3 = (bf16[4,128,128]{2,1,0:T(8,128)(2,1)S(1)}, bf16[4,128,128]{2,1,0:T(8,128)(2,1)S(1)}, u32[]{:S(2)}, u32[]{:S(2)}) collective-permute-start(bf16[4,128,128]{2,1,0:T(8,128)(2,1)S(1)} %add_convert_fusion.1), channel_id=1, source_target_pairs={{0,4},{1,5},{2,6},{3,7},{4,0},{5,1},{6,2},{7,3},{8,12},{9,13},{10,... | collective-permute-start | bytes 393224 | tf_op jit(solution)/shard_map/ppermute | solution.py:19
  24.8 8.9 %collective-permute-start.4 = (bf16[4,128,128]{2,1,0:T(8,128)(2,1)S(1)}, bf16[4,128,128]{2,1,0:T(8,128)(2,1)S(1)}, u32[]{:S(2)}, u32[]{:S(2)}) collective-permute-start(bf16[4,128,128]{2,1,0:T(8,128)(2,1)S(1)} %add_convert_fusion), channel_id=1, source_target_pairs={{0,8},{1,9},{2,10},{3,11},{4,12},{5,13},{6,14},{7,15},{8,0},{9,1},... | collective-permute-start | bytes 393224 | tf_op jit(solution)/shard_map/ppermute | solution.py:19
  27.5 6.6 %collective-permute-start.5 = (bf16[2,4,128,128]{3,2,1,0:T(8,128)(2,1)S(1)}, bf16[2,4,128,128]{3,2,1,0:T(8,128)(2,1)S(1)}, u32[]{:S(2)}, u32[]{:S(2)}) collective-permute-start(bf16[2,4,128,128]{3,2,1,0:T(8,128)(2,1)S(1)} %pad_maximum_fusion.1), channel_id=1, source_target_pairs={{0,2},{1,3},{2,0},{3,1},{4,6},{5,7},{6,4},{7,5},{8,10},{9,11},{10,... | collective-permute-start | bytes 786440 | tf_op jit(solution)/shard_map/ppermute | solution.py:19
  34.1 2.8 %collective-permute-start.6 = (bf16[2,8,128,128]{3,2,1,0:T(8,128)(2,1)S(1)}, bf16[2,8,128,128]{3,2,1,0:T(8,128)(2,1)S(1)}, u32[]{:S(2)}, u32[]{:S(2)}) collective-permute-start(bf16[2,8,128,128]{3,2,1,0:T(8,128)(2,1)S(1)} %pad_maximum_fusion.lower_ref), channel_id=1, source_target_pairs={{0,1},{1,0},{2,3},{3,2},{4,5},{5,4},{6,7},{7,6},{8,9},{9,8},{10,11... | collective-permute-start | bytes 1572872 | tf_op jit(solution)/shard_map/ppermute | solution.py:19
  34.2 5.9 %collective-permute-start.8 = (bf16[4,128,128]{2,1,0:T(8,128)(2,1)S(1)}, bf16[4,128,128]{2,1,0:T(8,128)(2,1)S(1)}, u32[]{:S(2)}, u32[]{:S(2)}) collective-permute-start(bf16[4,128,128]{2,1,0:T(8,128)(2,1)S(1)} %collective-permute-done.4.last_ref), channel_id=1, source_target_pairs={{0,2},{1,3},{2,0},{3,1},{4,6},{5,7},{6,4},{7,5},{8,10},{9,11},{10,... | collective-permute-start | bytes 393224 | tf_op jit(solution)/shard_map/ppermute | solution.py:19
  35.6 1.4 %collective-permute-start.7 = (bf16[4,128,128]{2,1,0:T(8,128)(2,1)S(1)}, bf16[4,128,128]{2,1,0:T(8,128)(2,1)S(1)}, u32[]{:S(2)}, u32[]{:S(2)}) collective-permute-start(bf16[4,128,128]{2,1,0:T(8,128)(2,1)S(1)} %collective-permute-done.4.last_ref), channel_id=1, source_target_pairs={{0,1},{1,0},{2,3},{3,2},{4,5},{5,4},{6,7},{7,6},{8,9},{9,8},{10,11... | collective-permute-start | bytes 393224 | tf_op jit(solution)/shard_map/ppermute | solution.py:19
  40.1 1.3 %collective-permute-start.9 = (bf16[4,128,128]{2,1,0:T(8,128)(2,1)S(1)}, bf16[4,128,128]{2,1,0:T(8,128)(2,1)S(1)}, u32[]{:S(2)}, u32[]{:S(2)}) collective-permute-start(bf16[4,128,128]{2,1,0:T(8,128)(2,1)S(1)} %collective-permute-done.8.last_ref), channel_id=1, source_target_pairs={{0,1},{1,0},{2,3},{3,2},{4,5},{5,4},{6,7},{7,6},{8,9},{9,8},{10,11... | collective-permute-start | bytes 393224 | tf_op jit(solution)/shard_map/ppermute | solution.py:19
